TPU v7x, 32 devices: a whole 2x2x4 slice. The times are simulated.
32 devices in a mesh: ctx: 2 (over y), uly: 4 (over x, core), tp: 4 (over z).
Axes of the slice: x: 2, y: 2, z: 4, core: 2. Of those that a mesh axis runs over, the one named last changes fastest.
Arguments:
- inputs: bfloat16 [2, 4096, 2048], P(None, ('ctx', 'uly', 'tp')), may hold values from -6 to 6
- doc_ids: int32 [2, 4096], replicated, may hold values from -1 to 3, as said below
- attn_norm: float32 [2048], replicated, may hold values from 0.5 to 1.5
- w_query: bfloat16 [2048, 2048], P(None, 'tp'), may hold values from -0.125 to 0.125
- w_key: bfloat16 [2048, 1024], P(None, 'tp'), may hold values from -0.125 to 0.125
- w_value: bfloat16 [2048, 1024], P(None, 'tp'), may hold values from -0.125 to 0.125
- w_headgate: bfloat16 [2048, 16], P(None, 'tp'), may hold values from -0.125 to 0.125
- query_norm: float32 [128], replicated, may hold values from 0.5 to 1.5
- key_norm: float32 [128], replicated, may hold values from 0.5 to 1.5
- w_output: bfloat16 [2048, 2048], P('tp'), may hold values from -0.5 to 0.5
- mlp_norm: float32 [2048], replicated, may hold values from 0.5 to 1.5
- w_gate: bfloat16 [2048, 6144], P(None, 'tp'), may hold values from -0.125 to 0.125
- w_up: bfloat16 [2048, 6144], P(None, 'tp'), may hold values from -0.125 to 0.125
- w_down: bfloat16 [6144, 2048], P('tp'), may hold values from -0.15625 to 0.15625
- cotangent: bfloat16 [2, 4096, 2048], P(None, ('ctx', 'uly', 'tp')), may hold values from -6 to 6
Outputs:
- outputs: bfloat16 [2, 4096, 2048], P(None, ('ctx', 'uly', 'tp'))
- grad_inputs: float32 [2, 4096, 2048], P(None, ('ctx', 'uly', 'tp'))
- grad_attn_norm: float32 [2048], replicated
- grad_query: float32 [2048, 2048], P(('ctx', 'uly'), 'tp')
- grad_key: float32 [2048, 1024], P(('ctx', 'uly'), 'tp')
- grad_value: float32 [2048, 1024], P(('ctx', 'uly'), 'tp')
- grad_headgate: float32 [2048, 16], P(('ctx', 'uly'), 'tp')
- grad_query_norm: float32 [128], replicated
- grad_key_norm: float32 [128], replicated
- grad_output: float32 [2048, 2048], P('tp', ('ctx', 'uly'))
- grad_mlp_norm: float32 [2048], replicated
- grad_gate: float32 [2048, 6144], P(('ctx', 'uly'), 'tp')
- grad_up: float32 [2048, 6144], P(('ctx', 'uly'), 'tp')
- grad_down: float32 [6144, 2048], P('tp', ('ctx', 'uly'))
Inputs may be any that keep to these rules, and one draw needn't show every extreme that they name: `doc_ids`: along a row the ids never fall before the padding; document 0 of every row covers at least the first 2560 positions; the row ends in at least 128 padding tokens of id -1, and id 4 - 1 appears in every row.
All inputs are finite; a program needn't handle non-finite values.
Results may differ from a plain program's by a relative error of at most 0.03.
Values may be sent and summed in bfloat16 or wider, within the bound.
A program may use at most 384 MiB of HBM per device.

v0:
```python
import jax
import jax.numpy as jnp
from jax import lax
from jax.sharding import PartitionSpec as P

epsilon = 1e-06
rope_base = 1000000.0
masked_score = -1e30


def rms_scale(values, gain):
    return values * lax.rsqrt(jnp.mean(values * values, axis=-1, keepdims=True) + epsilon) * gain


def rotate(values, positions):
    half_dim = values.shape[-1] // 2
    frequency = rope_base ** (-(jnp.arange(half_dim, dtype=jnp.float32) * 2.0 / values.shape[-1]))
    angles = positions.astype(jnp.float32)[:, None] * frequency[None, :]
    cosine = jnp.cos(angles)[None, :, None, :]
    sine_part = jnp.sin(angles)[None, :, None, :]
    lead_part = values[..., :half_dim]
    tail_part = values[..., half_dim:]
    return jnp.concatenate(
        [lead_part * cosine - tail_part * sine_part, tail_part * cosine + lead_part * sine_part],
        axis=-1,
    )


def spread(values):
    return lax.all_gather(values, "tp", axis=1, tiled=True)


def collect(values):
    return lax.psum_scatter(
        values.astype(jnp.bfloat16), "tp", scatter_dimension=1, tiled=True
    ).astype(jnp.float32)


def flatten(values):
    return values.reshape(-1, values.shape[-1])


def outer_sum(left, right):
    return lax.dot_general(
        flatten(left), flatten(right), (((0,), (0,)), ((), ())), preferred_element_type=jnp.float32
    )


def back_mult(values, weight):
    return lax.dot_general(
        values, weight, (((values.ndim - 1,), (1,)), ((), ())), preferred_element_type=jnp.float32
    )


def visible(query_pos, key_pos, query_seg, key_seg):
    earlier = key_pos[None, None, :] <= query_pos[None, :, None]
    same_doc = (query_seg[:, :, None] == key_seg[:, None, :]) & (key_seg[:, None, :] >= 0)
    return earlier & same_doc | (key_pos[None, None, :] == query_pos[None, :, None])


def key_mask(doc_ids, query_pos, query_seg, count):
    key_pos = jnp.arange(count, dtype=jnp.int32)
    return visible(query_pos, key_pos, query_seg, doc_ids)[:, None, None]


def forward_step(queries, query_pos, query_seg, doc_ids, scale, carry, piece):
    running, totals, accum = carry
    keys_in, values_in = piece
    allowed = key_mask(doc_ids, query_pos, query_seg, keys_in.shape[1])
    scores = (
        jnp.einsum("sqhgd,snhd->shgqn", queries, keys_in, preferred_element_type=jnp.float32)
        * scale
    )
    scores = jnp.where(allowed, scores, masked_score)
    peak = jnp.maximum(running, jnp.max(scores, axis=-1))
    weights = jnp.where(allowed, jnp.exp(scores - peak[..., None]), 0.0)
    totals = jnp.sum(weights, axis=-1)
    accum = jnp.einsum(
        "shgqn,snhd->shgqd",
        weights.astype(jnp.bfloat16),
        values_in,
        preferred_element_type=jnp.float32,
    )
    return (peak, totals, accum)


def backward_step(queries, grad_attended, log_total, delta, query_pos, query_seg, doc_ids, scale):

    def step(carry, piece, start):
        keys_in, values_in = piece
        allowed = key_mask(doc_ids, query_pos, query_seg, keys_in.shape[1])
        scores = (
            jnp.einsum("sqhgd,snhd->shgqn", queries, keys_in, preferred_element_type=jnp.float32)
            * scale
        )
        weights = jnp.where(allowed, jnp.exp(scores - log_total[..., None]), 0.0)
        value_part = jnp.einsum(
            "shgqn,sqhgd->snhd",
            weights.astype(jnp.bfloat16),
            grad_attended,
            preferred_element_type=jnp.float32,
        )
        prob_grad = jnp.einsum(
            "sqhgd,snhd->shgqn", grad_attended, values_in, preferred_element_type=jnp.float32
        )
        score_grad = (weights * (prob_grad - delta[..., None])).astype(jnp.bfloat16)
        grad_queries = (
            jnp.einsum("shgqn,snhd->sqhgd", score_grad, keys_in, preferred_element_type=jnp.float32)
            * scale
        )
        key_part = (
            jnp.einsum("shgqn,sqhgd->snhd", score_grad, queries, preferred_element_type=jnp.float32)
            * scale
        )
        return (grad_queries, key_part, value_part)

    return step


def per_device(
    inputs,
    doc_ids,
    attn_norm,
    w_query,
    w_key,
    w_value,
    w_headgate,
    query_norm,
    key_norm,
    w_output,
    mlp_norm,
    w_gate,
    w_up,
    w_down,
    cotangent,
):
    n_tensor = lax.axis_size("tp")
    n_uly = lax.axis_size("uly")
    seqs, rows, width = inputs.shape
    group = rows * n_tensor
    head_dim = query_norm.shape[0]
    q_heads = w_query.shape[1] // head_dim
    kv_heads = w_key.shape[1] // head_dim
    repeat = q_heads // kv_heads
    total_len = doc_ids.shape[1]
    scale = head_dim ** (-0.5)
    block_start = (lax.axis_index("ctx") * n_uly + lax.axis_index("uly")) * group
    positions = block_start + jnp.arange(group, dtype=jnp.int32)
    inputs_f = inputs.astype(jnp.float32)
    first_local, norm_one_back = jax.vjp(rms_scale, inputs_f, attn_norm)
    first_in = spread(first_local.astype(jnp.bfloat16))
    q_raw = jnp.dot(first_in, w_query, preferred_element_type=jnp.float32).reshape(
        seqs, group, q_heads, head_dim
    )
    k_raw = jnp.dot(first_in, w_key, preferred_element_type=jnp.float32).reshape(
        seqs, group, kv_heads, head_dim
    )
    v_raw = jnp.dot(first_in, w_value, preferred_element_type=jnp.float32).reshape(
        seqs, group, kv_heads, head_dim
    )
    gate_logit = jnp.dot(first_in, w_headgate, preferred_element_type=jnp.float32).astype(
        jnp.bfloat16
    )

    def shape_heads(q_in, k_in, q_gain, k_gain):
        return (
            rotate(rms_scale(q_in, q_gain), positions),
            rotate(rms_scale(k_in, k_gain), positions),
        )

    (q_rot, k_rot), heads_back = jax.vjp(shape_heads, q_raw, k_raw, query_norm, key_norm)
    q_low = q_rot.astype(jnp.bfloat16)
    k_low = k_rot.astype(jnp.bfloat16)
    v_low = v_raw.astype(jnp.bfloat16)
    query_seg = lax.dynamic_slice_in_dim(doc_ids, block_start, group, 1)
    queries = q_low.reshape(seqs, group, kv_heads, repeat, head_dim)
    head_gate = gate_logit.reshape(seqs, group, kv_heads, repeat)
    init = (
        jnp.full((seqs, kv_heads, repeat, group), masked_score, jnp.float32),
        jnp.zeros((seqs, kv_heads, repeat, group), jnp.float32),
        jnp.zeros((seqs, kv_heads, repeat, group, head_dim), jnp.float32),
    )
    running, totals, accum = forward_step(
        queries,
        positions,
        query_seg,
        doc_ids,
        scale,
        init,
        (
            lax.all_gather(k_low, ("ctx", "uly"), axis=1, tiled=True),
            lax.all_gather(v_low, ("ctx", "uly"), axis=1, tiled=True),
        ),
    )
    log_total = running + jnp.log(totals)
    attended = (accum / totals[..., None]).transpose(0, 3, 1, 2, 4)
    sigma = jax.nn.sigmoid(head_gate.astype(jnp.float32))
    gated_heads = (attended * sigma[..., None]).astype(jnp.bfloat16)
    gated = gated_heads
    gated = gated.reshape(seqs, group, q_heads * head_dim)
    middle = inputs_f + collect(jnp.dot(gated, w_output, preferred_element_type=jnp.float32))
    second_local, norm_two_back = jax.vjp(rms_scale, middle, mlp_norm)
    second_in = spread(second_local.astype(jnp.bfloat16))
    gate = jnp.dot(second_in, w_gate, preferred_element_type=jnp.float32)
    up_part = jnp.dot(second_in, w_up, preferred_element_type=jnp.float32)
    hidden_f, swish_back = jax.vjp(lambda left, right: jax.nn.silu(left) * right, gate, up_part)
    hidden = hidden_f.astype(jnp.bfloat16)
    outputs = (
        middle + collect(jnp.dot(hidden, w_down, preferred_element_type=jnp.float32))
    ).astype(jnp.bfloat16)
    cot_rows = spread(cotangent)
    grad_down = outer_sum(hidden, cot_rows)
    d_hidden = back_mult(cot_rows, w_down)
    d_gate, d_up = swish_back(d_hidden)
    d_gate = d_gate.astype(jnp.bfloat16)
    d_up = d_up.astype(jnp.bfloat16)
    grad_gate = outer_sum(second_in, d_gate)
    grad_up = outer_sum(second_in, d_up)
    d_second = collect(back_mult(d_gate, w_gate) + back_mult(d_up, w_up))
    d_mid_norm, grad_mlp_norm = norm_two_back(d_second)
    d_mid = cotangent.astype(jnp.float32) + d_mid_norm
    d_branch = spread(d_mid.astype(jnp.bfloat16))
    grad_output = outer_sum(gated, d_branch)
    d_gated = back_mult(d_branch, w_output).astype(jnp.bfloat16)
    d_gated_heads = d_gated.reshape(seqs, group, kv_heads, repeat, head_dim)
    d_gated_f = d_gated_heads.astype(jnp.float32)
    d_attended = (d_gated_f * sigma[..., None]).astype(jnp.bfloat16)
    d_logit = (jnp.sum(d_gated_f * attended, axis=-1) * sigma * (1.0 - sigma)).astype(jnp.bfloat16)
    delta = jnp.sum(d_attended.astype(jnp.float32) * attended, axis=-1).transpose(0, 2, 3, 1)
    back_fn = backward_step(
        queries, d_attended, log_total, delta, positions, query_seg, doc_ids, scale
    )
    key_heads = k_low.shape[2]
    back_init = (
        jnp.zeros(queries.shape, jnp.float32),
        jnp.zeros((seqs, total_len, key_heads, head_dim), jnp.float32),
        jnp.zeros((seqs, total_len, key_heads, head_dim), jnp.float32),
    )
    grad_queries, grad_keys, grad_values = back_fn(
        back_init,
        (
            lax.all_gather(k_low, ("ctx", "uly"), axis=1, tiled=True),
            lax.all_gather(v_low, ("ctx", "uly"), axis=1, tiled=True),
        ),
        jnp.int32(0),
    )
    k_back, v_back = (
        lax.psum_scatter(
            grad_keys.astype(jnp.bfloat16), ("ctx", "uly"), scatter_dimension=1, tiled=True
        ).astype(jnp.float32),
        lax.psum_scatter(
            grad_values.astype(jnp.bfloat16), ("ctx", "uly"), scatter_dimension=1, tiled=True
        ).astype(jnp.float32),
    )
    q_back = (
        grad_queries.astype(jnp.bfloat16)
        .astype(jnp.float32)
        .reshape(seqs, group, q_heads, head_dim)
    )
    logit_low = d_logit.reshape(seqs, group, q_heads)
    key_low = k_back.astype(jnp.bfloat16)
    value_low = v_back.astype(jnp.bfloat16).reshape(seqs, group, kv_heads * head_dim)
    d_q_raw, d_k_raw, grad_query_norm, grad_key_norm = heads_back(
        (q_back, key_low.astype(jnp.float32))
    )
    d_q_low = d_q_raw.astype(jnp.bfloat16).reshape(seqs, group, q_heads * head_dim)
    d_k_low = d_k_raw.astype(jnp.bfloat16).reshape(seqs, group, kv_heads * head_dim)
    grad_query = outer_sum(first_in, d_q_low)
    grad_key = outer_sum(first_in, d_k_low)
    grad_value = outer_sum(first_in, value_low)
    grad_headgate = outer_sum(first_in, logit_low)
    d_first = collect(
        back_mult(d_q_low, w_query)
        + back_mult(d_k_low, w_key)
        + back_mult(value_low, w_value)
        + back_mult(logit_low, w_headgate)
    )
    d_in_norm, grad_attn_norm = norm_one_back(d_first)
    grad_inputs = d_mid + d_in_norm
    grad_query, grad_key, grad_value, grad_headgate, grad_output, grad_gate, grad_up, grad_down = (
        lax.psum_scatter(
            grad_query.astype(jnp.bfloat16), ("ctx", "uly"), scatter_dimension=0, tiled=True
        ).astype(jnp.float32),
        lax.psum_scatter(
            grad_key.astype(jnp.bfloat16), ("ctx", "uly"), scatter_dimension=0, tiled=True
        ).astype(jnp.float32),
        lax.psum_scatter(
            grad_value.astype(jnp.bfloat16), ("ctx", "uly"), scatter_dimension=0, tiled=True
        ).astype(jnp.float32),
        lax.psum_scatter(
            grad_headgate.astype(jnp.bfloat16), ("ctx", "uly"), scatter_dimension=0, tiled=True
        ).astype(jnp.float32),
        lax.psum_scatter(
            grad_output.astype(jnp.bfloat16), ("ctx", "uly"), scatter_dimension=1, tiled=True
        ).astype(jnp.float32),
        lax.psum_scatter(
            grad_gate.astype(jnp.bfloat16), ("ctx", "uly"), scatter_dimension=0, tiled=True
        ).astype(jnp.float32),
        lax.psum_scatter(
            grad_up.astype(jnp.bfloat16), ("ctx", "uly"), scatter_dimension=0, tiled=True
        ).astype(jnp.float32),
        lax.psum_scatter(
            grad_down.astype(jnp.bfloat16), ("ctx", "uly"), scatter_dimension=1, tiled=True
        ).astype(jnp.float32),
    )
    grad_attn_norm, grad_query_norm, grad_key_norm, grad_mlp_norm = lax.psum(
        (grad_attn_norm, grad_query_norm, grad_key_norm, grad_mlp_norm), ("ctx", "uly", "tp")
    )
    return (
        outputs,
        grad_inputs,
        grad_attn_norm,
        grad_query,
        grad_key,
        grad_value,
        grad_headgate,
        grad_query_norm,
        grad_key_norm,
        grad_output,
        grad_mlp_norm,
        grad_gate,
        grad_up,
        grad_down,
    )


def solution(mesh):
    placed = (
        P(None, ("ctx", "uly", "tp"), None),
        P(),
        P(),
        P(None, "tp"),
        P(None, "tp"),
        P(None, "tp"),
        P(None, "tp"),
        P(),
        P(),
        P("tp", None),
        P(),
        P(None, "tp"),
        P(None, "tp"),
        P("tp", None),
        P(None, ("ctx", "uly", "tp"), None),
    )
    return jax.shard_map(
        per_device,
        mesh=mesh,
        in_specs=placed,
        out_specs=(
            P(None, ("ctx", "uly", "tp"), None),
            P(None, ("ctx", "uly", "tp"), None),
            P(),
            P(("ctx", "uly"), "tp"),
            P(("ctx", "uly"), "tp"),
            P(("ctx", "uly"), "tp"),
            P(("ctx", "uly"), "tp"),
            P(),
            P(),
            P("tp", ("ctx", "uly")),
            P(),
            P(("ctx", "uly"), "tp"),
            P(("ctx", "uly"), "tp"),
            P("tp", ("ctx", "uly")),
        ),
        check_vma=False,
    )
```

profile of v0, /device:TPU:0, one launch (start us, length us, event | category | flops | bytes accessed | tf_op | source)
XLA Modules:
  0.0 1401.1 jit_solution(8949041921783533437)
XLA Ops:
  14.5 81.8 %all-gather.7.cloned.1.call-done = bf16[2,512,2048]{2,1,0:T(8,128)(2,1)} async-done(((bf16[2,128,2048]{2,1,0:T(8,128)(2,1)}), bf16[2,512,2048]{2,1,0:T(8,128)(2,1)}) %all-gather.7.cloned.1.call-update) | async-done | bytes 4194320 | tf_op jit(solution)/shard_map/all_gather | solution.py:30
  141.0 29.6 %fusion.4 = (f32[2,2,2,512]{3,2,1,0:T(2,128)S(1)}, f32[2,2,4096,512,2]{3,2,4,1,0:T(8,128)}) fusion(pred[2,512,4096]{1,2,0:T(8,128)(4,1)} %and_or_fusion, bf16[2,512,2,2,64]{4,1,3,2,0:T(8,128)(2,1)} %bitcast.239, bf16[2,512,2,2,64]{4,1,3,2,0:T(8,128)(2,1)S(1)} %bitcast.237, bf16[2,4096,2,128]{3,1,2,0:T(8,128)(2,1)} %all-gather.9.cloned.1.call-done), kind=kOutput, calls=%fused_computation.8 | convolution fusion | flops 4347392000 | bytes 76562432 | tf_op jit(solution)/shard_map/sqhgd,snhd->shgqn/dot_general | solution.py:71
  170.6 23.2 %fusion.6 = f32[2,2,2,512]{3,2,1,0:T(2,128)S(1)} fusion(f32[2,2,4096,512,2]{3,2,4,1,0:T(8,128)} %get-tuple-element.52, f32[2,2,2,512]{3,2,1,0:T(2,128)S(1)} %broadcast_maximum_fusion, pred[2,512,4096]{1,2,0:T(8,128)(4,1)} %and_or_fusion), kind=kLoop, calls=%fused_computation.10 | loop fusion | flops 83881984 | bytes 71335936 | tf_op jit(solution)/shard_map/reduce_sum | solution.py:77
  193.9 27.8 %multiply_convert_fusion.4 = (bf16[2,512,2,2,128]{1,4,3,2,0:T(8,128)(2,1)S(1)}, f32[2,512,2,2,128]{1,4,3,2,0:T(8,128)}) fusion(f32[2,512,2,2]{1,3,2,0:T(2,128)S(1)} %reshape.332, f32[2,512,2,2]{1,3,2,0:T(2,128)S(1)} %bitcast.245, f32[2,2,4096,512,2]{3,2,4,1,0:T(8,128)} %get-tuple-element.52, f32[2,2,2,512]{3,2,1,0:T(2,128)S(1)} %broadcast_maximum_fusion, ...), kind=kOutput, calls=%fused_computation.109 | convolution fusion | flops 4380426240 | bytes 78692352 | tf_op jit(solution)/shard_map/shgqn,snhd->shgqd/dot_general | solution.py:78
  227.8 76.3 %reduce-scatter.17.cloned.1.call-done = bf16[2,128,2048]{2,1,0:T(8,128)(2,1)} async-done(((bf16[2,512,2048]{2,1,0:T(8,128)(2,1)}), bf16[2,128,2048]{2,1,0:T(8,128)(2,1)}) %reduce-scatter.17.cloned.1.call-update) | async-done | bytes 1048592 | tf_op jit(solution)/shard_map/reduce_scatter | solution.py:34
  308.4 78.5 %all-gather.15.cloned.1.call-done = bf16[2,512,2048]{2,1,0:T(8,128)(2,1)} async-done(((bf16[2,128,2048]{2,1,0:T(8,128)(2,1)}), bf16[2,512,2048]{2,1,0:T(8,128)(2,1)}) %all-gather.15.cloned.1.call-update) | async-done | bytes 4194320 | tf_op jit(solution)/shard_map/all_gather | solution.py:30
  398.6 69.7 %all-gather.13.cloned.1.call-done = bf16[2,512,2048]{2,1,0:T(8,128)(2,1)} async-done(((bf16[2,128,2048]{2,1,0:T(8,128)(2,1)}), bf16[2,512,2048]{2,1,0:T(8,128)(2,1)}) %all-gather.13.cloned.1.call-update) | async-done | bytes 4194320 | tf_op jit(solution)/shard_map/all_gather | solution.py:30
  480.2 16.7 %fusion.19 = (bf16[2,512,1536]{2,1,0:T(8,128)(2,1)}, bf16[2,512,1536]{2,1,0:T(8,128)(2,1)S(1)}, bf16[2,512,1536]{2,1,0:T(8,128)(2,1)}) fusion(f32[2,512,1536]{2,1,0:T(8,128)} %fusion.20, f32[2,512,1536]{2,1,0:T(8,128)} %fusion.26, bf16[2,512,2048]{2,1,0:T(8,128)(2,1)} %all-gather.13.cloned.1.call-done, bf16[2048,1536]{1,0:T(8,128)(2,1)} %param.26), kind=kOutput, calls=%fused_computation.30 | convolution fusion | flops 6467616768 | bytes 32505856 | tf_op jit(solution)/shard_map/dot_general | solution.py:204
  516.6 75.4 %reduce-scatter.21.cloned.1.call-done = bf16[2,128,2048]{2,1,0:T(8,128)(2,1)} async-done(((bf16[2,512,2048]{2,1,0:T(8,128)(2,1)}), bf16[2,128,2048]{2,1,0:T(8,128)(2,1)}) %reduce-scatter.21.cloned.1.call-update) | async-done | bytes 1048592 | tf_op jit(solution)/shard_map/reduce_scatter | solution.py:34
  599.0 81.3 %all-gather.17.cloned.1.call-done = bf16[2,512,2048]{2,1,0:T(8,128)(2,1)} async-done(((bf16[2,128,2048]{2,1,0:T(8,128)(2,1)}), bf16[2,512,2048]{2,1,0:T(8,128)(2,1)}) %all-gather.17.cloned.1.call-update) | async-done | bytes 4194320 | tf_op jit(solution)/shard_map/all_gather | solution.py:30
  685.8 27.2 %fusion.34 = bf16[2,4096,2,128]{1,3,2,0:T(8,128)(2,1)} fusion(f32[2,2,4096,512,2]{3,2,4,1,0:T(8,128)} %get-tuple-element.52, f32[2,2,2,512]{3,2,1,0:T(2,128)S(1)} %log_add_fusion, pred[2,512,4096]{1,2,0:T(8,128)(4,1)} %and_or_fusion, bf16[2,512,2,2,128]{1,4,3,2,0:T(8,128)(2,1)S(1)} %bitcast.234, f32[2,512,2,2]{1,3,2,0:T(2,128)S(1)} %reshape.332), kind=kOutput, calls=%fused_computation.48 | convolution fusion | flops 4365746176 | bytes 76578816 | tf_op jit(solution)/shard_map/shgqn,sqhgd->snhd/dot_general | solution.py:97
  713.1 46.3 %fusion.1 = bf16[2,2,2,512,4096]{3,4,2,1,0:T(8,128)(2,1)} fusion(f32[2,2,4096,512,2]{3,2,4,1,0:T(8,128)} %get-tuple-element.52, f32[2,2,2,512]{3,2,1,0:T(2,128)S(1)} %bitcast.248, f32[2,2,2,512]{3,2,1,0:T(2,128)S(1)} %log_add_fusion, pred[2,512,4096]{1,2,0:T(8,128)(4,1)} %and_or_fusion, bf16[2,4096,2,128]{1,3,2,0:T(8,128)(2,1)} %all-gather.11.cloned.1.call-done, ...), kind=kOutput, calls=%fused_computation.2 | convolution fusion | flops 4397203456 | bytes 110149632 | tf_op jit(solution)/shard_map/sqhgd,snhd->shgqn/dot_general | solution.py:103
  759.4 16.6 %fusion.33 = bf16[2,4096,2,128]{3,1,2,0:T(8,128)(2,1)} fusion(bf16[2,2,2,512,4096]{3,4,2,1,0:T(8,128)(2,1)} %fusion.1, bf16[2,512,2,2,64]{4,1,3,2,0:T(8,128)(2,1)S(1)} %bitcast.240, bf16[2,512,2,2,64]{4,1,3,2,0:T(8,128)(2,1)S(1)} %bitcast.238), kind=kOutput, calls=%fused_computation.47 | convolution fusion | flops 4301258752 | bytes 38797312 | tf_op jit(solution)/shard_map/shgqn,sqhgd->snhd/dot_general | solution.py:112
  823.6 15.1 %fusion.76 = f32[2,2,128,2,512]{4,2,3,1,0:T(8,128)S(1)} fusion(bf16[2,2,2,512,4096]{3,4,2,1,0:T(8,128)(2,1)} %fusion.1, bf16[2,4096,2,128]{3,1,2,0:T(8,128)(2,1)} %all-gather.9.cloned.1.call-done), kind=kOutput, calls=%fused_computation.115 | convolution fusion | flops 4296540160 | bytes 39845888 | tf_op jit(solution)/shard_map/shgqn,snhd->sqhgd/dot_general | solution.py:108
  919.1 38.0 %reduce-scatter.37.cloned.1.call-done = bf16[256,1536]{1,0:T(8,128)(2,1)} async-done(((bf16[2048,1536]{1,0:T(8,128)(2,1)}), bf16[256,1536]{1,0:T(8,128)(2,1)}) %reduce-scatter.37.cloned.1.call-update) | async-done | bytes 786448 | tf_op jit(solution)/shard_map/reduce_scatter | solution.py:296
  959.6 62.6 %reduce-scatter.39.cloned.1.call-done = bf16[256,1536]{1,0:T(8,128)(2,1)} async-done(((bf16[2048,1536]{1,0:T(8,128)(2,1)}), bf16[256,1536]{1,0:T(8,128)(2,1)}) %reduce-scatter.39.cloned.1.call-update) | async-done | bytes 786448 | tf_op jit(solution)/shard_map/reduce_scatter | solution.py:299
  1024.7 35.5 %reduce-scatter.43.cloned.1.call-done = bf16[256,4]{1,0:T(8,128)(2,1)} async-done(((bf16[2048,4]{1,0:T(8,128)(2,1)}), bf16[256,4]{1,0:T(8,128)(2,1)}) %reduce-scatter.43.cloned.1.call-update) | async-done | bytes 2064
  1061.8 42.8 %reduce-scatter.35.cloned.1.call-done = bf16[512,256]{1,0:T(8,128)(2,1)} async-done(((bf16[512,2048]{1,0:T(8,128)(2,1)}), bf16[512,256]{1,0:T(8,128)(2,1)}) %reduce-scatter.35.cloned.1.call-update) | async-done | bytes 262160 | tf_op jit(solution)/shard_map/reduce_scatter | solution.py:293
  1106.4 43.5 %reduce-scatter.29.cloned.1.call-done = bf16[256,512]{1,0:T(8,128)(2,1)} async-done(((bf16[2048,512]{1,0:T(8,128)(2,1)}), bf16[256,512]{1,0:T(8,128)(2,1)}) %reduce-scatter.29.cloned.1.call-update) | async-done | bytes 262160 | tf_op jit(solution)/shard_map/reduce_scatter | solution.py:281
  1151.7 37.3 %reduce-scatter.33.cloned.1.call-done = bf16[256,256]{1,0:T(8,128)(2,1)} async-done(((bf16[2048,256]{1,0:T(8,128)(2,1)}), bf16[256,256]{1,0:T(8,128)(2,1)}) %reduce-scatter.33.cloned.1.call-update) | async-done | bytes 131088 | tf_op jit(solution)/shard_map/reduce_scatter | solution.py:287
  1190.6 38.0 %reduce-scatter.31.cloned.1.call-done = bf16[256,256]{1,0:T(8,128)(2,1)} async-done(((bf16[2048,256]{1,0:T(8,128)(2,1)}), bf16[256,256]{1,0:T(8,128)(2,1)}) %reduce-scatter.31.cloned.1.call-update) | async-done | bytes 131088 | tf_op jit(solution)/shard_map/reduce_scatter | solution.py:284
  1230.3 77.4 %reduce-scatter.27.cloned.1.call-done = bf16[2,128,2048]{2,1,0:T(8,128)(2,1)} async-done(((bf16[2,512,2048]{2,1,0:T(8,128)(2,1)}), bf16[2,128,2048]{2,1,0:T(8,128)(2,1)}) %reduce-scatter.27.cloned.1.call-update) | async-done | bytes 1048592 | tf_op jit(solution)/shard_map/reduce_scatter | solution.py:34
  1310.0 46.3 %all-reduce.4 = (f32[2048]{0:T(1024)}, f32[128]{0:T(128)}, f32[128]{0:T(128)}, f32[2048]{0:T(1024)}) all-reduce(f32[2048]{0:T(1024)S(1)} %get-tuple-element.22, f32[128]{0:T(128)S(1)} %get-tuple-element.14, f32[128]{0:T(128)S(1)} %get-tuple-element.18, ...), channel_id=1, replica_groups=mesh['ctx'=2,'uly'=4,'tp'=4] {'ctx','uly','tp'}, use_global_device_ids=true, to_apply=%region_19.20 | all-reduce | flops 4352 | bytes 34816 | tf_op jit(solution)/shard_map/psum | solution.py:306
  1356.4 32.0 %reduce-scatter.19.cloned.1.call-done = bf16[2,128,2048]{2,1,0:T(8,128)(2,1)} async-done(((bf16[2,512,2048]{2,1,0:T(8,128)(2,1)}), bf16[2,128,2048]{2,1,0:T(8,128)(2,1)}) %reduce-scatter.19.cloned.1.call-update) | async-done | bytes 1048592 | tf_op jit(solution)/shard_map/reduce_scatter | solution.py:34
  (262 shorter events, 266.7 us)
Async XLA Ops:
  7.2 89.1 %all-gather.7.cloned.1.call-start = ((), (), s32[]{:S(2)}) async-start(), calls=%async_computation.14 | async-start | bytes 5242880 | tf_op jit(solution)/shard_map/all_gather | solution.py:30
  12.7 128.4 %all-gather.9.cloned.1.call-start = ((), (), s32[]{:S(2)}) async-start(), calls=%async_computation.15 | async-start | bytes 4718592 | tf_op jit(solution)/shard_map/all_gather | solution.py:191
  105.6 88.2 %all-gather.11.cloned.1.call-start = ((), (), s32[]{:S(2)}) async-start(), calls=%async_computation.16 | async-start | bytes 4718592 | tf_op jit(solution)/shard_map/all_gather | solution.py:192
  133.7 170.4 %reduce-scatter.17.cloned.1.call-start = ((), (), s32[]{:S(2)}) async-start(), calls=%async_computation.17 | async-start | bytes 5242880 | tf_op jit(solution)/shard_map/reduce_scatter | solution.py:34
  227.0 159.9 %all-gather.15.cloned.1.call-start = ((), (), s32[]{:S(2)}) async-start(), calls=%async_computation.20 | async-start | bytes 5242880 | tf_op jit(solution)/shard_map/all_gather | solution.py:30
  227.6 240.7 %all-gather.13.cloned.1.call-start = ((), (), s32[]{:S(2)}) async-start(), calls=%async_computation.18 | async-start | bytes 5242880 | tf_op jit(solution)/shard_map/all_gather | solution.py:30
  308.4 283.6 %reduce-scatter.21.cloned.1.call-start = ((), (), s32[]{:S(2)}) async-start(), calls=%async_computation.21 | async-start | bytes 5242880 | tf_op jit(solution)/shard_map/reduce_scatter | solution.py:34
  516.5 163.8 %all-gather.17.cloned.1.call-start = ((), (), s32[]{:S(2)}) async-start(), calls=%async_computation.22 | async-start | bytes 5242880 | tf_op jit(solution)/shard_map/all_gather | solution.py:30
  598.9 272.4 %reduce-scatter.25.cloned.1.call-start = ((), (), s32[]{:S(2)}) async-start(), calls=%async_computation.24 | async-start | bytes 4718592 | tf_op jit(solution)/shard_map/reduce_scatter | solution.py:251
  713.0 172.0 %reduce-scatter.23.cloned.1.call-start = ((), (), s32[]{:S(2)}) async-start(), calls=%async_computation.23 | async-start | bytes 4718592 | tf_op jit(solution)/shard_map/reduce_scatter | solution.py:248
  776.1 140.5 %reduce-scatter.41.cloned.1.call-start = ((), (), s32[]{:S(2)}) async-start(), calls=%async_computation.32 | async-start | bytes 7077888 | tf_op jit(solution)/shard_map/reduce_scatter | solution.py:302
  787.5 169.7 %reduce-scatter.37.cloned.1.call-start = ((), (), s32[]{:S(2)}) async-start(), calls=%async_computation.30 | async-start | bytes 7077888 | tf_op jit(solution)/shard_map/reduce_scatter | solution.py:296
  799.5 222.7 %reduce-scatter.39.cloned.1.call-start = ((), (), s32[]{:S(2)}) async-start(), calls=%async_computation.31 | async-start | bytes 7077888 | tf_op jit(solution)/shard_map/reduce_scatter | solution.py:299
  811.2 249.1 %reduce-scatter.43.cloned.1.call-start = ((), (), s32[]{:S(2)}) async-start(), calls=%async_computation.33 | async-start | bytes 589824
  817.6 287.0 %reduce-scatter.35.cloned.1.call-start = ((), (), s32[]{:S(2)}) async-start(), calls=%async_computation.29 | async-start | bytes 2359296 | tf_op jit(solution)/shard_map/reduce_scatter | solution.py:293
  823.6 326.3 %reduce-scatter.29.cloned.1.call-start = ((), (), s32[]{:S(2)}) async-start(), calls=%async_computation.26 | async-start | bytes 2359296 | tf_op jit(solution)/shard_map/reduce_scatter | solution.py:281
  869.7 319.3 %reduce-scatter.33.cloned.1.call-start = ((), (), s32[]{:S(2)}) async-start(), calls=%async_computation.28 | async-start | bytes 1179648 | tf_op jit(solution)/shard_map/reduce_scatter | solution.py:287
  877.2 351.4 %reduce-scatter.31.cloned.1.call-start = ((), (), s32[]{:S(2)}) async-start(), calls=%async_computation.27 | async-start | bytes 1179648 | tf_op jit(solution)/shard_map/reduce_scatter | solution.py:284
  894.1 413.7 %reduce-scatter.27.cloned.1.call-start = ((), (), s32[]{:S(2)}) async-start(), calls=%async_computation.25 | async-start | bytes 5242880 | tf_op jit(solution)/shard_map/reduce_scatter | solution.py:34
  904.3 484.1 %reduce-scatter.19.cloned.1.call-start = ((), (), s32[]{:S(2)}) async-start(), calls=%async_computation.19 | async-start | bytes 5242880 | tf_op jit(solution)/shard_map/reduce_scatter | solution.py:34
  919.1 437.3 %copy-start.51 = (f32[2,128]{1,0:T(2,128)S(1)}, f32[2,128]{1,0:T(2,128)}, u32[]{:S(2)}) copy-start(f32[2,128]{1,0:T(2,128)} %copy-done.50) | copy-start | bytes 3076
  919.1 469.3 %copy-start.35 = (f32[2048]{0:T(1024)S(1)}, f32[2048]{0:T(1024)}, u32[]{:S(2)}) copy-start(f32[2048]{0:T(1024)} %param.25) | copy-start | bytes 24580
  919.1 469.3 %copy-start.45 = (f32[2,128]{1,0:T(2,128)S(1)}, f32[2,128]{1,0:T(2,128)}, u32[]{:S(2)}) copy-start(f32[2,128]{1,0:T(2,128)} %copy-done.44) | copy-start | bytes 3076
  919.1 469.3 %copy-start.49 = (f32[2,128]{1,0:T(2,128)S(1)}, f32[2,128]{1,0:T(2,128)}, u32[]{:S(2)}) copy-start(f32[2,128]{1,0:T(2,128)} %copy-done.48) | copy-start | bytes 3076
  (58 other events, 2916.8 us)
Sparse Core Ops, SparseCore 0:
  12.8 83.4 all-gather.6
  105.7 35.2 all-gather.8
  143.5 37.4 all-gather.10
  227.1 76.9 reduce-scatter.16
  305.6 81.2 all-gather.14
  389.0 79.2 all-gather.12
  516.7 75.2 reduce-scatter.20
  599.1 81.2 all-gather.16
  713.1 49.8 reduce-scatter.24
  776.2 50.3 reduce-scatter.22
  830.0 61.7 reduce-scatter.40
  895.4 61.7 reduce-scatter.36
  960.5 61.6 reduce-scatter.38
  1026.1 34.1 reduce-scatter.42
  1063.4 41.2 reduce-scatter.34
  1108.7 41.2 reduce-scatter.28
  1152.9 36.0 reduce-scatter.32
  1192.6 36.0 reduce-scatter.30
  1231.0 76.7 reduce-scatter.26
  1310.0 78.3 reduce-scatter.18
where the time goes:
time: 1410 us; the launch traced here: 1400 us
  waiting for transfers between devices  878 us (62%)
  matrix products  332 us (24%)
  other arithmetic  98.1 us (7%)
  blocking collectives  46.3 us (3%)
  local copies, waits for them, and re-layouts  28.5 us (2%)
  between operations  15.4 us (1%)
    all_gather x4, waiting for transfers between devices, spread(): return lax.all_gather(values, 'tp', axis=1, tiled=True)  311 us
    reduce_scatter x4, waiting for transfers between devices, collect(): lax.psum_scatter(values.astype(jnp.bfloat16), 'tp', scatter_dimension=1,...  261 us
    reduce_scatter x1, waiting for transfers between devices, per_device(): lax.psum_scatter(grad_up.astype(jnp.bfloat16), ('ctx', 'uly'), scatter_di...  62.6 us
    dot_general x8, matrix products, outer_sum(): lax.dot_general(flatten(left), flatten(right), (((0,), (0,)), ((), ())),...  56.6 us
    dot_general x8, matrix products, back_mult(): lax.dot_general(values, weight, (((values.ndim - 1,), (1,)), ((), ())), p...  54 us
    psum x1, blocking collectives, per_device(): lax.psum((grad_attn_norm, grad_query_norm, grad_key_norm, grad_mlp_norm),...  46.3 us
    dot_general x1, matrix products, step(): jnp.einsum('sqhgd,snhd->shgqn', grad_attended, values_in, preferred_eleme...  46.3 us
    reduce_scatter x1, waiting for transfers between devices, per_device(): lax.psum_scatter(grad_query.astype(jnp.bfloat16), ('ctx', 'uly'), scatter...  43.5 us
  transfers between devices with their start and end apart: 20, of which 16 were waited for; matrix products, arithmetic and copies ran while one was open for 22% of the time, Pallas kernels for 0%

commit v1 on v0

v1 whole, which is shorter than its diff:
```python
import functools
import math

import jax
import jax.numpy as jnp
from jax import lax
from jax.experimental import pallas as pl
from jax.experimental.pallas import tpu as pltpu
from jax.sharding import PartitionSpec as P

epsilon = 1e-06
rope_base = 1000000.0
log2e = 1.0 / math.log(2.0)
bf16 = jnp.bfloat16
f32 = jnp.float32
vmem_bytes = 48 * 1024 * 1024

MESH = pl.DeviceIdType.MESH
NT = (((1,), (1,)), ((), ()))
NN = (((1,), (0,)), ((), ()))
TN = (((0,), (0,)), ((), ()))


def mm(left, right, dims=NN):
    return lax.dot_general(left, right, dims, preferred_element_type=f32)


def params(**more):
    return pltpu.CompilerParams(vmem_limit_bytes=vmem_bytes, **more)


def cost(flops, moved, trans=0):
    return pl.CostEstimate(flops=int(flops), bytes_accessed=int(moved), transcendentals=int(trans))


def full(shape):
    return pl.BlockSpec(shape, lambda *_: (0,) * len(shape))


def rms_inverse(values):
    return lax.rsqrt(jnp.mean(values * values, axis=-1, keepdims=True) + epsilon)


def rope_tables(positions, head_dim):
    half = head_dim // 2
    frequency = rope_base ** (-(jnp.arange(half, dtype=f32) * 2.0 / head_dim))
    angles = positions.astype(f32)[:, None] * frequency[None, :]
    cosine, sine = jnp.cos(angles), jnp.sin(angles)
    return jnp.concatenate([cosine, cosine], 1), jnp.concatenate([-sine, sine], 1)


def project_kernel(heads, kv_heads, dim, scale, x_ref, w_ref, cos_ref, sin_ref, qg_ref, kg_ref,
                   q_ref, kv_ref, nq_ref, nk_ref, rq_ref, rk_ref, logit_ref):
    cosine, sine = cos_ref[...], sin_ref[...]
    raw = mm(x_ref[...], w_ref[...])

    def rope(unit, gain):
        scaled = unit * gain
        return scaled * cosine + pltpu.roll(scaled, dim // 2, 1) * sine

    for h in range(heads + kv_heads):
        values = raw[:, h * dim:(h + 1) * dim]
        inverse = rms_inverse(values)
        unit = values * inverse
        if h < heads:
            at = slice(h * dim, (h + 1) * dim)
            q_ref[:, at] = (rope(unit, qg_ref[...]) * (scale * log2e)).astype(bf16)
            nq_ref[:, at] = unit.astype(bf16)
            rq_ref[:, h:h + 1] = inverse
        else:
            g = h - heads
            at = slice(g * dim, (g + 1) * dim)
            kv_ref[:, at] = rope(unit, kg_ref[...]).astype(bf16)
            nk_ref[:, at] = unit.astype(bf16)
            rk_ref[:, g:g + 1] = inverse
    first = (heads + kv_heads) * dim
    kv_ref[:, kv_heads * dim:] = raw[:, first:first + kv_heads * dim].astype(bf16)
    first += kv_heads * dim
    logit_ref[...] = raw[:, first:first + heads].astype(bf16).astype(f32)


def project(x, w, tables, query_norm, key_norm, heads, kv_heads, scale, block=256):
    rows, width = x.shape
    dim = query_norm.shape[0]
    cosine, sine = tables
    block = min(block, cosine.shape[0])
    around = cosine.shape[0] // block
    kernel = functools.partial(project_kernel, heads, kv_heads, dim, scale)

    def by_row(cols):
        return pl.BlockSpec((block, cols), lambda i: (i, 0))

    table = pl.BlockSpec((block, dim), lambda i: (i % around, 0))
    shapes = [
        (heads * dim, bf16), (2 * kv_heads * dim, bf16), (heads * dim, bf16), (kv_heads * dim, bf16),
        (heads, f32), (kv_heads, f32), (heads, f32),
    ]
    return pl.pallas_call(
        kernel,
        grid=(rows // block,),
        in_specs=[by_row(width), full(w.shape), table, table, full((1, dim)), full((1, dim))],
        out_specs=[by_row(c) for c, _ in shapes],
        out_shape=[jax.ShapeDtypeStruct((rows, c), t) for c, t in shapes],
        compiler_params=params(),
        cost_estimate=cost(2 * rows * width * w.shape[1], 2 * (rows * width + w.size) + rows * 4096),
        name="project",
    )(x, w, cosine, sine, query_norm[None], key_norm[None])


def bounds_loop(bounds_ref, row, body):
    lo, full_lo, full_hi, hi = (bounds_ref[row, i] for i in range(4))
    lax.fori_loop(lo, full_lo, lambda j, c: body(j, True), None)
    lax.fori_loop(full_lo, full_hi, lambda j, c: body(j, False), None)
    lax.fori_loop(full_hi, hi, lambda j, c: body(j, True), None)


def attend_kernel(heads, kv_heads, dim, block, bounds_ref, q_ref, kv_ref, start_ref, pos_ref, logit_ref,
                  att_ref, gated_ref, lse_ref, q2_ref, acc_ref, sum_ref):
    row = pl.program_id(0)
    group = q_ref.shape[1]
    repeat = heads // kv_heads
    for h in range(kv_heads):
        for g in range(repeat):
            at = slice((h * repeat + g) * dim, (h * repeat + g + 1) * dim)
            q2_ref[g * group:(g + 1) * group, :] = q_ref[0, :, at]
        acc_ref[...] = jnp.zeros_like(acc_ref)
        sum_ref[...] = jnp.zeros_like(sum_ref)

        def body(j, masked):
            at = pl.ds(pl.multiple_of(j * block, block), block)
            keys = kv_ref[0, at, h * dim:(h + 1) * dim]
            values = kv_ref[0, at, (kv_heads + h) * dim:(kv_heads + h + 1) * dim]
            if masked:
                spot = j * block + lax.broadcasted_iota(jnp.int32, (group, block), 1)
                allowed = (spot >= start_ref[0]) & (spot <= pos_ref[...])
            for g in range(repeat):
                part = slice(g * group, (g + 1) * group)
                weight = jnp.exp2(mm(q2_ref[part, :], keys, NT))
                if masked:
                    weight = jnp.where(allowed, weight, 0.0)
                total = weight[:, :dim]
                for i in range(1, block // dim):
                    total = total + weight[:, i * dim:(i + 1) * dim]
                sum_ref[part, :] += total
                acc_ref[part, :] += mm(weight.astype(bf16), values)

        bounds_loop(bounds_ref, row, body)
        for g in range(repeat):
            part = slice(g * group, (g + 1) * group)
            n = h * repeat + g
            at = slice(n * dim, (n + 1) * dim)
            total = jnp.sum(sum_ref[part, :], axis=1, keepdims=True)
            attended = acc_ref[part, :] / total
            att_ref[0, :, at] = attended.astype(bf16)
            gated_ref[0, :, at] = (attended * jax.nn.sigmoid(logit_ref[0, :, n:n + 1])).astype(bf16)
            lse_ref[0, n:n + 1, :] = jnp.log2(jnp.sum(sum_ref[part, :].T, axis=0, keepdims=True))


def attend(q, kv, bounds, start_col, pos_col, logits, heads, kv_heads, dim, block):
    rows, group, width = q.shape
    total = kv.shape[1]
    repeat = heads // kv_heads

    def by_row(*shape):
        return pl.BlockSpec((1, *shape), lambda r, *_: (r, 0, 0))

    return pl.pallas_call(
        functools.partial(attend_kernel, heads, kv_heads, dim, block),
        grid_spec=pltpu.PrefetchScalarGridSpec(
            num_scalar_prefetch=1,
            grid=(rows,),
            in_specs=[
                by_row(group, width), by_row(total, kv.shape[2]), by_row(group, 1), full((group, 1)),
                by_row(group, heads),
            ],
            out_specs=[by_row(group, width), by_row(group, width), by_row(heads, group)],
            scratch_shapes=[
                pltpu.VMEM((repeat * group, dim), bf16),
                pltpu.VMEM((repeat * group, dim), f32),
                pltpu.VMEM((repeat * group, dim), f32),
            ],
        ),
        out_shape=[
            jax.ShapeDtypeStruct((rows, group, width), bf16),
            jax.ShapeDtypeStruct((rows, group, width), bf16),
            jax.ShapeDtypeStruct((rows, heads, group), f32),
        ],
        compiler_params=params(),
        cost_estimate=cost(
            2 * rows * heads * group * total * dim, 2 * kv.size + 6 * q.size, rows * heads * group * total // 2
        ),
        name="attend",
    )(bounds, q, kv, start_col, pos_col, logits)


def attend_back_kernel(heads, kv_heads, dim, block, scale, bounds_ref, q_ref, kv_ref, dgated_ref, att_ref,
                       logit_ref, logit_row_ref, lse_ref, start_ref, pos_ref, nq_ref, rq_ref, cos_ref, sin_ref,
                       gain_ref, dq_ref, dlogit_ref, dkv_ref, dgain_ref,
                       q2_ref, da2_ref, delta_ref, lse2_ref, dq2_ref):
    row = pl.program_id(0)
    group = q_ref.shape[1]
    repeat = heads // kv_heads
    cosine, sine, gain = cos_ref[...], sin_ref[...], gain_ref[...]

    @pl.when(row == 0)
    def _():
        dgain_ref[...] = jnp.zeros_like(dgain_ref)

    dkv_ref[...] = jnp.zeros_like(dkv_ref)
    for h in range(kv_heads):
        for g in range(repeat):
            n = h * repeat + g
            at = slice(n * dim, (n + 1) * dim)
            part = slice(g * group, (g + 1) * group)
            q2_ref[part, :] = q_ref[0, :, at]
            grad = dgated_ref[0, :, at].astype(f32)
            sigma = jax.nn.sigmoid(logit_ref[0, :, n:n + 1])
            da2_ref[part, :] = (grad * sigma).astype(bf16)
            dot = jnp.sum((grad * att_ref[0, :, at].astype(f32)).T, axis=0, keepdims=True)
            sigma_row = jax.nn.sigmoid(logit_row_ref[0, n:n + 1, :])
            dlogit_ref[0, n:n + 1, :] = dot * sigma_row * (1.0 - sigma_row)
            delta_ref[:, part] = dot * sigma_row
            lse2_ref[:, part] = lse_ref[0, n:n + 1, :]
        dq2_ref[...] = jnp.zeros_like(dq2_ref)

        def body(j, masked):
            at = pl.ds(pl.multiple_of(j * block, block), block)
            keys = kv_ref[0, at, h * dim:(h + 1) * dim]
            values = kv_ref[0, at, (kv_heads + h) * dim:(kv_heads + h + 1) * dim]
            if masked:
                spot = j * block + lax.broadcasted_iota(jnp.int32, (block, group), 0)
                allowed = (spot >= start_ref[0]) & (spot <= pos_ref[...])
            dk = jnp.zeros((block, dim), f32)
            dv = jnp.zeros((block, dim), f32)
            for g in range(repeat):
                part = slice(g * group, (g + 1) * group)
                weight = jnp.exp2(mm(keys, q2_ref[part, :], NT) - lse2_ref[:, part])
                if masked:
                    weight = jnp.where(allowed, weight, 0.0)
                dv += mm(weight.astype(bf16), da2_ref[part, :])
                dprob = mm(values, da2_ref[part, :], NT)
                dscore = (weight * (dprob - delta_ref[:, part])).astype(bf16)
                dk += mm(dscore, q2_ref[part, :])
                dq2_ref[part, :] += mm(dscore, keys, TN)
            dkv_ref[0, at, h * dim:(h + 1) * dim] = (dk * (1.0 / log2e)).astype(bf16)
            dkv_ref[0, at, (kv_heads + h) * dim:(kv_heads + h + 1) * dim] = dv.astype(bf16)

        bounds_loop(bounds_ref, row, body)
        for g in range(repeat):
            n = h * repeat + g
            at = slice(n * dim, (n + 1) * dim)
            part = slice(g * group, (g + 1) * group)
            turned = (dq2_ref[part, :] * scale).astype(bf16).astype(f32)
            back = turned * cosine - pltpu.roll(turned, dim // 2, 1) * sine
            unit = nq_ref[0, :, at].astype(f32)
            dgain_ref[...] += jnp.sum(back * unit, axis=0, keepdims=True)
            inner = back * gain
            mean = jnp.mean(inner * unit, axis=1, keepdims=True)
            dq_ref[0, :, at] = (rq_ref[0, :, n:n + 1] * (inner - unit * mean)).astype(bf16)


def attend_back(q, kv, dgated, att, logits, logit_rows, lse, bounds, start_row, pos_row, nq, rq, tables, gain,
                heads, kv_heads, dim, block, scale):
    rows, group, width = q.shape
    total = kv.shape[1]
    repeat = heads // kv_heads
    cosine, sine = tables

    def by_row(*shape):
        return pl.BlockSpec((1, *shape), lambda r, *_: (r, 0, 0))

    wide = by_row(group, width)
    return pl.pallas_call(
        functools.partial(attend_back_kernel, heads, kv_heads, dim, block, scale),
        grid_spec=pltpu.PrefetchScalarGridSpec(
            num_scalar_prefetch=1,
            grid=(rows,),
            in_specs=[
                wide, by_row(total, kv.shape[2]), wide, wide, by_row(group, heads), by_row(heads, group),
                by_row(heads, group), by_row(1, group), full((1, group)), wide, by_row(group, heads),
                full((group, dim)), full((group, dim)), full((1, dim)),
            ],
            out_specs=[wide, by_row(heads, group), by_row(total, kv.shape[2]), full((1, dim))],
            scratch_shapes=[
                pltpu.VMEM((repeat * group, dim), bf16),
                pltpu.VMEM((repeat * group, dim), bf16),
                pltpu.VMEM((1, repeat * group), f32),
                pltpu.VMEM((1, repeat * group), f32),
                pltpu.VMEM((repeat * group, dim), f32),
            ],
        ),
        out_shape=[
            jax.ShapeDtypeStruct((rows, group, width), bf16),
            jax.ShapeDtypeStruct((rows, heads, group), f32),
            jax.ShapeDtypeStruct(kv.shape, bf16),
            jax.ShapeDtypeStruct((1, dim), f32),
        ],
        compiler_params=params(),
        cost_estimate=cost(
            5 * rows * heads * group * total * dim, 4 * kv.size + 10 * q.size, rows * heads * group * total // 2
        ),
        name="attend_back",
    )(bounds, q, kv, dgated, att, logits, logit_rows, lse, start_row, pos_row, nq, rq, cosine, sine, gain[None])


def key_back_kernel(kv_heads, dim, dkv_ref, nk_ref, rk_ref, cos_ref, sin_ref, gain_ref, dk_ref, dgain_ref):
    @pl.when(pl.program_id(0) == 0)
    def _():
        dgain_ref[...] = jnp.zeros_like(dgain_ref)

    for h in range(kv_heads):
        at = slice(h * dim, (h + 1) * dim)
        turned = dkv_ref[0, :, at].astype(f32)
        back = turned * cos_ref[...] - pltpu.roll(turned, dim // 2, 1) * sin_ref[...]
        unit = nk_ref[0, :, at].astype(f32)
        dgain_ref[...] += jnp.sum(back * unit, axis=0, keepdims=True)
        inner = back * gain_ref[...]
        mean = jnp.mean(inner * unit, axis=1, keepdims=True)
        dk_ref[0, :, at] = (rk_ref[0, :, h:h + 1] * (inner - unit * mean)).astype(bf16)
    dk_ref[0, :, kv_heads * dim:] = dkv_ref[0, :, kv_heads * dim:]


def key_back(dkv, nk, rk, tables, gain, kv_heads, dim):
    rows, group, width = dkv.shape

    def by_row(*shape):
        return pl.BlockSpec((1, *shape), lambda r: (r, 0, 0))

    return pl.pallas_call(
        functools.partial(key_back_kernel, kv_heads, dim),
        grid=(rows,),
        in_specs=[
            by_row(group, width), by_row(group, kv_heads * dim), by_row(group, kv_heads), full((group, dim)),
            full((group, dim)), full((1, dim)),
        ],
        out_specs=[by_row(group, width), full((1, dim))],
        out_shape=[jax.ShapeDtypeStruct((rows, group, width), bf16), jax.ShapeDtypeStruct((1, dim), f32)],
        compiler_params=params(),
        cost_estimate=cost(20 * dkv.size, 6 * dkv.size),
        name="key_back",
    )(dkv, nk, rk, *tables, gain[None])


def line_barrier(n, me):
    barrier = pltpu.get_barrier_semaphore()
    for way in (1, -1):
        @pl.when((me + way >= 0) & (me + way < n))
        def _():
            pl.semaphore_signal(barrier, inc=1, device_id={"tp": jnp.clip(me + way, 0, n - 1)}, device_id_type=MESH)
    edge = (me == 0) | (me == n - 1)

    @pl.when(edge)
    def _():
        pl.semaphore_wait(barrier, 1)

    @pl.when(jnp.logical_not(edge))
    def _():
        pl.semaphore_wait(barrier, 2)


def line_all_sum(n, seqs, rows, piece, finish, part_ref, out_ref, land_ref, stage_ref, sems):
    rs_send, rs_recv, ag_send, ag_recv = sems
    me = lax.axis_index("tp")
    line_barrier(n, me)
    cuts = [(q, c) for q in range(seqs) for c in range(rows // piece)]

    def inside(place):
        return (place >= 0) & (place < n)

    def at(ref, owner, s):
        q, c = cuts[s]
        return ref.at[q, pl.ds(pl.multiple_of(owner * rows + c * piece, piece), piece)]

    def reduce_copy(way, k, s, source):
        d = 0 if way == 1 else 1
        return pltpu.make_async_remote_copy(
            src_ref=source, dst_ref=land_ref.at[d, k - 1, s], send_sem=rs_send.at[d, k - 1, s],
            recv_sem=rs_recv.at[d, k - 1, s], device_id={"tp": jnp.clip(me + way, 0, n - 1)}, device_id_type=MESH)

    def spread_copy(way, k, s, owner):
        d = 0 if way == 1 else 1
        rows_ref = at(out_ref, owner, s)
        return pltpu.make_async_remote_copy(
            src_ref=rows_ref, dst_ref=rows_ref, send_sem=ag_send.at[d, k - 1, s],
            recv_sem=ag_recv.at[d, k - 1, s], device_id={"tp": jnp.clip(me + way, 0, n - 1)}, device_id_type=MESH)

    def reduce_step(k, s):
        for way in (1, -1):
            d = 0 if way == 1 else 1
            dest = me + way * (n - k)
            sends = inside(me + way) & inside(dest)
            safe = jnp.clip(dest, 0, n - 1)
            if k == 1:
                @pl.when(sends)
                def _():
                    reduce_copy(way, k, s, at(part_ref, safe, s)).start()
            else:
                got = sends & inside(me - way)

                @pl.when(got)
                def _():
                    reduce_copy(way, k - 1, s, stage_ref.at[d, 0, s]).wait_recv()
                    stage_ref[d, k - 2, s] = (
                        at(part_ref, safe, s)[...].astype(f32) + land_ref[d, k - 2, s].astype(f32)).astype(bf16)
                    reduce_copy(way, k, s, stage_ref.at[d, k - 2, s]).start()

                @pl.when(sends & jnp.logical_not(inside(me - way)))
                def _():
                    reduce_copy(way, k, s, at(part_ref, safe, s)).start()

    def own_step(s):
        q, c = cuts[s]
        for way in (1, -1):
            d = 0 if way == 1 else 1

            @pl.when(inside(me - way))
            def _():
                reduce_copy(way, n - 1, s, stage_ref.at[d, 0, s]).wait_recv()

            @pl.when(jnp.logical_not(inside(me - way)))
            def _():
                land_ref[d, n - 2, s] = jnp.zeros_like(land_ref[d, n - 2, s])
        total = (at(part_ref, me, s)[...].astype(f32) + land_ref[0, n - 2, s].astype(f32)
                 + land_ref[1, n - 2, s].astype(f32))
        at(out_ref, me, s)[...] = finish(q, c, total)

    def spread_step(k, s):
        for way in (1, -1):
            owner = me - way * (k - 1)
            if k > 1:
                @pl.when(inside(owner))
                def _():
                    spread_copy(way, k - 1, s, jnp.clip(owner, 0, n - 1)).wait_recv()
            if k < n:
                @pl.when(inside(owner) & inside(me + way))
                def _():
                    spread_copy(way, k, s, jnp.clip(owner, 0, n - 1)).start()

    stages = []
    for k in range(1, n):
        stages.append(functools.partial(reduce_step, k))

    def turn(s):
        own_step(s)
        spread_step(1, s)

    stages.append(turn)
    for k in range(2, n + 1):
        stages.append(functools.partial(spread_step, k))
    for step in range(len(cuts) + len(stages) - 1):
        for s in range(len(cuts)):
            if 0 <= step - s < len(stages):
                stages[step - s](s)
    for s in range(len(cuts)):
        for way in (1, -1):
            d = 0 if way == 1 else 1
            for k in range(1, n):
                dest = me + way * (n - k)

                @pl.when(inside(me + way) & inside(dest))
                def _():
                    reduce_copy(way, k, s, land_ref.at[d, 0, s]).wait_send()
                owner = me - way * (k - 1)

                @pl.when(inside(owner) & inside(me + way))
                def _():
                    spread_copy(way, k, s, jnp.clip(owner, 0, n - 1)).wait_send()


def line_scratch(n, seqs, rows, piece, width):
    count = seqs * (rows // piece)
    return [
        pltpu.VMEM((2, n - 1, count, piece, width), bf16),
        pltpu.VMEM((2, max(n - 2, 1), count, piece, width), bf16),
        pltpu.SemaphoreType.DMA((2, n - 1, count)), pltpu.SemaphoreType.DMA((2, n - 1, count)),
        pltpu.SemaphoreType.DMA((2, n - 1, count)), pltpu.SemaphoreType.DMA((2, n - 1, count)),
    ]


def norm_forward_kernel(n, seqs, rows, piece, part_ref, x_ref, gain_ref, out_ref, mid_ref, land_ref, stage_ref, *sems):
    def finish(q, c, total):
        at = slice(c * piece, (c + 1) * piece)
        mid = x_ref[q, at].astype(f32) + total
        mid_ref[q, at] = mid
        return (mid * rms_inverse(mid) * gain_ref[...]).astype(bf16)

    line_all_sum(n, seqs, rows, piece, finish, part_ref, out_ref, land_ref, stage_ref, sems)


def norm_back_kernel(n, seqs, rows, piece, part_ref, cot_ref, mid_ref, gain_ref, out_ref, dmid_ref, dgain_ref,
                     land_ref, stage_ref, *sems):
    dgain_ref[...] = jnp.zeros_like(dgain_ref)

    def finish(q, c, total):
        at = slice(c * piece, (c + 1) * piece)
        mid = mid_ref[q, at]
        inverse = rms_inverse(mid)
        unit = mid * inverse
        dgain_ref[...] += jnp.sum(total * unit, axis=0, keepdims=True)
        inner = total * gain_ref[...]
        mean = jnp.mean(inner * unit, axis=-1, keepdims=True)
        d_mid = cot_ref[q, at].astype(f32) + inverse * (inner - unit * mean)
        dmid_ref[q, at] = d_mid
        return d_mid.astype(bf16)

    line_all_sum(n, seqs, rows, piece, finish, part_ref, out_ref, land_ref, stage_ref, sems)


def line_call(kernel, n, local, part, others, extra, collective_id, name):
    seqs, rows, width = local
    piece = min(64, rows)
    vm = pl.BlockSpec(memory_space=pltpu.VMEM)
    shapes = [jax.ShapeDtypeStruct(part.shape, bf16), jax.ShapeDtypeStruct(local, f32), *extra]
    return pl.pallas_call(
        functools.partial(kernel, n, seqs, rows, piece),
        in_specs=[vm] * (1 + len(others)),
        out_specs=[vm] * len(shapes),
        out_shape=shapes,
        scratch_shapes=line_scratch(n, seqs, rows, piece, width),
        compiler_params=params(collective_id=collective_id, has_side_effects=True),
        cost_estimate=cost(20 * part.size, 100_000_000),
        name=name,
    )(part, *others)


def plane_place(n_uly):
    return lax.axis_index("ctx") * n_uly + lax.axis_index("uly")


def plane_device(place, n_uly):
    return {"ctx": place // n_uly, "uly": lax.rem(place, n_uly)}


def plane_barrier(bits, me, n_uly):
    barrier = pltpu.get_barrier_semaphore()
    for b in range(bits):
        pl.semaphore_signal(barrier, inc=1, device_id=plane_device(me ^ (1 << b), n_uly), device_id_type=MESH)
    pl.semaphore_wait(barrier, bits)


def ways(bits):
    upper = list(range(1, bits))
    return upper, upper[::-1]


def span(order):
    out = [0]
    for b in order:
        out += [e | (1 << b) for e in out]
    return out


def plane_gather_kernel(bits, n_uly, own_ref, out_ref, copy_sem, send_sem, recv_sem):
    me = plane_place(n_uly)
    rows, half = own_ref.shape[1], own_ref.shape[2] // 2
    plane_barrier(bits, me, n_uly)
    orders = [w + [0] for w in ways(bits)]

    def block(place, d):
        return out_ref.at[:, pl.ds(pl.multiple_of(place * rows, rows), rows), pl.ds(d * half, half)]

    def copy(d, level, e):
        bit = orders[d][level]
        source = own_ref.at[:, :, pl.ds(d * half, half)] if e == 0 else block(me ^ e, d)
        return pltpu.make_async_remote_copy(
            src_ref=source, dst_ref=block(me ^ e, d), send_sem=send_sem.at[d, e | (1 << bit)],
            recv_sem=recv_sem.at[d, e | (1 << bit)], device_id=plane_device(me ^ (1 << bit), n_uly),
            device_id_type=MESH)

    own = [pltpu.make_async_copy(own_ref.at[:, :, pl.ds(d * half, half)], block(me, d), copy_sem.at[d]) for d in range(2)]
    for c in own:
        c.start()
    for level in range(bits):
        for d in range(2):
            for e in span(orders[d][:level]):
                if level > 0 and e >> orders[d][level - 1] & 1:
                    continue
                copy(d, level, e).start()
        for d in range(2):
            for e in span(orders[d][:level]):
                copy(d, level, e).wait_recv()
                if level + 1 < bits:
                    copy(d, level + 1, e | (1 << orders[d][level])).start()
    for d in range(2):
        own[d].wait()
        for level in range(bits):
            for e in span(orders[d][:level]):
                copy(d, level, e).wait_send()


def plane_gather(own, sizes, collective_id):
    n_ctx, n_uly = sizes
    count = n_ctx * n_uly
    bits = count.bit_length() - 1
    seqs, rows, width = own.shape
    if own.size * count * 2 > 12 << 20 or count != 1 << bits or bits < 2:
        return lax.all_gather(own, ("ctx", "uly"), axis=1, tiled=True)
    vm = pl.BlockSpec(memory_space=pltpu.VMEM)
    return pl.pallas_call(
        functools.partial(plane_gather_kernel, bits, n_uly),
        in_specs=[vm], out_specs=vm,
        out_shape=jax.ShapeDtypeStruct((seqs, rows * count, width), own.dtype),
        scratch_shapes=[pltpu.SemaphoreType.DMA((2,)), pltpu.SemaphoreType.DMA((2, count)), pltpu.SemaphoreType.DMA((2, count))],
        compiler_params=params(collective_id=collective_id, has_side_effects=True),
        cost_estimate=cost(0, 100_000_000),
        name="plane_gather",
    )(own)


class PlaneSum:
    def __init__(self, bits, n_uly, make, store, buf_ref, land_ref, send, recv):
        self.bits, self.n_uly, self.make, self.store = bits, n_uly, make, store
        self.buf, self.land, self.send, self.recv = buf_ref, land_ref, send, recv
        self.me = plane_place(n_uly)
        width = buf_ref.shape[-1]
        half = max(width // 256, 1) * 128
        self.parts = [(0, half), (half, width - half)]
        self.orders = ways(bits)

    @staticmethod
    def scratch(bits, rows, width):
        n = 1 << bits
        return [
            pltpu.VMEM((n, rows, width), bf16), pltpu.VMEM((n - 1, rows, width), bf16),
            pltpu.SemaphoreType.DMA((3, n)), pltpu.SemaphoreType.DMA((3, n)),
        ]

    def first_copy(self, e):
        return pltpu.make_async_remote_copy(
            src_ref=self.buf.at[e], dst_ref=self.land.at[e - 1], send_sem=self.send.at[2, e],
            recv_sem=self.recv.at[2, e], device_id=plane_device(self.me ^ 1, self.n_uly), device_id_type=MESH)

    def copy(self, d, level, e):
        at = pl.ds(*self.parts[d])
        return pltpu.make_async_remote_copy(
            src_ref=self.buf.at[e, :, at], dst_ref=self.land.at[e - 1, :, at], send_sem=self.send.at[d, e],
            recv_sem=self.recv.at[d, e],
            device_id=plane_device(self.me ^ (1 << self.orders[d][level]), self.n_uly), device_id_type=MESH)

    def sent(self, d, level):
        return [(1 << self.orders[d][level]) | e for e in span(self.orders[d][level + 1:])]

    def compute(self):
        n = 1 << self.bits
        for e in range(1, n, 2):
            self.buf[e] = self.make(self.me ^ e).astype(bf16)
            self.first_copy(e).start()
        for e in range(0, n, 2):
            self.buf[e] = self.make(self.me ^ e).astype(bf16)

    def pair(self):
        for e in range(1, 1 << self.bits, 2):
            self.first_copy(e).wait_recv()
            self.buf[e - 1] = (self.buf[e - 1].astype(f32) + self.land[e - 1].astype(f32)).astype(bf16)

    def push(self, level):
        for d in range(2):
            for e in self.sent(d, level):
                self.copy(d, level, e).start()

    def pull(self, level):
        for d in range(2):
            at = pl.ds(*self.parts[d])
            for e in self.sent(d, level):
                kept = e ^ (1 << self.orders[d][level])
                self.copy(d, level, e).wait_recv()
                total = self.buf[kept, :, at].astype(f32) + self.land[e - 1, :, at].astype(f32)
                if level == self.bits - 2:
                    self.store(at, total)
                else:
                    self.buf[kept, :, at] = total.astype(bf16)

    def finish(self):
        for e in range(1, 1 << self.bits, 2):
            self.first_copy(e).wait_send()
        for d in range(2):
            for level in range(self.bits - 1):
                for e in self.sent(d, level):
                    self.copy(d, level, e).wait_send()


def blocks_sum_kernel(bits, n_uly, parts_ref, out_ref, *scratch):
    me = plane_place(n_uly)
    plane_barrier(bits, me, n_uly)
    seqs, rows = out_ref.shape[0], out_ref.shape[1]

    def make(place):
        return parts_ref[:, pl.ds(pl.multiple_of(place * rows, rows), rows)].reshape(seqs * rows, -1)

    def store(at, total):
        out_ref[:, :, at] = total.reshape(seqs, rows, -1).astype(out_ref.dtype)

    job = PlaneSum(bits, n_uly, make, store, *scratch)
    job.compute()
    job.pair()
    for level in range(bits - 1):
        job.push(level)
        job.pull(level)
    job.finish()


def blocks_sum(parts, sizes, collective_id):
    n_ctx, n_uly = sizes
    count = n_ctx * n_uly
    bits = count.bit_length() - 1
    seqs, total, width = parts.shape
    rows = total // count
    if parts.size * 2 > 12 << 20 or count != 1 << bits or bits < 2:
        return lax.psum_scatter(parts, ("ctx", "uly"), scatter_dimension=1, tiled=True)
    vm = pl.BlockSpec(memory_space=pltpu.VMEM)
    return pl.pallas_call(
        functools.partial(blocks_sum_kernel, bits, n_uly),
        in_specs=[vm],
        out_specs=vm,
        out_shape=jax.ShapeDtypeStruct((seqs, rows, width), bf16),
        scratch_shapes=PlaneSum.scratch(bits, seqs * rows, width),
        compiler_params=params(collective_id=collective_id, has_side_effects=True),
        cost_estimate=cost(10 * parts.size, 100_000_000),
        name="blocks_sum",
    )(parts)


def outer_sums_kernel(bits, n_uly, use, *refs):
    count, kinds = len(use), max(use) + 1
    lefts, refs = [refs[k] for k in use], refs[kinds:]
    rights, outs, scratch = refs[:count], refs[count:2 * count], refs[2 * count:]
    plane_barrier(bits, plane_place(n_uly), n_uly)
    jobs = []
    for i in range(count):
        each = outs[i].shape[0]

        def make(place, i=i, each=each):
            left = lefts[i][:, pl.ds(pl.multiple_of(place * each, each), each)]
            return mm(left, rights[i][...], TN)

        def store(at, total, i=i):
            outs[i][:, at] = total

        jobs.append(PlaneSum(bits, n_uly, make, store, *scratch[4 * i:4 * i + 4]))
    last = bits - 2
    for i in range(count + last + 1):
        if i < count:
            jobs[i].compute()
            jobs[i].pair()
            jobs[i].push(0)
        for level in range(last + 1):
            j = i - 1 - level
            if 0 <= j < count:
                jobs[j].pull(level)
                if level < last:
                    jobs[j].push(level + 1)
                else:
                    jobs[j].finish()


def outer_sums(kinds, use, rights, sizes, collective_id):
    lefts = [kinds[k] for k in use]
    n_ctx, n_uly = sizes
    places = n_ctx * n_uly
    bits = places.bit_length() - 1
    count = len(lefts)
    if places != 1 << bits or bits < 2 or lefts[0].shape[1] // places % 128:
        return [
            lax.psum_scatter(mm(l, r, TN).astype(bf16), ("ctx", "uly"), scatter_dimension=0, tiled=True).astype(f32)
            for l, r in zip(lefts, rights)
        ]
    vm = pl.BlockSpec(memory_space=pltpu.VMEM)
    shapes = [(l.shape[1] // places, r.shape[1]) for l, r in zip(lefts, rights)]
    scratch = []
    for shape in shapes:
        scratch += PlaneSum.scratch(bits, *shape)
    work = sum(l.size * r.shape[1] for l, r in zip(lefts, rights))
    return pl.pallas_call(
        functools.partial(outer_sums_kernel, bits, n_uly, use),
        in_specs=[vm] * (len(kinds) + count),
        out_specs=[vm] * count,
        out_shape=[jax.ShapeDtypeStruct(s, f32) for s in shapes],
        scratch_shapes=scratch,
        compiler_params=pltpu.CompilerParams(
            collective_id=collective_id, has_side_effects=True, vmem_limit_bytes=60 * 1024 * 1024),
        cost_estimate=cost(2 * work, 200_000_000),
        name="outer_sums",
    )(*kinds, *rights)


def flatten(values):
    return values.reshape(-1, values.shape[-1])


def spread(values):
    return lax.all_gather(values.astype(bf16), "tp", axis=1, tiled=True)


def collect(values):
    return lax.psum_scatter(values.astype(bf16), "tp", scatter_dimension=1, tiled=True).astype(f32)


def per_device(sizes, inputs, doc_ids, attn_norm, w_query, w_key, w_value, w_headgate, query_norm, key_norm, w_output,
               mlp_norm, w_gate, w_up, w_down, cotangent):
    n_tensor = lax.axis_size("tp")
    n_uly = sizes[1]
    seqs, rows, width = inputs.shape
    group = rows * n_tensor
    dim = query_norm.shape[0]
    heads = w_query.shape[1] // dim
    kv_heads = w_key.shape[1] // dim
    scale = dim ** (-0.5)
    plane = ("ctx", "uly")
    place = lax.axis_index("ctx") * n_uly + lax.axis_index("uly")
    block_start = place * group
    positions = block_start + jnp.arange(group, dtype=jnp.int32)
    tables = rope_tables(positions, dim)
    block = min(512, group)

    def wide(values):
        return values.reshape(seqs, group, -1)

    query_doc = lax.dynamic_slice_in_dim(doc_ids, block_start, group, 1)
    before = (doc_ids[:, None, :] >= 0) & (doc_ids[:, None, :] < query_doc[:, :, None])
    start = jnp.where(query_doc >= 0, jnp.sum(before.astype(jnp.int32), axis=-1), positions[None, :])
    lowest, highest = jnp.min(start, axis=1), jnp.max(start, axis=1)
    hi = jnp.full_like(lowest, (block_start + group + block - 1) // block)
    lo = lowest // block
    full_lo = jnp.clip((highest + block - 1) // block, lo, hi)
    full_hi = jnp.clip(jnp.full_like(lowest, (block_start + 1) // block), full_lo, hi)
    bounds = jnp.stack([lo, full_lo, full_hi, hi], axis=1)

    pad = 128 - heads
    w_first = jnp.concatenate([w_query, w_key, w_value, jnp.pad(w_headgate, ((0, 0), (0, pad)))], axis=1)
    q_cols, kv_cols = heads * dim, kv_heads * dim
    n_main = q_cols + 2 * kv_cols

    xs = inputs.astype(f32)
    inv_one = rms_inverse(xs)
    first = spread(xs * inv_one * attn_norm)
    q, kv, nq, nk, rq, rk, logits = (
        wide(m) for m in project(flatten(first), w_first, tables, query_norm, key_norm, heads, kv_heads, scale))
    cot_in, _ = lax.optimization_barrier((cotangent, first))
    cot_all = spread(cot_in)
    kv = plane_gather(kv, sizes, 0)
    att, gated, lse = attend(q, kv, bounds, start[:, :, None], positions[:, None], logits, heads, kv_heads, dim, block)

    local = inputs.shape
    second, middle = line_call(
        norm_forward_kernel, n_tensor, local, wide(mm(flatten(gated), w_output).astype(bf16)),
        (inputs, mlp_norm[None]), (), 1, "norm_forward")

    a2, cot = flatten(second), flatten(cot_all)
    gate, up = mm(a2, w_gate), mm(a2, w_up)
    d_hidden = mm(cot, w_down, NT)
    sig = jax.nn.sigmoid(gate)
    silu = gate * sig
    hidden = (silu * up).astype(bf16)
    d_gate = (d_hidden * up * sig * (1.0 + gate * (1.0 - sig))).astype(bf16)
    d_up = (d_hidden * silu).astype(bf16)
    d_second = (mm(d_gate, w_gate, NT) + mm(d_up, w_up, NT)).astype(bf16)
    d_branch, d_mid, grad_mlp_norm = line_call(
        norm_back_kernel, n_tensor, local, wide(d_second), (cotangent, middle, mlp_norm[None]),
        (jax.ShapeDtypeStruct((1, width), f32),), 2, "norm_back")

    late_hidden, d_branch = lax.optimization_barrier((hidden, d_branch))
    outputs = (middle + collect(wide(mm(late_hidden, w_down)))).astype(bf16)

    d_gated = wide(mm(flatten(d_branch), w_output, NT).astype(bf16))
    d_q, d_logit, d_kv, d_qgain = attend_back(
        q, kv, d_gated, att, logits, logits.transpose(0, 2, 1), lse, bounds, start[:, None, :], positions[None, :], nq,
        rq, tables, query_norm, heads, kv_heads, dim, block, scale)
    d_kv = blocks_sum(d_kv, sizes, 3)
    d_kv, d_kgain = key_back(d_kv, nk, rk, tables, key_norm, kv_heads, dim)
    d_logit = jnp.pad(d_logit.astype(bf16).transpose(0, 2, 1), ((0, 0), (0, 0), (0, pad)))
    d_all = flatten(jnp.concatenate([d_q, d_kv, d_logit], axis=-1))
    d_first = collect(wide(mm(d_all, w_first, NT)))

    grad_first, grad_output = outer_sums(
        (flatten(first), flatten(d_branch)), (0, 1), (d_all, flatten(gated)), sizes, 4)
    grad_gate, grad_up, grad_down = outer_sums((a2, cot), (0, 0, 1), (d_gate, d_up, hidden), sizes, 5)

    share = grad_first.shape[0]
    own_rows = lax.dynamic_slice_in_dim(w_first, place * share, share, 0).astype(f32)
    own_norm = jnp.sum(grad_first * own_rows, axis=1) / lax.dynamic_slice_in_dim(attn_norm, place * share, share, 0)
    grad_attn_norm = lax.dynamic_update_slice_in_dim(jnp.zeros((width,), f32), own_norm, place * share, 0)
    grad_attn_norm, grad_query_norm, grad_key_norm, grad_mlp_norm = lax.psum(
        (grad_attn_norm, d_qgain[0], d_kgain[0], grad_mlp_norm[0]), ("ctx", "uly", "tp"))

    unit = xs * inv_one
    inner = d_first * attn_norm
    grad_inputs = d_mid + inv_one * (inner - unit * jnp.mean(inner * unit, axis=-1, keepdims=True))
    return (
        outputs,
        grad_inputs,
        grad_attn_norm,
        grad_first[:, :q_cols],
        grad_first[:, q_cols:q_cols + kv_cols],
        grad_first[:, q_cols + kv_cols:n_main],
        grad_first[:, n_main:n_main + heads],
        grad_query_norm,
        grad_key_norm,
        grad_output.T,
        grad_mlp_norm,
        grad_gate,
        grad_up,
        grad_down.T,
    )


def solution(mesh):
    tokens = P(None, ("ctx", "uly", "tp"), None)
    column, line, whole = P(None, "tp"), P("tp", None), P()
    rows_split, cols_split = P(("ctx", "uly"), "tp"), P("tp", ("ctx", "uly"))
    return jax.shard_map(
        functools.partial(per_device, (mesh.shape["ctx"], mesh.shape["uly"])),
        mesh=mesh,
        in_specs=(
            tokens, whole, whole, column, column, column, column, whole, whole, line, whole, column, column, line,
            tokens,
        ),
        out_specs=(
            tokens, tokens, whole, rows_split, rows_split, rows_split, rows_split, whole, whole, cols_split, whole,
            rows_split, rows_split, cols_split,
        ),
        check_vma=False,
    )
```

time: 1410 us -> 841 us (0.60)
  waiting for transfers between devices: 878 us -> 76.4 us
  Pallas kernels: 0 us -> 562 us
  matrix products: 332 us -> 89.9 us
  other arithmetic: 98.1 us -> 24.8 us
    pallas_call x0 -> x10, Pallas kernels: none -> 562 us  [the longest x2 239 us: line_call(): pl.pallas_call(functools.partial(kernel, n, seqs, rows, piece), in_specs=...]
    reduce_scatter x13 -> x2, waiting for transfers between devices: 524 us -> 0.02 us  [collect(): lax.psum_scatter(values.astype(bf16), 'tp', scatter_dimension=1, tiled=True)]
    dot_general x30 -> x9, matrix products: 332 us -> 89.9 us  [mm(): return lax.dot_general(left, right, dims, preferred_element_type=f32)]
    all_gather x6 -> x2, waiting for transfers between devices: 318 us -> 76.3 us  [spread(): return lax.all_gather(values.astype(bf16), 'tp', axis=1, tiled=True)]
    unnamed x21 -> x4, waiting for transfers between devices: 36.4 us -> 0.07 us
    reduce_sum x7 -> x4, other arithmetic: 37.9 us -> 7.61 us  [the longest x1 2.58 us: per_device(): jnp.sum(before.astype(jnp.int32), axis=-1)]
    convert_element_type x15 -> x3, other arithmetic: 32.8 us -> 5.14 us  [the longest x1 2.63 us: per_device(): outputs = (middle + collect(wide(mm(late_hidden, w_down)))).astype(bf16)]
  transfers between devices with their start and end apart: 20 -> 4, of which waited for: 16 -> 1; matrix products, arithmetic and copies ran while one was open for 22% -> 8% of each run, Pallas kernels for 0% -> 40%
where the time goes in v1:
time: 841 us; the launch traced here: 836 us
  Pallas kernels  562 us (67%)
  matrix products  89.9 us (11%)
  waiting for transfers between devices  76.4 us (9%)
  blocking collectives  38.7 us (5%)
  local copies, waits for them, and re-layouts  28.7 us (3%)
  other arithmetic  24.8 us (3%)
  between operations  14.9 us (2%)
    pallas_call x2, Pallas kernels, line_call(): pl.pallas_call(functools.partial(kernel, n, seqs, rows, piece), in_specs=...  239 us
    pallas_call x2, Pallas kernels, outer_sums(): pl.pallas_call(functools.partial(outer_sums_kernel, bits, n_uly, use), in...  143 us
    pallas_call x1, Pallas kernels, blocks_sum(): pl.pallas_call(functools.partial(blocks_sum_kernel, bits, n_uly), in_spec...  94.4 us
    dot_general x9, matrix products, mm(): return lax.dot_general(left, right, dims, preferred_element_type=f32)  89.9 us
    all_gather x2, waiting for transfers between devices, spread(): return lax.all_gather(values.astype(bf16), 'tp', axis=1, tiled=True)  76.3 us
    pallas_call x1, Pallas kernels, plane_gather(): pl.pallas_call(functools.partial(plane_gather_kernel, bits, n_uly), in_sp...  48.7 us
    psum x1, blocking collectives, per_device(): lax.psum((grad_attn_norm, d_qgain[0], d_kgain[0], grad_mlp_norm[0]), ('ct...  38.7 us
    unnamed x106, local copies, waits for them, and re-layouts  19.6 us
  transfers between devices with their start and end apart: 4, of which 1 were waited for; matrix products, arithmetic and copies ran while one was open for 8% of the time, Pallas kernels for 40%

profile of v1, /device:TPU:0, one launch (start us, length us, event | category | flops | bytes accessed | tf_op | source)
XLA Modules:
  0.0 836.1 jit_solution(17727125760692807014)
XLA Ops:
  12.2 2.6 convert_reduce_fusion
  19.3 76.3 %all-gather.3.cloned.1.call-done = bf16[2,512,2048]{2,1,0:T(8,128)(2,1)} async-done(((bf16[2,128,2048]{2,1,0:T(8,128)(2,1)}), bf16[2,512,2048]{2,1,0:T(8,128)(2,1)}) %all-gather.3.cloned.1.call-update) | async-done | bytes 4194320 | tf_op jit(solution)/shard_map/all_gather | solution.py:791
  96.0 5.3 fusion.2.w_ref
  101.3 9.4 %project.1 = (bf16[1024,512]{1,0:T(8,128)(2,1)S(1)}, bf16[1024,512]{1,0:T(8,128)(2,1)S(1)}, bf16[1024,512]{1,0:T(8,128)(2,1)S(1)}, bf16[1024,256]{1,0:T(8,128)(2...) custom-call(bf16[1024,2048]{1,0:T(8,128)(2,1)} %bitcast.86, ...), custom_call_target="tpu_custom_call" | custom-call | flops 4831838208 | bytes 13107200 | tf_op jit(solution)/shard_map/project/pallas_call | solution.py:98
  118.2 48.7 %plane_gather.1.kv_ref = bf16[2,4096,512]{2,1,0:T(8,128)(2,1)} custom-call(bf16[2,512,512]{2,1,0:T(8,128)(2,1)S(1)} %bitcast.53), custom_call_target="tpu_custom_call" | custom-call | bytes 100000000 | tf_op jit(solution)/shard_map/plane_gather/pallas_call | solution.py:599
  167.0 9.1 %attend.1 = (bf16[2,512,512]{2,1,0:T(8,128)(2,1)S(1)}, bf16[2,512,512]{2,1,0:T(8,128)(2,1)S(1)}, f32[2,4,512]{2,1,0:T(4,128)S(1)}) custom-call(s32[2,4]{1,0:T(2,128)S(1)} %pad_add_fusion.bounds_ref, bf16[2,512,512]{2,1,0:T(8,128)(2,1)S(1)} %bitcast.69, bf16[2,4096,512]{2,1,0:T(8,128)(2,1)} %plane_gather.1.kv_ref, s32[2,512,1]{2,1,0:T(8,128)S(1)} %copy-done.14, ...), custom_call_target="tpu_custom_call" | custom-call | flops 4294967296 | bytes 11534336 | tf_op jit(solution)/shard_map/attend/pallas_call | solution.py:167
  176.1 4.4 convolution_convert_fusion.1
  180.5 120.0 %norm_forward.1 = (bf16[2,512,2048]{2,1,0:T(8,128)(2,1)}, f32[2,128,2048]{2,1,0:T(8,128)S(1)}) custom-call(bf16[2,512,2048]{2,1,0:T(8,128)(2,1)} %bitcast.74, bf16[2,128,2048]{2,1,0:T(8,128)(2,1)S(1)} %copy-done.2, f32[1,2048]{1,0:T(1,128)S(1)} %bitcast.58), custom_call_target="tpu_custom_call" | custom-call | flops 41943040 | bytes 100000000 | tf_op jit(solution)/shard_map/norm_forward/pallas_call | solution.py:514
  300.6 10.9 %fusion.25 = f32[1024,1536]{1,0:T(8,128)} fusion(bf16[1024,2048]{1,0:T(8,128)(2,1)} %bitcast.90, bf16[2048,1536]{1,0:T(8,128)(2,1)S(1)} %bitcast.85), kind=kOutput, calls=%fused_computation.63 | convolution fusion | flops 6442450944 | bytes 16777216 | tf_op jit(solution)/shard_map/dot_general | solution.py:25
  311.5 10.5 %fusion.26 = f32[1024,1536]{1,0:T(8,128)} fusion(bf16[1024,2048]{1,0:T(8,128)(2,1)S(1)} %bitcast.92, bf16[2048,1536]{1,0:T(8,128)(2,1)} %param.27), kind=kOutput, calls=%fused_computation.64 | convolution fusion | flops 6442450944 | bytes 16777216 | tf_op jit(solution)/shard_map/dot_general | solution.py:25
  322.0 16.0 %multiply_convert_fusion = (bf16[1024,1536]{1,0:T(8,128)(2,1)S(1)}, bf16[1024,1536]{1,0:T(8,128)(2,1)S(1)}, bf16[1024,1536]{1,0:T(8,128)(2,1)}) fusion(f32[1024,1536]{1,0:T(8,128)} %fusion.25, f32[1024,1536]{1,0:T(8,128)} %fusion.26, bf16[1024,2048]{1,0:T(8,128)(2,1)} %bitcast.88, bf16[1536,2048]{1,0:T(8,128)(2,1)} %param.28), kind=kOutput, calls=%fused_computation.4 | convolution fusion | flops 6466043904 | bytes 32505856 | tf_op jit(solution)/shard_map/dot_general | solution.py:25
  338.1 11.1 %fusion.27 = f32[1024,2048]{1,0:T(8,128)S(1)} fusion(bf16[1024,1536]{1,0:T(8,128)(2,1)S(1)} %get-tuple-element.125.refs_2_, bf16[2048,1536]{1,0:T(8,128)(2,1)} %param.26), kind=kOutput, calls=%fused_computation.65 | convolution fusion | flops 6442450944 | bytes 17825792 | tf_op jit(solution)/shard_map/dot_general | solution.py:25
  349.2 11.5 %add_convert_fusion = bf16[1024,2048]{1,0:T(8,128)(2,1)} fusion(f32[1024,2048]{1,0:T(8,128)S(1)} %fusion.27, bf16[1024,1536]{1,0:T(8,128)(2,1)S(1)} %get-tuple-element.124.refs_3_, bf16[2048,1536]{1,0:T(8,128)(2,1)} %param.27), kind=kOutput, calls=%fused_computation.3 | convolution fusion | flops 6446645248 | bytes 22020096 | tf_op jit(solution)/shard_map/dot_general | solution.py:25
  360.7 118.9 %norm_back.1 = (bf16[2,512,2048]{2,1,0:T(8,128)(2,1)}, f32[2,128,2048]{2,1,0:T(8,128)S(1)}, f32[1,2048]{1,0:T(1,128)S(1)}) custom-call(bf16[2,512,2048]{2,1,0:T(8,128)(2,1)} %bitcast.76, bf16[2,128,2048]{2,1,0:T(8,128)(2,1)S(1)} %copy-done.6, f32[2,128,2048]{2,1,0:T(8,128)S(1)} %copy-done.4, f32[1,2048]{1,0:T(1,128)S(1)} %bitcast.59), custom_call_target="tpu_custom_call" | custom-call | flops 41943040 | bytes 100000000 | tf_op jit(solution)/shard_map/norm_back/pallas_call | solution.py:514
  479.7 5.3 convolution_convert_fusion.2
  485.1 17.1 %attend_back.1 = (bf16[2,512,512]{2,1,0:T(8,128)(2,1)S(1)}, f32[2,4,512]{2,1,0:T(4,128)S(1)}, bf16[2,4096,512]{2,1,0:T(8,128)(2,1)}, f32[1,128]{1,0:T(1,128)S(1)}) custom-call(s32[2,4]{1,0:T(2,128)S(1)} %pad_add_fusion.bounds_ref, bf16[2,512,512]{2,1,0:T(8,128)(2,1)S(1)} %bitcast.70, bf16[2,4096,512]{2,1,0:T(8,128)(2,1)} %plane_gather.1.kv_ref, ...), custom_call_target="tpu_custom_call" | custom-call | flops 10737418240 | bytes 22020096 | tf_op jit(solution)/shard_map/attend_back/pallas_call | solution.py:273
  502.2 94.4 %blocks_sum.1.dkv_ref = bf16[2,512,512]{2,1,0:T(8,128)(2,1)S(1)} custom-call(bf16[2,4096,512]{2,1,0:T(8,128)(2,1)} %get-tuple-element.59.parts_ref), custom_call_target="tpu_custom_call" | custom-call | flops 41943040 | bytes 100000000 | tf_op jit(solution)/shard_map/blocks_sum/pallas_call | solution.py:711
  602.7 8.9 %fusion.6 = bf16[2,512,2048]{2,1,0:T(8,128)(2,1)} fusion(bf16[2,512,4]{2,1,0:T(8,128)(2,1)} %bitcast.79, bf16[2,512,512]{2,1,0:T(8,128)(2,1)S(1)} %get-tuple-element.62, bf16[2,512,512]{2,1,0:T(8,128)(2,1)S(1)} %get-tuple-element.58, bf16[2048,4]{1,0:T(8,128)(2,1)} %copy-done.36, bf16[2048,256]{1,0:T(8,128)(2,1)} %param.20, bf16[2048,256]{1,0:T(8,128)(2,1)} %param.19, ...), kind=kOutput, calls=%fused_computation.15 | convolution fusion | flops 4866965504 | bytes 10510336 | tf_op jit(solution)/shard_map/dot_general | solution.py:25
  611.7 11.3 %convolution_convert_fusion = bf16[1024,2048]{1,0:T(8,128)(2,1)} fusion(bf16[1024,1536]{1,0:T(8,128)(2,1)} %get-tuple-element.51.refs_4_, bf16[1536,2048]{1,0:T(8,128)(2,1)} %param.28), kind=kOutput, calls=%fused_computation.14 | convolution fusion | flops 6444548096 | bytes 13631488 | tf_op jit(solution)/shard_map/dot_general | solution.py:25
  625.8 46.1 %outer_sums.2 = (f32[256,1152]{1,0:T(8,128)}, f32[256,512]{1,0:T(8,128)}) custom-call(bf16[1024,2048]{1,0:T(8,128)(2,1)} %bitcast.87, bf16[1024,2048]{1,0:T(8,128)(2,1)} %bitcast.94, bf16[1024,1152]{1,0:T(8,128)(2,1)} %bitcast.77, bf16[1024,512]{1,0:T(8,128)(2,1)} %bitcast.68), custom_call_target="tpu_custom_call" | custom-call | flops 6979321856 | bytes 200000000 | tf_op jit(solution)/shard_map/outer_sums/pallas_call | solution.py:773
  674.7 97.3 %outer_sums.3 = (f32[256,1536]{1,0:T(8,128)}, f32[256,1536]{1,0:T(8,128)}, f32[256,1536]{1,0:T(8,128)}) custom-call(bf16[1024,2048]{1,0:T(8,128)(2,1)} %bitcast.91, bf16[1024,2048]{1,0:T(8,128)(2,1)} %bitcast.89, bf16[1024,1536]{1,0:T(8,128)(2,1)} %copy-done.46, bf16[1024,1536]{1,0:T(8,128)(2,1)} %copy-done.47, bf16[1024,1536]{1,0:T(8,128)(2,1)} %get-tuple-element.51.refs_4_), custom_call_target="tpu_custom_call" | custom-call | flops 19327352832 | bytes 200000000 | tf_op jit(solution)/shard_map/outer_sums/pallas_call | solution.py:773
  772.1 3.2 copy.78
  779.8 38.7 %all-reduce.2 = (f32[2048]{0:T(1024)}, f32[128]{0:T(128)}, f32[128]{0:T(128)}, f32[2048]{0:T(1024)}) all-reduce(f32[2048]{0:T(1024)S(1)} %divide_dynamic-update-slice_fusion, f32[128]{0:T(128)S(1)} %bitcast.61, f32[128]{0:T(128)S(1)} %bitcast.62, f32[2048]{0:T(1024)S(1)} %bitcast.60), channel_id=1, replica_groups=mesh['ctx'=2,'uly'=4,'tp'=4] {'ctx','uly','tp'}, use_global_device_ids=true, to_apply=%region_8.9 | all-reduce | flops 4352 | bytes 34816 | tf_op jit(solution)/shard_map/psum | solution.py:882
  822.2 2.6 add_convert_fusion.1
  (153 shorter events, 41.4 us)
Async XLA Ops:
  7.2 168.9 %copy-start = (bf16[512,2048]{1,0:T(8,128)(2,1)S(1)}, bf16[512,2048]{1,0:T(8,128)(2,1)}, u32[]{:S(2)}) copy-start(bf16[512,2048]{1,0:T(8,128)(2,1)} %param.24) | copy-start | bytes 6291460
  7.2 8.9 %copy-start.44 = (bf16[2048,4]{0,1:T(4,128)(2,1)S(1)}, bf16[2048,4]{0,1:T(4,128)(2,1)}, u32[]{:S(2)}) copy-start(bf16[2048,4]{0,1:T(4,128)(2,1)} %param.21) | copy-start | bytes 49156
  7.2 88.4 %all-gather.3.cloned.1.call-start = ((), (), s32[]{:S(2)}) async-start(), calls=%async_computation.2 | async-start | bytes 5242880 | tf_op jit(solution)/shard_map/all_gather | solution.py:791
  12.0 310.0 %all-gather.5.cloned.1.call-start = ((), (), s32[]{:S(2)}) async-start(), calls=%async_computation.3 | async-start | bytes 5242880 | tf_op jit(solution)/shard_map/all_gather | solution.py:791
  16.5 84.8 %copy-start.36 = (bf16[2048,4]{1,0:T(8,128)(2,1)}, bf16[2048,4]{1,0:T(8,128)(2,1)S(1)}, u32[]{:S(2)}) copy-start(bf16[2048,4]{1,0:T(8,128)(2,1)S(1)} %copy.70) | copy-start | bytes 49156
  95.7 5.6 copy-start.24
  95.7 5.6 copy-start.25
  95.7 724.7 %reduce-scatter.5.cloned.1.call-start = ((), (), s32[]{:S(2)}) async-start(), calls=%async_computation.5 | async-start | bytes 5242880 | tf_op jit(solution)/shard_map/reduce_scatter | solution.py:795
  118.2 48.8 %copy-start.14 = (s32[2,512,1]{2,1,0:T(8,128)S(1)}, s32[2,512,1]{2,1,0:T(8,128)}, u32[]{:S(2)}) copy-start(s32[2,512,1]{2,1,0:T(8,128)} %copy.72.start_ref) | copy-start | bytes 12292
  118.2 48.8 %copy-start.15 = (f32[2,512,4]{2,1,0:T(8,128)S(1)}, f32[2,512,4]{2,1,0:T(8,128)}, u32[]{:S(2)}) copy-start(f32[2,512,4]{2,1,0:T(8,128)} %copy.73.logit_ref) | copy-start | bytes 49156
  118.2 48.8 %copy-start.22 = (s32[512,1]{1,0:T(8,128)S(1)}, s32[512,1]{1,0:T(8,128)}, u32[]{:S(2)}) copy-start(s32[512,1]{1,0:T(8,128)} %iota_add_fusion.pos_ref) | copy-start | bytes 6148
  118.2 48.8 %copy-start.28 = (bf16[1024,512]{1,0:T(8,128)(2,1)S(1)}, bf16[1024,512]{1,0:T(8,128)(2,1)}, u32[]{:S(2)}) copy-start(bf16[1024,512]{1,0:T(8,128)(2,1)} %copy-done.27) | copy-start | bytes 3145732
  176.1 124.5 %slice-start = ((s8[6291456]{0:T(1024)(128)(4,1)}), s8[4194304]{0:T(1024)(128)(4,1)S(1)}, s32[]{:S(2)}) async-start(s8[6291456]{0:T(1024)(128)(4,1)} %bitcast.84), calls=%async_computation.6 | async-start | bytes 8388608
  176.1 124.5 %slice-start.1 = ((s8[6291456]{0:T(1024)(128)(4,1)}), s8[2097152]{0:T(1024)(128)(4,1)S(1)}, s32[]{:S(2)}) async-start(s8[6291456]{0:T(1024)(128)(4,1)} %bitcast.84), calls=%async_computation.7 | async-start | bytes 4194304
  300.6 10.9 %copy-start.3 = (f32[2,128,2048]{2,1,0:T(8,128)}, f32[2,128,2048]{2,1,0:T(8,128)S(1)}, u32[]{:S(2)}) copy-start(f32[2,128,2048]{2,1,0:T(8,128)S(1)} %get-tuple-element.47.mid_ref) | copy-start | bytes 6291460
  300.6 10.9 %copy-start.45 = (bf16[2,512,2048]{2,1,0:T(8,128)(2,1)S(1)}, bf16[2,512,2048]{2,1,0:T(8,128)(2,1)}, u32[]{:S(2)}) copy-start(bf16[2,512,2048]{2,1,0:T(8,128)(2,1)} %get-tuple-element.48) | copy-start | bytes 12582916
  338.0 11.1 %copy-start.46 = (bf16[1024,1536]{1,0:T(8,128)(2,1)}, bf16[1024,1536]{1,0:T(8,128)(2,1)S(1)}, u32[]{:S(2)}) copy-start(bf16[1024,1536]{1,0:T(8,128)(2,1)S(1)} %get-tuple-element.125.refs_2_) | copy-start | bytes 9437188
  338.0 11.1 %copy-start.47 = (bf16[1024,1536]{1,0:T(8,128)(2,1)}, bf16[1024,1536]{1,0:T(8,128)(2,1)S(1)}, u32[]{:S(2)}) copy-start(bf16[1024,1536]{1,0:T(8,128)(2,1)S(1)} %get-tuple-element.124.refs_3_) | copy-start | bytes 9437188
  349.1 11.6 %copy-start.4 = (f32[2,128,2048]{2,1,0:T(8,128)S(1)}, f32[2,128,2048]{2,1,0:T(8,128)}, u32[]{:S(2)}) copy-start(f32[2,128,2048]{2,1,0:T(8,128)} %copy-done.3) | copy-start | bytes 6291460
  349.2 11.6 %copy-start.6 = (bf16[2,128,2048]{2,1,0:T(8,128)(2,1)S(1)}, bf16[2,128,2048]{2,1,0:T(8,128)(2,1)}, u32[]{:S(2)}) copy-start(bf16[2,128,2048]{2,1,0:T(8,128)(2,1)} %cot_ref.1) | copy-start | bytes 3145732
  611.7 210.5 %reduce-scatter.3.cloned.1.call-start = ((), (), s32[]{:S(2)}) async-start(), calls=%async_computation.4 | async-start | bytes 5242880 | tf_op jit(solution)/shard_map/reduce_scatter | solution.py:795
  772.0 7.5 copy-start.40
  772.0 48.3 %copy-start.43 = (f32[2,128]{1,0:T(2,128)S(1)}, f32[2,128]{1,0:T(2,128)}, u32[]{:S(2)}) copy-start(f32[2,128]{1,0:T(2,128)} %copy-done.42) | copy-start | bytes 3076
  772.1 50.1 %copy-start.5 = (f32[2,128,2048]{2,1,0:T(8,128)S(1)}, f32[2,128,2048]{2,1,0:T(8,128)}, u32[]{:S(2)}) copy-start(f32[2,128,2048]{2,1,0:T(8,128)} %copy-done.3) | copy-start | bytes 6291460
  (30 other events, 87.5 us)
Sparse Core Ops, SparseCore 0:
  12.2 83.4 all-gather.2
  97.2 79.2 all-gather.4
  611.8 77.9 reduce-scatter.4
  692.1 77.2 reduce-scatter.2

commit v2 on v1

--- a/solution.py
+++ b/solution.py
@@ -13,7 +13,7 @@
 log2e = 1.0 / math.log(2.0)
 bf16 = jnp.bfloat16
 f32 = jnp.float32
-vmem_bytes = 48 * 1024 * 1024
+vmem_bytes = 61 * 1024 * 1024
 
 MESH = pl.DeviceIdType.MESH
 NT = (((1,), (1,)), ((), ()))
@@ -358,157 +358,176 @@
         pl.semaphore_wait(barrier, 2)
 
 
-def line_all_sum(n, seqs, rows, piece, finish, part_ref, out_ref, land_ref, stage_ref, sems):
-    rs_send, rs_recv, ag_send, ag_recv = sems
-    me = lax.axis_index("tp")
-    line_barrier(n, me)
-    cuts = [(q, c) for q in range(seqs) for c in range(rows // piece)]
-
-    def inside(place):
-        return (place >= 0) & (place < n)
-
-    def at(ref, owner, s):
-        q, c = cuts[s]
-        return ref.at[q, pl.ds(pl.multiple_of(owner * rows + c * piece, piece), piece)]
-
-    def reduce_copy(way, k, s, source):
+def line_and_plane_barrier(n, me, bits, n_uly):
+    barrier = pltpu.get_barrier_semaphore()
+    place = plane_place(n_uly)
+    for way in (1, -1):
+        @pl.when((me + way >= 0) & (me + way < n))
+        def _():
+            pl.semaphore_signal(barrier, inc=1, device_id={"tp": jnp.clip(me + way, 0, n - 1)}, device_id_type=MESH)
+    for b in range(bits):
+        pl.semaphore_signal(barrier, inc=1, device_id=plane_device(place ^ (1 << b), n_uly), device_id_type=MESH)
+    edge = (me == 0) | (me == n - 1)
+
+    @pl.when(edge)
+    def _():
+        pl.semaphore_wait(barrier, bits + 1)
+
+    @pl.when(jnp.logical_not(edge))
+    def _():
+        pl.semaphore_wait(barrier, bits + 2)
+
+
+class LineSum:
+    def __init__(self, n, pieces, part_at, own, land_ref, sems, out_at=None):
+        self.n, self.pieces, self.part_at, self.own, self.land, self.out_at = n, pieces, part_at, own, land_ref, out_at
+        self.rs_send, self.rs_recv = sems[:2]
+        if out_at:
+            self.ag_send, self.ag_recv = sems[2:]
+        self.me = lax.axis_index("tp")
+        self.stages = [functools.partial(self.reduce_step, k) for k in range(1, n)] + [self.own_step]
+        if out_at:
+            self.stages += [functools.partial(self.spread_step, k) for k in range(2, n + 1)]
+
+    def inside(self, place):
+        return (place >= 0) & (place < self.n)
+
+    def near(self, way):
+        return {"tp": jnp.clip(self.me + way, 0, self.n - 1)}
+
+    def reduce_copy(self, way, k, s, source):
         d = 0 if way == 1 else 1
         return pltpu.make_async_remote_copy(
-            src_ref=source, dst_ref=land_ref.at[d, k - 1, s], send_sem=rs_send.at[d, k - 1, s],
-            recv_sem=rs_recv.at[d, k - 1, s], device_id={"tp": jnp.clip(me + way, 0, n - 1)}, device_id_type=MESH)
-
-    def spread_copy(way, k, s, owner):
+            src_ref=source, dst_ref=self.land.at[d, k - 1, s], send_sem=self.rs_send.at[d, k - 1, s],
+            recv_sem=self.rs_recv.at[d, k - 1, s], device_id=self.near(way), device_id_type=MESH)
+
+    def spread_copy(self, way, k, s, owner):
         d = 0 if way == 1 else 1
-        rows_ref = at(out_ref, owner, s)
+        rows = self.out_at(jnp.clip(owner, 0, self.n - 1), s)
         return pltpu.make_async_remote_copy(
-            src_ref=rows_ref, dst_ref=rows_ref, send_sem=ag_send.at[d, k - 1, s],
-            recv_sem=ag_recv.at[d, k - 1, s], device_id={"tp": jnp.clip(me + way, 0, n - 1)}, device_id_type=MESH)
-
-    def reduce_step(k, s):
+            src_ref=rows, dst_ref=rows, send_sem=self.ag_send.at[d, k - 1, s], recv_sem=self.ag_recv.at[d, k - 1, s],
+            device_id=self.near(way), device_id_type=MESH)
+
+    def reduce_step(self, k, s):
         for way in (1, -1):
             d = 0 if way == 1 else 1
-            dest = me + way * (n - k)
-            sends = inside(me + way) & inside(dest)
-            safe = jnp.clip(dest, 0, n - 1)
-            if k == 1:
-                @pl.when(sends)
+            first = jnp.logical_not(self.inside(self.me - way))
+            dest = self.me + way * (self.n - k)
+            part = self.part_at(jnp.clip(dest, 0, self.n - 1), s)
+
+            @pl.when(first & self.inside(dest))
+            def _():
+                self.reduce_copy(way, k, s, part).start()
+
+            if k > 1:
+                @pl.when(self.inside(self.me - way) & self.inside(dest))
                 def _():
-                    reduce_copy(way, k, s, at(part_ref, safe, s)).start()
-            else:
-                got = sends & inside(me - way)
-
-                @pl.when(got)
-                def _():
-                    reduce_copy(way, k - 1, s, stage_ref.at[d, 0, s]).wait_recv()
-                    stage_ref[d, k - 2, s] = (
-                        at(part_ref, safe, s)[...].astype(f32) + land_ref[d, k - 2, s].astype(f32)).astype(bf16)
-                    reduce_copy(way, k, s, stage_ref.at[d, k - 2, s]).start()
-
-                @pl.when(sends & jnp.logical_not(inside(me - way)))
-                def _():
-                    reduce_copy(way, k, s, at(part_ref, safe, s)).start()
-
-    def own_step(s):
-        q, c = cuts[s]
+                    landed = self.land.at[d, k - 2, s]
+                    self.reduce_copy(way, k - 1, s, landed).wait_recv()
+                    landed[...] = (part[...].astype(f32) + landed[...].astype(f32)).astype(bf16)
+                    self.reduce_copy(way, k, s, landed).start()
+
+    def own_step(self, s):
         for way in (1, -1):
             d = 0 if way == 1 else 1
-
-            @pl.when(inside(me - way))
+            landed = self.land.at[d, self.n - 2, s]
+
+            @pl.when(self.inside(self.me - way))
             def _():
-                reduce_copy(way, n - 1, s, stage_ref.at[d, 0, s]).wait_recv()
-
-            @pl.when(jnp.logical_not(inside(me - way)))
+                self.reduce_copy(way, self.n - 1, s, landed).wait_recv()
+
+            @pl.when(jnp.logical_not(self.inside(self.me - way)))
             def _():
-                land_ref[d, n - 2, s] = jnp.zeros_like(land_ref[d, n - 2, s])
-        total = (at(part_ref, me, s)[...].astype(f32) + land_ref[0, n - 2, s].astype(f32)
-                 + land_ref[1, n - 2, s].astype(f32))
-        at(out_ref, me, s)[...] = finish(q, c, total)
-
-    def spread_step(k, s):
+                landed[...] = jnp.zeros_like(landed)
+
+        total = self.part_at(self.me, s)[...].astype(f32)
+        for d in range(2):
+            total = total + self.land[d, self.n - 2, s].astype(f32)
+        rows = self.own(s, total)
+        if self.out_at:
+            self.out_at(self.me, s)[...] = rows
+            self.spread_step(1, s)
+
+    def spread_step(self, k, s):
         for way in (1, -1):
-            owner = me - way * (k - 1)
+            owner = self.me - way * (k - 1)
             if k > 1:
-                @pl.when(inside(owner))
+                @pl.when(self.inside(owner))
                 def _():
-                    spread_copy(way, k - 1, s, jnp.clip(owner, 0, n - 1)).wait_recv()
-            if k < n:
-                @pl.when(inside(owner) & inside(me + way))
+                    self.spread_copy(way, k - 1, s, owner).wait_recv()
+            if k < self.n:
+                @pl.when(self.inside(owner) & self.inside(self.me + way))
                 def _():
-                    spread_copy(way, k, s, jnp.clip(owner, 0, n - 1)).start()
-
-    stages = []
-    for k in range(1, n):
-        stages.append(functools.partial(reduce_step, k))
-
-    def turn(s):
-        own_step(s)
-        spread_step(1, s)
-
-    stages.append(turn)
-    for k in range(2, n + 1):
-        stages.append(functools.partial(spread_step, k))
-    for step in range(len(cuts) + len(stages) - 1):
-        for s in range(len(cuts)):
-            if 0 <= step - s < len(stages):
-                stages[step - s](s)
-    for s in range(len(cuts)):
-        for way in (1, -1):
-            d = 0 if way == 1 else 1
-            for k in range(1, n):
-                dest = me + way * (n - k)
-
-                @pl.when(inside(me + way) & inside(dest))
-                def _():
-                    reduce_copy(way, k, s, land_ref.at[d, 0, s]).wait_send()
-                owner = me - way * (k - 1)
-
-                @pl.when(inside(owner) & inside(me + way))
-                def _():
-                    spread_copy(way, k, s, jnp.clip(owner, 0, n - 1)).wait_send()
+                    self.spread_copy(way, k, s, owner).start()
+
+    def drain_reduce(self):
+        for s in range(self.pieces):
+            for way in (1, -1):
+                for k in range(1, self.n):
+                    @pl.when(self.inside(self.me + way) & self.inside(self.me + way * (self.n - k)))
+                    def _():
+                        self.reduce_copy(way, k, s, self.land.at[0, 0, s]).wait_send()
+
+    def drain_spread(self):
+        for s in range(self.pieces):
+            for way in (1, -1):
+                for k in range(1, self.n):
+                    owner = self.me - way * (k - 1)
+
+                    @pl.when(self.inside(owner) & self.inside(self.me + way))
+                    def _():
+                        self.spread_copy(way, k, s, owner).wait_send()
+
+    def run(self, beside=()):
+        beside, done = list(beside), 0
+        slots = self.pieces * len(self.stages)
+        for step in range(self.pieces + len(self.stages) - 1):
+            for s in range(self.pieces):
+                if 0 <= step - s < len(self.stages):
+                    self.stages[step - s](s)
+                    slots -= 1
+                    until = len(beside) if slots == 0 else done + -(-(len(beside) - done) // (slots + 1))
+                    for item in beside[done:until]:
+                        item()
+                    done = until
+        self.drain_reduce()
+        self.drain_spread()
+
+
+def line_all_sum(n, seqs, rows, piece, finish, part_ref, out_ref, land_ref, sems, beside=()):
+    cuts = [(q, c) for q in range(seqs) for c in range(rows // piece)]
+
+    def at(ref):
+        return lambda owner, s: ref.at[
+            cuts[s][0], pl.ds(pl.multiple_of(owner * rows + cuts[s][1] * piece, piece), piece)]
+
+    LineSum(n, len(cuts), at(part_ref), lambda s, total: finish(*cuts[s], total), land_ref, sems, at(out_ref)).run(
+        beside)
 
 
 def line_scratch(n, seqs, rows, piece, width):
     count = seqs * (rows // piece)
     return [
         pltpu.VMEM((2, n - 1, count, piece, width), bf16),
-        pltpu.VMEM((2, max(n - 2, 1), count, piece, width), bf16),
         pltpu.SemaphoreType.DMA((2, n - 1, count)), pltpu.SemaphoreType.DMA((2, n - 1, count)),
         pltpu.SemaphoreType.DMA((2, n - 1, count)), pltpu.SemaphoreType.DMA((2, n - 1, count)),
     ]
 
 
-def norm_forward_kernel(n, seqs, rows, piece, part_ref, x_ref, gain_ref, out_ref, mid_ref, land_ref, stage_ref, *sems):
+def norm_forward_kernel(n, seqs, rows, piece, part_ref, x_ref, gain_ref, out_ref, mid_ref, land_ref, *sems):
     def finish(q, c, total):
         at = slice(c * piece, (c + 1) * piece)
         mid = x_ref[q, at].astype(f32) + total
         mid_ref[q, at] = mid
         return (mid * rms_inverse(mid) * gain_ref[...]).astype(bf16)
 
-    line_all_sum(n, seqs, rows, piece, finish, part_ref, out_ref, land_ref, stage_ref, sems)
-
-
-def norm_back_kernel(n, seqs, rows, piece, part_ref, cot_ref, mid_ref, gain_ref, out_ref, dmid_ref, dgain_ref,
-                     land_ref, stage_ref, *sems):
-    dgain_ref[...] = jnp.zeros_like(dgain_ref)
-
-    def finish(q, c, total):
-        at = slice(c * piece, (c + 1) * piece)
-        mid = mid_ref[q, at]
-        inverse = rms_inverse(mid)
-        unit = mid * inverse
-        dgain_ref[...] += jnp.sum(total * unit, axis=0, keepdims=True)
-        inner = total * gain_ref[...]
-        mean = jnp.mean(inner * unit, axis=-1, keepdims=True)
-        d_mid = cot_ref[q, at].astype(f32) + inverse * (inner - unit * mean)
-        dmid_ref[q, at] = d_mid
-        return d_mid.astype(bf16)
-
-    line_all_sum(n, seqs, rows, piece, finish, part_ref, out_ref, land_ref, stage_ref, sems)
+    line_barrier(n, lax.axis_index("tp"))
+    line_all_sum(n, seqs, rows, piece, finish, part_ref, out_ref, land_ref, sems)
 
 
 def line_call(kernel, n, local, part, others, extra, collective_id, name):
     seqs, rows, width = local
-    piece = min(64, rows)
+    piece = min(32, rows)
     vm = pl.BlockSpec(memory_space=pltpu.VMEM)
     shapes = [jax.ShapeDtypeStruct(part.shape, bf16), jax.ShapeDtypeStruct(local, f32), *extra]
     return pl.pallas_call(
@@ -625,15 +644,21 @@
             pltpu.SemaphoreType.DMA((3, n)), pltpu.SemaphoreType.DMA((3, n)),
         ]
 
+    def slot(self, e):
+        return e
+
+    def view(self, ref, i, d):
+        return ref.at[(i, *[slice(None)] * (len(ref.shape) - 2), pl.ds(*self.parts[d]))]
+
     def first_copy(self, e):
         return pltpu.make_async_remote_copy(
             src_ref=self.buf.at[e], dst_ref=self.land.at[e - 1], send_sem=self.send.at[2, e],
             recv_sem=self.recv.at[2, e], device_id=plane_device(self.me ^ 1, self.n_uly), device_id_type=MESH)
 
     def copy(self, d, level, e):
-        at = pl.ds(*self.parts[d])
         return pltpu.make_async_remote_copy(
-            src_ref=self.buf.at[e, :, at], dst_ref=self.land.at[e - 1, :, at], send_sem=self.send.at[d, e],
+            src_ref=self.view(self.buf, self.slot(e), d), dst_ref=self.view(self.land, e - 1, d),
+            send_sem=self.send.at[d, e],
             recv_sem=self.recv.at[d, e],
             device_id=plane_device(self.me ^ (1 << self.orders[d][level]), self.n_uly), device_id_type=MESH)
 
@@ -651,7 +676,8 @@
     def pair(self):
         for e in range(1, 1 << self.bits, 2):
             self.first_copy(e).wait_recv()
-            self.buf[e - 1] = (self.buf[e - 1].astype(f32) + self.land[e - 1].astype(f32)).astype(bf16)
+            kept = self.slot(e - 1)
+            self.buf[kept] = (self.buf[kept].astype(f32) + self.land[e - 1].astype(f32)).astype(bf16)
 
     def push(self, level):
         for d in range(2):
@@ -660,15 +686,14 @@
 
     def pull(self, level):
         for d in range(2):
-            at = pl.ds(*self.parts[d])
             for e in self.sent(d, level):
-                kept = e ^ (1 << self.orders[d][level])
+                kept = self.view(self.buf, self.slot(e ^ (1 << self.orders[d][level])), d)
                 self.copy(d, level, e).wait_recv()
-                total = self.buf[kept, :, at].astype(f32) + self.land[e - 1, :, at].astype(f32)
+                total = kept[...].astype(f32) + self.view(self.land, e - 1, d)[...].astype(f32)
                 if level == self.bits - 2:
-                    self.store(at, total)
+                    self.store(pl.ds(*self.parts[d]), total)
                 else:
-                    self.buf[kept, :, at] = total.astype(bf16)
+                    kept[...] = total.astype(bf16)
 
     def finish(self):
         for e in range(1, 1 << self.bits, 2):
@@ -753,13 +778,18 @@
                     jobs[j].finish()
 
 
+def fits_plane(sizes, width):
+    places = sizes[0] * sizes[1]
+    return places & (places - 1) == 0 and places >= 4 and width // places % 128 == 0
+
+
 def outer_sums(kinds, use, rights, sizes, collective_id):
     lefts = [kinds[k] for k in use]
     n_ctx, n_uly = sizes
     places = n_ctx * n_uly
     bits = places.bit_length() - 1
     count = len(lefts)
-    if places != 1 << bits or bits < 2 or lefts[0].shape[1] // places % 128:
+    if not fits_plane(sizes, lefts[0].shape[1]):
         return [
             lax.psum_scatter(mm(l, r, TN).astype(bf16), ("ctx", "uly"), scatter_dimension=0, tiled=True).astype(f32)
             for l, r in zip(lefts, rights)
@@ -777,10 +807,618 @@
         out_shape=[jax.ShapeDtypeStruct(s, f32) for s in shapes],
         scratch_shapes=scratch,
         compiler_params=pltpu.CompilerParams(
-            collective_id=collective_id, has_side_effects=True, vmem_limit_bytes=60 * 1024 * 1024),
+            collective_id=collective_id, has_side_effects=True, vmem_limit_bytes=vmem_bytes),
         cost_estimate=cost(2 * work, 200_000_000),
         name="outer_sums",
     )(*kinds, *rights)
+
+
+def back_finish(piece, cot_ref, mid_ref, gain_ref, dmid_ref, dgain_ref):
+    def finish(q, c, total):
+        at = slice(c * piece, (c + 1) * piece)
+        mid = mid_ref[q, at]
+        inverse = rms_inverse(mid)
+        unit = mid * inverse
+        dgain_ref[...] += jnp.sum(total * unit, axis=0, keepdims=True)
+        inner = total * gain_ref[...]
+        mean = jnp.mean(inner * unit, axis=-1, keepdims=True)
+        d_mid = cot_ref[q, at].astype(f32) + inverse * (inner - unit * mean)
+        dmid_ref[q, at] = d_mid
+        return d_mid.astype(bf16)
+
+    return finish
+
+
+def plain_back_kernel(n, seqs, rows, piece, part_ref, cot_ref, mid_ref, gain_ref, out_ref, dmid_ref, dgain_ref,
+                      land_ref, *sems):
+    dgain_ref[...] = jnp.zeros_like(dgain_ref)
+    line_barrier(n, lax.axis_index("tp"))
+    line_all_sum(n, seqs, rows, piece, back_finish(piece, cot_ref, mid_ref, gain_ref, dmid_ref, dgain_ref), part_ref,
+                 out_ref, land_ref, sems)
+
+
+class StreamedOuter:
+    def __init__(self, jobs, each, left_slots, right_slots, left_sems, right_sems):
+        self.jobs, self.each = jobs, each
+        self.left, self.right, self.left_sems, self.right_sems = left_slots, right_slots, left_sems, right_sems
+
+    def right_copy(self, i):
+        _, right, half, _ = self.jobs[i]
+        wide = self.right.shape[-1]
+        return pltpu.make_async_copy(
+            right.at[:, pl.ds(half * wide, wide)], self.right.at[i % 2], self.right_sems.at[i % 2])
+
+    def left_copy(self, i, turn, place):
+        at = pl.ds(pl.multiple_of(place * self.each, self.each), self.each)
+        return pltpu.make_async_copy(self.jobs[i][0].at[:, at], self.left.at[turn % 2], self.left_sems.at[turn % 2])
+
+    def product(self, i, turn, places, take):
+        if turn == 0:
+            if i == 0:
+                self.right_copy(0).start()
+                self.left_copy(0, 0, places[0]).start()
+            self.right_copy(i).wait()
+            if i + 1 < len(self.jobs):
+                self.right_copy(i + 1).start()
+        if turn + 1 < len(places):
+            self.left_copy(i, turn + 1, places[turn + 1]).start()
+        self.left_copy(i, turn, places[turn]).wait()
+        value = mm(self.left[turn % 2], self.right[i % 2], TN)
+        if turn + 1 == len(places) and i + 1 < len(self.jobs):
+            self.left_copy(i + 1, 0, places[0]).start()
+        take(value)
+
+
+def norm_back_kernel(n, seqs, rows, piece, bits, n_uly, part_ref, cot_ref, mid_ref, gain_ref, a2_ref, cot_all_ref,
+                     dgate_ref, dup_ref, hidden_ref, out_ref, dmid_ref, dgain_ref, ggate_ref, gup_ref, gdown_ref,
+                     land_ref, rs_send, rs_recv, ag_send, ag_recv, left_slots, right_slots, left_sems, right_sems,
+                     *plane_scratch):
+    dgain_ref[...] = jnp.zeros_like(dgain_ref)
+
+    finish = back_finish(piece, cot_ref, mid_ref, gain_ref, dmid_ref, dgain_ref)
+    wide = right_slots.shape[-1]
+    halves = ggate_ref.shape[1] // wide
+    jobs = [
+        (left, right, half, out)
+        for left, right, out in (
+            (a2_ref, dgate_ref, ggate_ref), (a2_ref, dup_ref, gup_ref), (cot_all_ref, hidden_ref, gdown_ref))
+        for half in range(halves)
+    ]
+    streamed = StreamedOuter(jobs, ggate_ref.shape[0], left_slots, right_slots, left_sems, right_sems)
+    sums = []
+    for i, (_, _, half, out) in enumerate(jobs):
+        def store(at, total, half=half, out=out):
+            to = pl.ds(half * wide + at.start, at.size)
+            if out is gdown_ref:
+                out[to] = total.T
+            else:
+                out[:, to] = total
+
+        buf = plane_scratch[i % 2]
+        land, send, recv = plane_scratch[2 + 3 * i:5 + 3 * i]
+        sums.append(PlaneSum(bits, n_uly, None, store, buf, land, send, recv))
+    last = bits - 2
+
+    order = list(range(1, 1 << bits, 2)) + list(range(0, 1 << bits, 2))
+    beside = []
+    for i in range(len(jobs) + last + 1):
+        for level in range(last, -1, -1):
+            j = i - 1 - level
+            if 0 <= j < len(jobs):
+                beside.append(functools.partial(sums[j].pull, level))
+                beside.append(functools.partial(sums[j].push, level + 1) if level < last else sums[j].finish)
+        if i < len(jobs):
+            job = sums[i]
+
+            def product(turn, i=i, job=job):
+                def take(value):
+                    job.buf[order[turn]] = value.astype(bf16)
+                    if order[turn] % 2:
+                        job.first_copy(order[turn]).start()
+
+                streamed.product(i, turn, [job.me ^ e for e in order], take)
+
+            beside += [functools.partial(product, turn) for turn in range(len(order))]
+            beside += [job.pair, functools.partial(job.push, 0)]
+
+    line_and_plane_barrier(n, lax.axis_index("tp"), bits, n_uly)
+    line_all_sum(n, seqs, rows, piece, finish, part_ref, out_ref, land_ref, (rs_send, rs_recv, ag_send, ag_recv),
+                 beside)
+
+
+def norm_back(part, cotangent, middle, gain, a2, cot_all, d_gate, d_up, hidden, n, sizes, collective_id):
+    n_ctx, n_uly = sizes
+    places = n_ctx * n_uly
+    bits = places.bit_length() - 1
+    seqs, rows, width = cotangent.shape
+    tokens, units = d_gate.shape
+    each = width // places
+    if not fits_plane(sizes, width) or units % 512:
+        out, d_mid, dgain = line_call(
+            plain_back_kernel, n, cotangent.shape, part, (cotangent, middle, gain[None]),
+            (jax.ShapeDtypeStruct((1, width), f32),), collective_id, "norm_back")
+        grads = outer_sums((a2, cot_all), (0, 0, 1), (d_gate, d_up, hidden), sizes, 0)
+        return (out, d_mid, dgain, *grads[:2], grads[2].T)
+    piece = min(64, rows)
+    half = units // 2
+    vm, anywhere = pl.BlockSpec(memory_space=pltpu.VMEM), pl.BlockSpec(memory_space=pl.ANY)
+    shapes = [
+        jax.ShapeDtypeStruct(part.shape, bf16), jax.ShapeDtypeStruct(cotangent.shape, f32),
+        jax.ShapeDtypeStruct((1, width), f32), *[jax.ShapeDtypeStruct((each, units), f32)] * 2,
+        jax.ShapeDtypeStruct((units, each), f32),
+    ]
+    plane_scratch = [PlaneSum.scratch(bits, each, half) for _ in range(6)]
+    return pl.pallas_call(
+        functools.partial(norm_back_kernel, n, seqs, rows, piece, bits, n_uly),
+        in_specs=[vm] * 4 + [anywhere] * 5,
+        out_specs=[vm] * len(shapes),
+        out_shape=shapes,
+        scratch_shapes=[
+            *line_scratch(n, seqs, rows, piece, width),
+            pltpu.VMEM((2, tokens, each), bf16), pltpu.VMEM((2, tokens, half), bf16),
+            pltpu.SemaphoreType.DMA((2,)), pltpu.SemaphoreType.DMA((2,)),
+            plane_scratch[0][0], plane_scratch[0][0],
+            *[item for scratch in plane_scratch for item in scratch[1:]],
+        ],
+        compiler_params=pltpu.CompilerParams(
+            collective_id=collective_id, has_side_effects=True, vmem_limit_bytes=vmem_bytes),
+        cost_estimate=cost(6 * tokens * units * width, 250_000_000),
+        name="norm_back",
+    )(part, cotangent, middle, gain[None], a2, cot_all, d_gate, d_up, hidden)
+
+
+class StoredSum(PlaneSum):
+    def __init__(self, bits, n_uly, source, store, buf_ref, land_ref, send, recv, load):
+        super().__init__(bits, n_uly, None, store, buf_ref, land_ref, send, recv)
+        self.source, self.load = source, load
+
+    @staticmethod
+    def scratch(bits, *shape):
+        n = 1 << bits
+        return [
+            pltpu.VMEM((n // 2, *shape), bf16), pltpu.VMEM((n - 1, *shape), bf16),
+            pltpu.SemaphoreType.DMA((3, n)), pltpu.SemaphoreType.DMA((3, n)), pltpu.SemaphoreType.DMA((n // 2,)),
+        ]
+
+    def slot(self, e):
+        return e // 2
+
+    def first_copy(self, e):
+        return pltpu.make_async_remote_copy(
+            src_ref=self.source(self.me ^ e), dst_ref=self.land.at[e - 1], send_sem=self.send.at[2, e],
+            recv_sem=self.recv.at[2, e], device_id=plane_device(self.me ^ 1, self.n_uly), device_id_type=MESH)
+
+    def load_copy(self, e):
+        return pltpu.make_async_copy(self.source(self.me ^ e), self.buf.at[e // 2], self.load.at[e // 2])
+
+    def compute(self):
+        for e in range(1, 1 << self.bits, 2):
+            self.first_copy(e).start()
+            self.load_copy(e - 1).start()
+
+    def pair(self):
+        for e in range(0, 1 << self.bits, 2):
+            self.load_copy(e).wait()
+        super().pair()
+
+
+def all_barrier(n, bits, n_uly):
+    barrier = pltpu.get_barrier_semaphore()
+    me, place = lax.axis_index("tp"), plane_place(n_uly)
+    for d in range(1, n):
+        pl.semaphore_signal(barrier, inc=1, device_id={"tp": lax.rem(me + d, n)}, device_id_type=MESH)
+    for b in range(bits):
+        pl.semaphore_signal(barrier, inc=1, device_id=plane_device(place ^ (1 << b), n_uly), device_id_type=MESH)
+    pl.semaphore_wait(barrier, n - 1 + bits)
+
+
+def layer_back_kernel(
+    n, bits, n_uly, heads, kv_heads, dim, dkv_ref, first_ref, dbranch_ref, dq_ref, dlogit_ref, nk_ref, rk_ref, cos_ref,
+    sin_ref, kgain_ref, wq_ref, wk_ref, wv_ref, wg_ref, gated_ref, x_ref, gain_ref, dmid_ref, dqgain_ref, dmlp_ref, gin_ref, gq_ref, gk_ref,
+    gv_ref, gh_ref, gout_ref, gattn_ref, gmlp_ref, gqn_ref, gkn_ref, all_ref, cut_ref, part_ref, sum_ref, line_land, rs_send, rs_recv, left_slots, left_sems,
+    vec_ref, vec_land, vec_send, vec_recv, *plane_scratch,
+):
+    seqs, _, cut_count, piece, _ = dq_ref.shape
+    rows, width = cut_count * piece, x_ref.shape[-1]
+    group = n * rows
+    cuts = [(q, c) for q in range(seqs) for c in range(cut_count)]
+    q_cols, kv_cols = heads * dim, kv_heads * dim
+    n_main = q_cols + 2 * kv_cols
+    each = gq_ref.shape[0]
+    place, line_me = plane_place(n_uly), lax.axis_index("tp")
+
+    vec_ref[0] = jnp.zeros_like(vec_ref[0])
+    vec_ref[0, :, width:2 * width] = dmlp_ref[...]
+    vec_ref[0, :, 2 * width:2 * width + dim] = dqgain_ref[...]
+
+    def row_at(q, t, c):
+        return q * group + t * rows + c * piece
+
+    def key_values(s):
+        q, c = cuts[s]
+
+        def store(at, total):
+            sum_ref[:, :, at] = total.astype(bf16)
+
+        return StoredSum(
+            bits, n_uly, lambda at: dkv_ref.at[q, pl.ds(pl.multiple_of(at * n, n), n), c], store,
+            *plane_scratch[5 * s:5 * s + 5])
+
+    sums = [key_values(s) for s in range(len(cuts))]
+
+    def turn(s):
+        q, c = cuts[s]
+        for t in range(n):
+            at = slice(t * piece, (t + 1) * piece)
+            cut_ref[at, :q_cols] = dq_ref[q, t, c]
+            for h in range(kv_heads):
+                turned = sum_ref[t, :, h * dim:(h + 1) * dim].astype(f32)
+                back = turned * cos_ref[t, c] - pltpu.roll(turned, dim // 2, 1) * sin_ref[t, c]
+                unit = nk_ref[q, t, c, :, h * dim:(h + 1) * dim].astype(f32)
+                vec_ref[0, :, 2 * width + dim:] += jnp.sum(back * unit, axis=0, keepdims=True)
+                inner = back * kgain_ref[...]
+                mean = jnp.mean(inner * unit, axis=1, keepdims=True)
+                cut_ref[at, q_cols + h * dim:q_cols + (h + 1) * dim] = (
+                    rk_ref[q, t, c, :, h:h + 1] * (inner - unit * mean)).astype(bf16)
+            cut_ref[at, q_cols + kv_cols:n_main] = sum_ref[t, :, kv_cols:]
+            cut_ref[at, n_main:] = dlogit_ref[q, t, c]
+        partial = mm(cut_ref[:, :q_cols], wq_ref[...], NT)
+        partial += mm(cut_ref[:, q_cols:q_cols + kv_cols], wk_ref[...], NT)
+        partial += mm(cut_ref[:, q_cols + kv_cols:n_main], wv_ref[...], NT)
+        partial += mm(cut_ref[:, n_main:n_main + heads], wg_ref[...], NT)
+        partial = partial.astype(bf16)
+        for t in range(n):
+            at = slice(t * piece, (t + 1) * piece)
+            to = slice(row_at(q, t, c), row_at(q, t, c) + piece)
+            part_ref[to] = partial[at]
+            all_ref[to] = cut_ref[at]
+
+    def part_at(owner, s):
+        q, c = cuts[s]
+        return part_ref.at[pl.ds(pl.multiple_of(row_at(q, owner, c), piece), piece)]
+
+    def own(s, total):
+        q, c = cuts[s]
+        at = slice(c * piece, (c + 1) * piece)
+        x = x_ref[q, at].astype(f32)
+        inverse = rms_inverse(x)
+        unit = x * inverse
+        inner = total * gain_ref[...]
+        mean = jnp.mean(inner * unit, axis=-1, keepdims=True)
+        gin_ref[q, at] = dmid_ref[q, at] + inverse * (inner - unit * mean)
+
+    line = LineSum(n, len(cuts), part_at, own, line_land, (rs_send, rs_recv))
+
+    order = list(range(1, 1 << bits, 2)) + list(range(0, 1 << bits, 2))
+    turns = [(dbranch_ref, e) for e in order] + [(first_ref, e) for e in order]
+
+    def left_copy(i):
+        source, e = turns[i]
+        at = pl.ds(pl.multiple_of((place ^ e) * each, each), each)
+        return pltpu.make_async_copy(source.at[:, at], left_slots.at[i % 2], left_sems.at[i % 2])
+
+    def store_out(at, total):
+        gout_ref[at] = total.T
+
+    def store_first(at, total):
+        first = 0
+        for out in (gq_ref, gk_ref, gv_ref, gh_ref):
+            lo, hi = max(first, at.start), min(first + out.shape[1], at.start + at.size)
+            if lo < hi:
+                out[:, lo - first:hi - first] = total[:, lo - at.start:hi - at.start]
+            first += out.shape[1]
+
+    scratch = plane_scratch[5 * len(cuts):]
+    out_sum = PlaneSum(bits, n_uly, None, store_out, *scratch[:4])
+    first_sum = PlaneSum(bits, n_uly, None, store_first, *scratch[4:])
+
+    def product(i):
+        e = turns[i][1]
+        if i + 1 < len(turns):
+            left_copy(i + 1).start()
+        left_copy(i).wait()
+        job = out_sum if i < len(order) else first_sum
+        value = mm(left_slots[i % 2], gated_ref[...] if i < len(order) else all_ref[...], TN)
+        job.buf[e] = value.astype(bf16)
+        if e % 2:
+            job.first_copy(e).start()
+        if job is first_sum:
+            at = pl.ds(pl.multiple_of((place ^ e) * each, each), each)
+            lanes, first = jnp.zeros((each, 128), f32), 0
+            for w_ref in (wq_ref, wk_ref, wv_ref):
+                for k in range(0, w_ref.shape[1], 128):
+                    lanes += value[:, first + k:first + k + 128] * w_ref[at, k:k + 128].astype(f32)
+                first += w_ref.shape[1]
+            total = jnp.sum(lanes.T, axis=0, keepdims=True)
+            last = value[:, n_main:n_main + heads] * wg_ref[at].astype(f32)
+            total += jnp.sum(last.T, axis=0, keepdims=True)
+            vec_ref[0, :, at] = total / gain_ref[:, at]
+
+    line_bits = n.bit_length() - 1
+    steps = bits + line_bits
+
+    def vec_copy(k):
+        partner = plane_device(place ^ (1 << k), n_uly) if k < bits else {"tp": line_me ^ (1 << (k - bits))}
+        return pltpu.make_async_remote_copy(
+            src_ref=vec_ref.at[k], dst_ref=vec_land.at[k], send_sem=vec_send.at[k], recv_sem=vec_recv.at[k],
+            device_id=partner, device_id_type=MESH)
+
+    def vec_step(k):
+        if k > 0:
+            vec_copy(k - 1).wait_recv()
+            vec_ref[k] = vec_ref[k - 1] + vec_land[k - 1]
+        if k < steps:
+            vec_copy(k).start()
+
+    def levels(job):
+        items = [job.pair, functools.partial(job.push, 0)]
+        for level in range(bits - 1):
+            items.append(functools.partial(job.pull, level))
+            if level + 1 < bits - 1:
+                items.append(functools.partial(job.push, level + 1))
+        return items
+
+    early = [functools.partial(product, i) for i in range(len(order))] + levels(out_sum)
+    late = [functools.partial(product, i) for i in range(len(order), len(turns))]
+    late += [first_sum.pair, functools.partial(first_sum.push, 0)]
+    rest = levels(first_sum)[2:]
+    for k in range(steps + 1):
+        late.append(functools.partial(vec_step, k))
+        if rest and k % 2:
+            late.append(rest.pop(0))
+    late += rest
+
+    all_barrier(n, bits, n_uly)
+    for job in sums:
+        job.compute()
+    left_copy(0).start()
+    ready = 0
+    for step in range(len(cuts) + bits - 1 + n - 1):
+        if step < len(cuts):
+            sums[step].pair()
+            sums[step].push(0)
+        for level in range(bits - 1):
+            j = step - 1 - level
+            if 0 <= j < len(cuts):
+                sums[j].pull(level)
+                if level + 1 < bits - 1:
+                    sums[j].push(level + 1)
+                else:
+                    turn(j)
+                    ready += 1
+        for s in range(len(cuts)):
+            stage = step - s - (bits - 1)
+            if 0 <= stage < n:
+                line.stages[stage](s)
+                queue = early or (late if ready == len(cuts) else [])
+                for item in queue[:3]:
+                    item()
+                del queue[:3]
+    for item in early + late:
+        item()
+    line.drain_reduce()
+    first = 0
+    for out in (gattn_ref, gmlp_ref, gqn_ref, gkn_ref):
+        out[...] = vec_ref[steps, :, first:first + out.shape[1]]
+        first += out.shape[1]
+    for k in range(steps):
+        vec_copy(k).wait_send()
+    for job in (*sums, out_sum, first_sum):
+        job.finish()
+
+
+def layer_back(d_kv, first, d_branch, d_q, d_logit, nk, rk, tables, key_norm, weights, gated, x, attn_norm, d_mid, d_qgain,
+               d_mlp, n, sizes, heads, kv_heads, collective_id):
+    n_ctx, n_uly = sizes
+    places = n_ctx * n_uly
+    bits = places.bit_length() - 1
+    seqs, rows, width = x.shape
+    group, dim = n * rows, key_norm.shape[0]
+    piece = min(64, rows)
+    cut_count = rows // piece
+    each = width // places
+    tokens = seqs * group
+    wide = (heads + 2 * kv_heads) * dim + d_logit.shape[-1]
+    small = 2 * width + 2 * dim
+    kv_wide = d_kv.shape[-1]
+    pieces = seqs * cut_count
+    steps = bits + n.bit_length() - 1
+
+    def tiles(values):
+        return values.reshape(seqs, n, cut_count, piece, values.shape[-1])
+
+    vm, anywhere = pl.BlockSpec(memory_space=pltpu.VMEM), pl.BlockSpec(memory_space=pl.ANY)
+    plane_scratch = []
+    for _ in range(pieces):
+        plane_scratch += StoredSum.scratch(bits, n, piece, kv_wide)
+    plane_scratch += PlaneSum.scratch(bits, each, heads * dim) + PlaneSum.scratch(bits, each, wide)
+    shapes = [
+        jax.ShapeDtypeStruct(shape, f32) for shape in (
+            x.shape, (each, heads * dim), (each, kv_heads * dim), (each, kv_heads * dim), (each, heads),
+            (heads * dim, each), (1, width), (1, width), (1, dim), (1, dim))
+    ]
+    line = line_scratch(n, seqs, rows, piece, width)
+    return pl.pallas_call(
+        functools.partial(layer_back_kernel, n, bits, n_uly, heads, kv_heads, dim),
+        in_specs=[anywhere] * 3 + [vm] * 17,
+        out_specs=[vm] * len(shapes),
+        out_shape=shapes,
+        scratch_shapes=[
+            pltpu.VMEM((tokens, wide), bf16), pltpu.VMEM((n * piece, wide), bf16), pltpu.VMEM((tokens, width), bf16),
+            pltpu.VMEM((n, piece, kv_wide), bf16), *line[:3],
+            pltpu.VMEM((2, tokens, each), bf16), pltpu.SemaphoreType.DMA((2,)),
+            pltpu.VMEM((steps + 1, 1, small), f32), pltpu.VMEM((steps, 1, small), f32),
+            pltpu.SemaphoreType.DMA((steps,)), pltpu.SemaphoreType.DMA((steps,)),
+            *plane_scratch,
+        ],
+        compiler_params=pltpu.CompilerParams(
+            collective_id=collective_id, has_side_effects=True, vmem_limit_bytes=vmem_bytes),
+        cost_estimate=cost(4 * tokens * width * wide, 250_000_000),
+        name="layer_back",
+    )(d_kv.reshape(seqs, places * n, cut_count, piece, kv_wide), first, d_branch, tiles(d_q), tiles(d_logit), tiles(nk),
+      tiles(rk), *[t.reshape(n, cut_count, piece, dim) for t in tables], key_norm[None], *weights, gated, x,
+      attn_norm[None], d_mid, d_qgain, d_mlp)
+
+
+class LineSpread(LineSum):
+    def __init__(self, n, pieces, own, out_at, sems):
+        super().__init__(n, pieces, None, own, None, (None, None, *sems), out_at)
+        self.stages = [self.own_step] + [functools.partial(self.spread_step, k) for k in range(2, n + 1)]
+
+    def own_step(self, s):
+        self.out_at(self.me, s)[...] = self.own(s)
+        self.spread_step(1, s)
+
+
+class PlaneSpread:
+    def __init__(self, bits, n_uly, block, send, recv):
+        self.bits, self.n_uly, self.block, self.send, self.recv = bits, n_uly, block, send, recv
+        self.me = plane_place(n_uly)
+        self.orders = [w + [0] for w in ways(bits)]
+
+    def copy(self, d, level, e):
+        bit = 1 << self.orders[d][level]
+        block = self.block(self.me ^ e, d)
+        return pltpu.make_async_remote_copy(
+            src_ref=block, dst_ref=block, send_sem=self.send.at[d, e | bit], recv_sem=self.recv.at[d, e | bit],
+            device_id=plane_device(self.me ^ bit, self.n_uly), device_id_type=MESH)
+
+    def pass_on(self, d, first, e):
+        for level in range(first, self.bits):
+            self.copy(d, level, e).start()
+
+    def begin(self):
+        for d in range(2):
+            self.pass_on(d, 0, 0)
+
+    def take(self, level):
+        for d in range(2):
+            for e in span(self.orders[d][:level]):
+                self.copy(d, level, e).wait_recv()
+                self.pass_on(d, level + 1, e | (1 << self.orders[d][level]))
+
+    def finish(self):
+        for d in range(2):
+            for level in range(self.bits):
+                for e in span(self.orders[d][:level]):
+                    self.copy(d, level, e).wait_send()
+
+
+def layer_front_kernel(
+    n, bits, n_uly, heads, kv_heads, dim, scale, x_ref, gain_ref, wq_ref, wk_ref, wv_ref, wg_ref, cos_ref, sin_ref,
+    qg_ref, kg_ref, a1_ref, q_ref, kv_ref, nq_ref, nk_ref, rq_ref, rk_ref, logit_ref, ag_send, ag_recv, kv_send,
+    kv_recv,
+):
+    seqs, _, cut_count, piece, width = a1_ref.shape
+    cuts = [(q, c) for q in range(seqs) for c in range(cut_count)]
+    place = plane_place(n_uly)
+    tokens = n * piece
+    half = kv_heads * dim
+
+    def own(s):
+        q, c = cuts[s]
+        x = x_ref[q, c * piece:(c + 1) * piece].astype(f32)
+        return (x * rms_inverse(x) * gain_ref[...]).astype(bf16)
+
+    line = LineSpread(
+        n, len(cuts), own, lambda owner, s: a1_ref.at[cuts[s][0], owner, cuts[s][1]], (ag_send, ag_recv))
+
+    def keys(s):
+        q, c = cuts[s]
+        return PlaneSpread(
+            bits, n_uly,
+            lambda at, d: kv_ref.at[q, pl.ds(pl.multiple_of(at * n, n), n), c, :, pl.ds(d * half, half)],
+            kv_send.at[s], kv_recv.at[s])
+
+    spreads = [keys(s) for s in range(len(cuts))]
+
+    def turn(s):
+        q, c = cuts[s]
+        a1 = a1_ref[q, :, c].reshape(tokens, width)
+        cosine, sine = cos_ref[:, c].reshape(tokens, dim), sin_ref[:, c].reshape(tokens, dim)
+
+        def tiles(values):
+            return values.reshape(n, piece, values.shape[-1])
+
+        def rope(unit, gain):
+            scaled = unit * gain
+            return scaled * cosine + pltpu.roll(scaled, dim // 2, 1) * sine
+
+        mine = pl.ds(pl.multiple_of(place * n, n), n)
+        raw = mm(a1, wk_ref[...])
+        for h in range(kv_heads):
+            at = slice(h * dim, (h + 1) * dim)
+            values = raw[:, at]
+            inverse = rms_inverse(values)
+            unit = values * inverse
+            kv_ref[q, mine, c, :, at] = tiles(rope(unit, kg_ref[...]).astype(bf16))
+            nk_ref[q, :, c, :, at] = tiles(unit.astype(bf16))
+            rk_ref[q, :, c, :, h:h + 1] = tiles(inverse)
+        kv_ref[q, mine, c, :, half:] = tiles(mm(a1, wv_ref[...]).astype(bf16))
+        spreads[s].begin()
+        raw = mm(a1, wq_ref[...])
+        for h in range(heads):
+            at = slice(h * dim, (h + 1) * dim)
+            values = raw[:, at]
+            inverse = rms_inverse(values)
+            unit = values * inverse
+            q_ref[q, :, c, :, at] = tiles((rope(unit, qg_ref[...]) * (scale * log2e)).astype(bf16))
+            nq_ref[q, :, c, :, at] = tiles(unit.astype(bf16))
+            rq_ref[q, :, c, :, h:h + 1] = tiles(inverse)
+        logit_ref[q, :, c] = tiles(mm(a1, wg_ref[...]).astype(bf16).astype(f32))
+
+    line_and_plane_barrier(n, lax.axis_index("tp"), bits, n_uly)
+    for step in range(len(cuts) + n - 1 + bits):
+        for s in range(len(cuts)):
+            stage = step - s
+            if 0 <= stage < n:
+                line.stages[stage](s)
+                if stage == n - 1:
+                    turn(s)
+        for s in range(len(cuts)):
+            level = step - s - n
+            if 0 <= level < bits:
+                spreads[s].take(level)
+    line.drain_spread()
+    for spread in spreads:
+        spread.finish()
+
+
+def layer_front(x, attn_norm, w_query, w_key, w_value, w_headgate, tables, query_norm, key_norm, n, sizes, scale,
+                collective_id):
+    n_ctx, n_uly = sizes
+    places = n_ctx * n_uly
+    bits = places.bit_length() - 1
+    seqs, rows, width = x.shape
+    dim = query_norm.shape[0]
+    heads, kv_heads = w_query.shape[1] // dim, w_key.shape[1] // dim
+    piece = min(64, rows)
+    cut_count = rows // piece
+    pieces = seqs * cut_count
+    vm = pl.BlockSpec(memory_space=pltpu.VMEM)
+
+    def tiled(devices, cols, kind):
+        return jax.ShapeDtypeStruct((seqs, devices * n, cut_count, piece, cols), kind)
+
+    shapes = [
+        tiled(1, width, bf16), tiled(1, heads * dim, bf16), tiled(places, 2 * kv_heads * dim, bf16),
+        tiled(1, heads * dim, bf16), tiled(1, kv_heads * dim, bf16), tiled(1, heads, f32), tiled(1, kv_heads, f32),
+        tiled(1, heads, f32),
+    ]
+    line_sems = [pltpu.SemaphoreType.DMA((2, n - 1, pieces))] * 2
+    plane_sems = [pltpu.SemaphoreType.DMA((pieces, 2, places))] * 2
+    made = pl.pallas_call(
+        functools.partial(layer_front_kernel, n, bits, n_uly, heads, kv_heads, dim, scale),
+        in_specs=[vm] * 10,
+        out_specs=[vm] * len(shapes),
+        out_shape=shapes,
+        scratch_shapes=[*line_sems, *plane_sems],
+        compiler_params=params(collective_id=collective_id, has_side_effects=True),
+        cost_estimate=cost(2 * seqs * n * rows * width * 1024, 200_000_000),
+        name="layer_front",
+    )(x, attn_norm[None], w_query, w_key, w_value, w_headgate,
+      *[t.reshape(n, cut_count, piece, dim) for t in tables], query_norm[None], key_norm[None])
+    return [m.reshape(seqs, -1, m.shape[-1]) for m in made]
 
 
 def flatten(values):
@@ -809,15 +1447,17 @@
     place = lax.axis_index("ctx") * n_uly + lax.axis_index("uly")
     block_start = place * group
     positions = block_start + jnp.arange(group, dtype=jnp.int32)
-    tables = rope_tables(positions, dim)
+    tables = lax.optimization_barrier(rope_tables(positions, dim))
     block = min(512, group)
 
     def wide(values):
         return values.reshape(seqs, group, -1)
 
     query_doc = lax.dynamic_slice_in_dim(doc_ids, block_start, group, 1)
-    before = (doc_ids[:, None, :] >= 0) & (doc_ids[:, None, :] < query_doc[:, :, None])
-    start = jnp.where(query_doc >= 0, jnp.sum(before.astype(jnp.int32), axis=-1), positions[None, :])
+    start = positions[None, :]
+    for d in range(4):
+        first_of = jnp.sum(((doc_ids >= 0) & (doc_ids < d)).astype(jnp.int32), axis=1)
+        start = jnp.where(query_doc == d, first_of[:, None], start)
     lowest, highest = jnp.min(start, axis=1), jnp.max(start, axis=1)
     hi = jnp.full_like(lowest, (block_start + group + block - 1) // block)
     lo = lowest // block
@@ -830,76 +1470,98 @@
     q_cols, kv_cols = heads * dim, kv_heads * dim
     n_main = q_cols + 2 * kv_cols
 
-    xs = inputs.astype(f32)
-    inv_one = rms_inverse(xs)
-    first = spread(xs * inv_one * attn_norm)
-    q, kv, nq, nk, rq, rk, logits = (
-        wide(m) for m in project(flatten(first), w_first, tables, query_norm, key_norm, heads, kv_heads, scale))
-    cot_in, _ = lax.optimization_barrier((cotangent, first))
-    cot_all = spread(cot_in)
-    kv = plane_gather(kv, sizes, 0)
+    if fits_plane(sizes, width):
+        first, q, kv, nq, nk, rq, rk, logits = layer_front(
+            inputs, attn_norm, w_query, w_key, w_value, w_headgate, tables, query_norm, key_norm, n_tensor, sizes, scale,
+            0)
+    else:
+        xs = inputs.astype(f32)
+        inv_one = rms_inverse(xs)
+        first = spread(xs * inv_one * attn_norm)
+        q, kv, nq, nk, rq, rk, logits = (
+            wide(m) for m in project(flatten(first), w_first, tables, query_norm, key_norm, heads, kv_heads, scale))
+        kv = plane_gather(kv, sizes, 0)
+    near = (seqs + 1) // 2
+    early_cot, kv = lax.optimization_barrier((cotangent[:near], kv))
+    cots = [spread(early_cot)]
     att, gated, lse = attend(q, kv, bounds, start[:, :, None], positions[:, None], logits, heads, kv_heads, dim, block)
 
     local = inputs.shape
+    part, cots = lax.optimization_barrier((wide(mm(flatten(gated), w_output).astype(bf16)), cots))
     second, middle = line_call(
-        norm_forward_kernel, n_tensor, local, wide(mm(flatten(gated), w_output).astype(bf16)),
+        norm_forward_kernel, n_tensor, local, part,
         (inputs, mlp_norm[None]), (), 1, "norm_forward")
 
-    a2, cot = flatten(second), flatten(cot_all)
+    if near < seqs:
+        late_cot, second = lax.optimization_barrier((cotangent[near:], second))
+        cots.append(spread(late_cot))
+    a2 = flatten(second)
     gate, up = mm(a2, w_gate), mm(a2, w_up)
-    d_hidden = mm(cot, w_down, NT)
     sig = jax.nn.sigmoid(gate)
     silu = gate * sig
     hidden = (silu * up).astype(bf16)
+    made, cots = lax.optimization_barrier((wide(mm(hidden, w_down).astype(bf16)), cots))
+    outs = [collect(made[:near])]
+    cot = flatten(jnp.concatenate(cots, axis=0))
+    d_hidden = mm(cot, w_down, NT)
     d_gate = (d_hidden * up * sig * (1.0 + gate * (1.0 - sig))).astype(bf16)
     d_up = (d_hidden * silu).astype(bf16)
     d_second = (mm(d_gate, w_gate, NT) + mm(d_up, w_up, NT)).astype(bf16)
-    d_branch, d_mid, grad_mlp_norm = line_call(
-        norm_back_kernel, n_tensor, local, wide(d_second), (cotangent, middle, mlp_norm[None]),
-        (jax.ShapeDtypeStruct((1, width), f32),), 2, "norm_back")
-
-    late_hidden, d_branch = lax.optimization_barrier((hidden, d_branch))
-    outputs = (middle + collect(wide(mm(late_hidden, w_down)))).astype(bf16)
-
+    d_branch, d_mid, grad_mlp_norm, grad_gate, grad_up, grad_down = norm_back(
+        wide(d_second), cotangent, middle, mlp_norm, a2, cot, d_gate, d_up, hidden, n_tensor, sizes, 2)
+
+    if near < seqs:
+        late_made, d_branch = lax.optimization_barrier((made[near:], d_branch))
+        outs.append(collect(late_made))
+    outputs = (middle + jnp.concatenate(outs, axis=0)).astype(bf16)
     d_gated = wide(mm(flatten(d_branch), w_output, NT).astype(bf16))
     d_q, d_logit, d_kv, d_qgain = attend_back(
         q, kv, d_gated, att, logits, logits.transpose(0, 2, 1), lse, bounds, start[:, None, :], positions[None, :], nq,
         rq, tables, query_norm, heads, kv_heads, dim, block, scale)
-    d_kv = blocks_sum(d_kv, sizes, 3)
-    d_kv, d_kgain = key_back(d_kv, nk, rk, tables, key_norm, kv_heads, dim)
     d_logit = jnp.pad(d_logit.astype(bf16).transpose(0, 2, 1), ((0, 0), (0, 0), (0, pad)))
-    d_all = flatten(jnp.concatenate([d_q, d_kv, d_logit], axis=-1))
-    d_first = collect(wide(mm(d_all, w_first, NT)))
-
-    grad_first, grad_output = outer_sums(
-        (flatten(first), flatten(d_branch)), (0, 1), (d_all, flatten(gated)), sizes, 4)
-    grad_gate, grad_up, grad_down = outer_sums((a2, cot), (0, 0, 1), (d_gate, d_up, hidden), sizes, 5)
-
-    share = grad_first.shape[0]
-    own_rows = lax.dynamic_slice_in_dim(w_first, place * share, share, 0).astype(f32)
-    own_norm = jnp.sum(grad_first * own_rows, axis=1) / lax.dynamic_slice_in_dim(attn_norm, place * share, share, 0)
-    grad_attn_norm = lax.dynamic_update_slice_in_dim(jnp.zeros((width,), f32), own_norm, place * share, 0)
-    grad_attn_norm, grad_query_norm, grad_key_norm, grad_mlp_norm = lax.psum(
-        (grad_attn_norm, d_qgain[0], d_kgain[0], grad_mlp_norm[0]), ("ctx", "uly", "tp"))
-
-    unit = xs * inv_one
-    inner = d_first * attn_norm
-    grad_inputs = d_mid + inv_one * (inner - unit * jnp.mean(inner * unit, axis=-1, keepdims=True))
+    if fits_plane(sizes, width):
+        grad_inputs, *grads = layer_back(
+            d_kv, flatten(first), flatten(d_branch), d_q, d_logit, nk, rk, tables, key_norm,
+            (w_query, w_key, w_value, w_headgate), flatten(gated), inputs, attn_norm, d_mid, d_qgain, grad_mlp_norm, n_tensor, sizes, heads, kv_heads, 3)
+        grad_query, grad_key, grad_value, grad_headgate, grad_output = grads[:5]
+        grad_attn_norm, grad_mlp_norm, grad_query_norm, grad_key_norm = (g[0] for g in grads[5:])
+    else:
+        d_kv = blocks_sum(d_kv, sizes, 3)
+        d_kv, d_kgain = key_back(d_kv, nk, rk, tables, key_norm, kv_heads, dim)
+        d_all = flatten(jnp.concatenate([d_q, d_kv, d_logit], axis=-1))
+        d_first = collect(wide(mm(d_all, w_first, NT)))
+
+        grad_first, grad_output = outer_sums(
+            (flatten(first), flatten(d_branch)), (0, 1), (d_all, flatten(gated)), sizes, 4)
+
+        share = grad_first.shape[0]
+        own_rows = lax.dynamic_slice_in_dim(w_first, place * share, share, 0).astype(f32)
+        own_norm = jnp.sum(grad_first * own_rows, axis=1) / lax.dynamic_slice_in_dim(attn_norm, place * share, share, 0)
+        grad_attn_norm = lax.dynamic_update_slice_in_dim(jnp.zeros((width,), f32), own_norm, place * share, 0)
+        grad_attn_norm, grad_query_norm, grad_key_norm, grad_mlp_norm = lax.psum(
+            (grad_attn_norm, d_qgain[0], d_kgain[0], grad_mlp_norm[0]), ("ctx", "uly", "tp"))
+
+        unit = xs * inv_one
+        inner = d_first * attn_norm
+        grad_inputs = d_mid + inv_one * (inner - unit * jnp.mean(inner * unit, axis=-1, keepdims=True))
+        grad_query, grad_key = grad_first[:, :q_cols], grad_first[:, q_cols:q_cols + kv_cols]
+        grad_value, grad_headgate = grad_first[:, q_cols + kv_cols:n_main], grad_first[:, n_main:n_main + heads]
+        grad_output = grad_output.T
     return (
         outputs,
         grad_inputs,
         grad_attn_norm,
-        grad_first[:, :q_cols],
-        grad_first[:, q_cols:q_cols + kv_cols],
-        grad_first[:, q_cols + kv_cols:n_main],
-        grad_first[:, n_main:n_main + heads],
+        grad_query,
+        grad_key,
+        grad_value,
+        grad_headgate,
         grad_query_norm,
         grad_key_norm,
-        grad_output.T,
+        grad_output,
         grad_mlp_norm,
         grad_gate,
         grad_up,
-        grad_down.T,
+        grad_down,
     )
 
 

time: 841 us -> 697 us (0.83)
  waiting for transfers between devices: 76.4 us -> 34 us
  blocking collectives: 38.7 us -> 0 us
  Pallas kernels: 562 us -> 525 us
  other arithmetic: 24.8 us -> 11.8 us
  matrix products: 89.9 us -> 77.3 us
    pallas_call x2 -> x1, Pallas kernels: 239 us -> 112 us  [line_call(): pl.pallas_call(functools.partial(kernel, n, seqs, rows, piece), in_specs=...]
    pallas_call x6 -> x3, Pallas kernels: 297 us -> 382 us  [the longest x1 146 us: layer_back(): pl.pallas_call(functools.partial(layer_back_kernel, n, bits, n_uly, heads...]
    all_gather x2, waiting for transfers between devices: 76.3 us -> 33.9 us  [spread(): return lax.all_gather(values.astype(bf16), 'tp', axis=1, tiled=True)]
    psum x1 -> x0, blocking collectives: 38.7 us -> none  [per_device(): lax.psum((grad_attn_norm, d_qgain[0], d_kgain[0], grad_mlp_norm[0]), ('ct...]
    dot_general x9 -> x8, matrix products: 89.9 us -> 77.3 us  [mm(): return lax.dot_general(left, right, dims, preferred_element_type=f32)]
    unnamed x106 -> x65, local copies, waits for them, and re-layouts: 19.6 us -> 15.4 us
  transfers between devices with their start and end apart: 4 -> 4, of which waited for: 1 -> 2; matrix products, arithmetic and copies ran while one was open for 8% -> 13% of each run, Pallas kernels for 40% -> 45%
where the time goes in v2:
time: 697 us; the launch traced here: 690 us
  Pallas kernels  525 us (75%)
  matrix products  77.3 us (11%)
  waiting for transfers between devices  34 us (5%)
  local copies, waits for them, and re-layouts  25.9 us (4%)
  between operations  14.5 us (2%)
  other arithmetic  11.8 us (2%)
    pallas_call x1, Pallas kernels, layer_back(): pl.pallas_call(functools.partial(layer_back_kernel, n, bits, n_uly, heads...  146 us
    pallas_call x1, Pallas kernels, norm_back(): pl.pallas_call(functools.partial(norm_back_kernel, n, seqs, rows, piece,...  135 us
    pallas_call x1, Pallas kernels, line_call(): pl.pallas_call(functools.partial(kernel, n, seqs, rows, piece), in_specs=...  112 us
    pallas_call x1, Pallas kernels, layer_front(): pl.pallas_call(functools.partial(layer_front_kernel, n, bits, n_uly, head...  101 us
    dot_general x8, matrix products, mm(): return lax.dot_general(left, right, dims, preferred_element_type=f32)  77.3 us
    all_gather x2, waiting for transfers between devices, spread(): return lax.all_gather(values.astype(bf16), 'tp', axis=1, tiled=True)  33.9 us
    pallas_call x1, Pallas kernels, attend_back(): pl.pallas_call(functools.partial(attend_back_kernel, heads, kv_heads, dim...  19.4 us
    unnamed x65, local copies, waits for them, and re-layouts  15.4 us
  transfers between devices with their start and end apart: 4, of which 2 were waited for; matrix products, arithmetic and copies ran while one was open for 13% of the time, Pallas kernels for 45%

profile of v2, /device:TPU:0, one launch (start us, length us, event | category | flops | bytes accessed | tf_op | source)
XLA Modules:
  0.0 689.9 jit_solution(12612226068893027677)
XLA Ops:
  7.3 1.9 copy.37.wg_ref
  11.9 2.3 fusion.9
  14.1 100.8 %layer_front.1 = (bf16[2,4,2,64,2048]{4,3,2,1,0:T(8,128)(2,1)}, bf16[2,4,2,64,512]{4,3,2,1,0:T(8,128)(2,1)}, bf16[2,32,2,64,512]{4,3,2,1,0:T(8,128)(2,1)}, bf16[...) custom-call(bf16[2,128,2048]{2,1,0:T(8,128)(2,1)} %x_ref.5, ...), custom_call_target="tpu_custom_call" | custom-call | flops 4294967296 | bytes 200000000 | tf_op jit(solution)/shard_map/layer_front/pallas_call | solution.py:1410
  118.3 12.1 %attend.1 = (bf16[2,512,512]{2,1,0:T(8,128)(2,1)}, bf16[2,512,512]{2,1,0:T(8,128)(2,1)}, f32[2,4,512]{2,1,0:T(4,128)}) custom-call(s32[2,4]{1,0:T(2,128)} %pad_add_fusion.bounds_ref, bf16[2,512,512]{2,1,0:T(8,128)(2,1)} %bitcast.89, bf16[2,4096,512]{2,1,0:T(8,128)(2,1)} %bitcast.82, s32[2,512,1]{2,1,0:T(8,128)} %copy.39.start_ref, ...), custom_call_target="tpu_custom_call" | custom-call | flops 4294967296 | bytes 11534336 | tf_op jit(solution)/shard_map/attend/pallas_call | solution.py:167
  130.4 5.7 convolution_convert_fusion.1
  136.0 23.2 %all-gather.3.cloned.1.call-done = bf16[1,512,2048]{2,1,0:T(8,128)(2,1)} async-done(((bf16[1,128,2048]{2,1,0:T(8,128)(2,1)}), bf16[1,512,2048]{2,1,0:T(8,128)(2,1)}) %all-gather.3.cloned.1.call-update) | async-done | bytes 2097168 | tf_op jit(solution)/shard_map/all_gather | solution.py:1429
  159.2 111.9 %norm_forward.1 = (bf16[2,512,2048]{2,1,0:T(8,128)(2,1)}, f32[2,128,2048]{2,1,0:T(8,128)}) custom-call(bf16[2,512,2048]{2,1,0:T(8,128)(2,1)} %bitcast.50, bf16[2,128,2048]{2,1,0:T(8,128)(2,1)} %x_ref.5, f32[1,2048]{1,0:T(1,128)} %bitcast.64), custom_call_target="tpu_custom_call" | custom-call | flops 41943040 | bytes 100000000 | tf_op jit(solution)/shard_map/norm_forward/pallas_call | solution.py:533
  271.4 10.7 %fusion.10 = f32[1024,1536]{1,0:T(8,128)S(1)} fusion(bf16[1024,2048]{1,0:T(8,128)(2,1)} %bitcast.73, bf16[2048,1536]{1,0:T(8,128)(2,1)} %param.26), kind=kOutput, calls=%fused_computation.50 | convolution fusion | flops 6442450944 | bytes 16777216 | tf_op jit(solution)/shard_map/dot_general | solution.py:25
  282.2 13.3 %multiply_convert_fusion.2 = (bf16[1024,1536]{1,0:T(8,128)(2,1)S(1)}, f32[1024,1536]{1,0:T(8,128)}) fusion(f32[1024,1536]{1,0:T(8,128)S(1)} %fusion.10, bf16[1024,2048]{1,0:T(8,128)(2,1)S(1)} %bitcast.75, bf16[2048,1536]{1,0:T(8,128)(2,1)} %param.27), kind=kOutput, calls=%fused_computation.3 | convolution fusion | flops 6451888128 | bytes 26214400 | tf_op jit(solution)/shard_map/dot_general | solution.py:25
  295.4 1.6 copy-done.18
  297.1 8.2 %convolution_convert_fusion = bf16[1024,2048]{1,0:T(8,128)(2,1)} fusion(bf16[1024,1536]{1,0:T(8,128)(2,1)S(1)} %get-tuple-element.139.hidden_ref, bf16[1536,2048]{1,0:T(8,128)(2,1)S(1)} %bitcast.70), kind=kOutput, calls=%fused_computation.7 | convolution fusion | flops 6444548096 | bytes 13631488 | tf_op jit(solution)/shard_map/dot_general | solution.py:25
  305.3 10.7 %all-gather.5.cloned.1.call-done = bf16[1,512,2048]{2,1,0:T(8,128)(2,1)} async-done(((bf16[1,128,2048]{2,1,0:T(8,128)(2,1)}), bf16[1,512,2048]{2,1,0:T(8,128)(2,1)}) %all-gather.5.cloned.1.call-update) | async-done | bytes 2097168 | tf_op jit(solution)/shard_map/all_gather | solution.py:1429
  315.9 4.9 fusion.8
  321.3 2.8 pad_maximum_fusion
  324.1 16.1 %multiply_convert_fusion = (bf16[1024,1536]{1,0:T(8,128)(2,1)}, bf16[1024,1536]{1,0:T(8,128)(2,1)S(1)}) fusion(f32[1024,1536]{1,0:T(8,128)} %copy-done.19, f32[1024,1536]{1,0:T(8,128)} %get-tuple-element.140, bf16[1024,2048]{1,0:T(8,128)(2,1)S(1)} %bitcast.51, bf16[1536,2048]{1,0:T(8,128)(2,1)} %param.28), kind=kOutput, calls=%fused_computation.1 | convolution fusion | flops 6462898176 | bytes 29360128 | tf_op jit(solution)/shard_map/dot_general | solution.py:25
  340.3 6.7 fusion.11
  347.0 11.1 %add_convert_fusion = bf16[1024,2048]{1,0:T(8,128)(2,1)} fusion(f32[1024,2048]{1,0:T(8,128)S(1)} %fusion.11, bf16[1024,1536]{1,0:T(8,128)(2,1)S(1)} %copy-done.20, bf16[2048,1536]{1,0:T(8,128)(2,1)} %param.27), kind=kOutput, calls=%fused_computation | convolution fusion | flops 6446645248 | bytes 22020096 | tf_op jit(solution)/shard_map/dot_general | solution.py:25
  358.1 135.1 %norm_back.1 = (bf16[2,512,2048]{2,1,0:T(8,128)(2,1)}, f32[2,128,2048]{2,1,0:T(8,128)}, f32[1,2048]{1,0:T(1,128)}, f32[256,1536]{1,0:T(8,128)}, f32[256,1536]{1,0:T(8,128)}, /*index=5*/f32[1536,256]{1,0:T(8,128)}) custom-call(bf16[2,512,2048]{2,1,0:T(8,128)(2,1)} %bitcast.88, bf16[2,128,2048]{2,1,0:T(8,128)(2,1)} %cot_ref.1, ...), custom_call_target="tpu_custom_call" | custom-call | flops 19327352832 | bytes 250000000 | tf_op jit(solution)/shard_map/norm_back/pallas_call | solution.py:951
  495.3 5.5 convolution_convert_fusion.2
  500.8 19.4 %attend_back.1 = (bf16[2,512,512]{2,1,0:T(8,128)(2,1)}, f32[2,4,512]{2,1,0:T(4,128)}, bf16[2,4096,512]{2,1,0:T(8,128)(2,1)}, f32[1,128]{1,0:T(1,128)}) custom-call(s32[2,4]{1,0:T(2,128)} %pad_add_fusion.bounds_ref, bf16[2,512,512]{2,1,0:T(8,128)(2,1)} %bitcast.90, bf16[2,4096,512]{2,1,0:T(8,128)(2,1)} %bitcast.83, bf16[2,512,512]{2,1,0:T(8,128)(2,1)} %bitcast.95, ...), custom_call_target="tpu_custom_call" | custom-call | flops 10737418240 | bytes 22020096 | tf_op jit(solution)/shard_map/attend_back/pallas_call | solution.py:273
  521.9 146.1 %layer_back.1 = (f32[2,128,2048]{2,1,0:T(8,128)}, f32[256,512]{1,0:T(8,128)}, f32[256,256]{1,0:T(8,128)}, f32[256,256]{1,0:T(8,128)}, f32[256,4]{1,0:T(8,128)}, ...) custom-call(bf16[2,32,2,64,512]{4,3,2,1,0:T(8,128)(2,1)} %bitcast.84, ...), custom_call_target="tpu_custom_call" | custom-call | flops 9663676416 | bytes 250000000 | tf_op jit(solution)/shard_map/layer_back/pallas_call | solution.py:1241
  668.0 1.6 copy.44
  669.6 3.2 add_convert_fusion.1
  672.9 1.3 copy.59
  (93 shorter events, 19.2 us)
Async XLA Ops:
  7.2 123.2 %copy-start = (bf16[512,2048]{1,0:T(8,128)(2,1)S(1)}, bf16[512,2048]{1,0:T(8,128)(2,1)}, u32[]{:S(2)}) copy-start(bf16[512,2048]{1,0:T(8,128)(2,1)} %param.24) | copy-start | bytes 6291460
  7.2 152.0 %all-gather.3.cloned.1.call-start = ((), (), s32[]{:S(2)}) async-start(), calls=%async_computation.2 | async-start | bytes 2621440 | tf_op jit(solution)/shard_map/all_gather | solution.py:1429
  14.1 101.1 %copy-start.11 = (s32[2,4096]{1,0:T(2,128)S(1)}, s32[2,4096]{1,0:T(2,128)}, u32[]{:S(2)}) copy-start(s32[2,4096]{1,0:T(2,128)} %param.16) | copy-start | bytes 98308
  115.0 201.0 %all-gather.5.cloned.1.call-start = ((), (), s32[]{:S(2)}) async-start(), calls=%async_computation.3 | async-start | bytes 2621440 | tf_op jit(solution)/shard_map/all_gather | solution.py:1429
  271.2 398.4 %reduce-scatter.3.cloned.1.call-start = ((), (), s32[]{:S(2)}) async-start(), calls=%async_computation.4 | async-start | bytes 2621440 | tf_op jit(solution)/shard_map/reduce_scatter | solution.py:1433
  271.4 10.7 %copy-start.14 = (bf16[2,512,2048]{2,1,0:T(8,128)(2,1)S(1)}, bf16[2,512,2048]{2,1,0:T(8,128)(2,1)}, u32[]{:S(2)}) copy-start(bf16[2,512,2048]{2,1,0:T(8,128)(2,1)} %get-tuple-element.71) | copy-start | bytes 12582916
  271.4 25.7 %slice-start = ((s8[6291456]{0:T(1024)(128)(4,1)}), s8[4194304]{0:T(1024)(128)(4,1)S(1)}, s32[]{:S(2)}) async-start(s8[6291456]{0:T(1024)(128)(4,1)} %bitcast.69), calls=%async_computation.6 | async-start | bytes 8388608
  282.2 13.3 %copy-start.19 = (f32[1024,1536]{1,0:T(8,128)}, f32[1024,1536]{1,0:T(8,128)S(1)}, u32[]{:S(2)}) copy-start(f32[1024,1536]{1,0:T(8,128)S(1)} %fusion.10) | copy-start | bytes 18874372
  282.2 14.9 %slice-start.1 = ((s8[6291456]{0:T(1024)(128)(4,1)}), s8[2097152]{0:T(1024)(128)(4,1)S(1)}, s32[]{:S(2)}) async-start(s8[6291456]{0:T(1024)(128)(4,1)} %bitcast.69), calls=%async_computation.7 | async-start | bytes 4194304
  320.9 348.8 %reduce-scatter.5.cloned.1.call-start = ((), (), s32[]{:S(2)}) async-start(), calls=%async_computation.5 | async-start | bytes 2621440 | tf_op jit(solution)/shard_map/reduce_scatter | solution.py:1433
  321.3 19.0 %slice-start.2 = ((s8[6291456]{0:T(1024)(128)(4,1)}), s8[4194304]{0:T(1024)(128)(4,1)S(1)}, s32[]{:S(2)}) async-start(s8[6291456]{0:T(1024)(128)(4,1)} %bitcast.71), calls=%async_computation.8 | async-start | bytes 8388608
  324.1 16.2 %copy-start.1 = (bf16[2,512,2048]{2,1,0:T(8,128)(2,1)}, bf16[2,512,2048]{2,1,0:T(8,128)(2,1)S(1)}, u32[]{:S(2)}) copy-start(bf16[2,512,2048]{2,1,0:T(8,128)(2,1)S(1)} %pad_maximum_fusion) | copy-start | bytes 12582916
  324.1 16.2 %slice-start.3 = ((s8[6291456]{0:T(1024)(128)(4,1)}), s8[2097152]{0:T(1024)(128)(4,1)S(1)}, s32[]{:S(2)}) async-start(s8[6291456]{0:T(1024)(128)(4,1)} %bitcast.71), calls=%async_computation.9 | async-start | bytes 4194304
  340.3 6.7 copy-start.17
  340.3 6.7 copy-start.20
  358.1 135.8 %copy-start.6 = (f32[2,4,2,64,4]{4,3,2,1,0:T(8,128)S(1)}, f32[2,4,2,64,4]{4,3,2,1,0:T(8,128)}, u32[]{:S(2)}) copy-start(f32[2,4,2,64,4]{4,3,2,1,0:T(8,128)} %get-tuple-element.65) | copy-start | bytes 49156
  669.6 5.3 copy-start.8
  669.6 6.1 copy-start.10
  669.6 6.8 copy-start.9
  672.9 5.2 copy-start.7
  672.9 6.0 copy-start.12
  672.9 6.6 copy-start.5
  674.2 6.4 copy-start.4
  675.6 6.1 copy-start.3
  (5 other events, 18.4 us)
Sparse Core Ops, SparseCore 0:
  115.1 44.0 all-gather.2
  271.3 44.6 all-gather.4
  321.0 42.5 reduce-scatter.2
  493.4 42.7 reduce-scatter.4

commit v3 on v2

--- a/solution.py
+++ b/solution.py
@@ -13,6 +13,10 @@
 log2e = 1.0 / math.log(2.0)
 bf16 = jnp.bfloat16
 f32 = jnp.float32
+back_quiet = (0, 2)
+back_piece = 32
+tail_piece = 64
+tail_items = 3
 vmem_bytes = 61 * 1024 * 1024
 
 MESH = pl.DeviceIdType.MESH
@@ -195,9 +199,24 @@
 
 def attend_back_kernel(heads, kv_heads, dim, block, scale, bounds_ref, q_ref, kv_ref, dgated_ref, att_ref,
                        logit_ref, logit_row_ref, lse_ref, start_ref, pos_ref, nq_ref, rq_ref, cos_ref, sin_ref,
-                       gain_ref, dq_ref, dlogit_ref, dkv_ref, dgain_ref,
-                       q2_ref, da2_ref, delta_ref, lse2_ref, dq2_ref):
+                       gain_ref, ggate_ref, gup_ref, gdown_ref, dq_ref, dlogit_ref, dkv_ref, dgain_ref, ggate_out,
+                       gup_out, gdown_out, q2_ref, da2_ref, delta_ref, lse2_ref, dq2_ref, *moved):
     row = pl.program_id(0)
+    slots, move_sems = moved[:3], moved[3]
+    takes = [
+        pltpu.make_async_copy(source, slot, move_sems.at[0, i])
+        for i, (source, slot) in enumerate(zip((ggate_ref, gup_ref, gdown_ref), slots))
+    ]
+    gives = [
+        pltpu.make_async_copy(slot, target, move_sems.at[1, i])
+        for i, (slot, target) in enumerate(zip(slots, (ggate_out, gup_out, gdown_out)))
+    ]
+
+    @pl.when(row == 0)
+    def _():
+        for move in takes:
+            move.start()
+
     group = q_ref.shape[1]
     repeat = heads // kv_heads
     cosine, sine, gain = cos_ref[...], sin_ref[...], gain_ref[...]
@@ -258,8 +277,19 @@
             mean = jnp.mean(inner * unit, axis=1, keepdims=True)
             dq_ref[0, :, at] = (rq_ref[0, :, n:n + 1] * (inner - unit * mean)).astype(bf16)
 
-
-def attend_back(q, kv, dgated, att, logits, logit_rows, lse, bounds, start_row, pos_row, nq, rq, tables, gain,
+    @pl.when(row == 0)
+    def _():
+        for take, give in zip(takes, gives):
+            take.wait()
+            give.start()
+
+    @pl.when(row == pl.num_programs(0) - 1)
+    def _():
+        for give in gives:
+            give.wait()
+
+
+def attend_back(q, kv, dgated, att, logits, logit_rows, lse, bounds, start_row, pos_row, nq, rq, tables, gain, moved,
                 heads, kv_heads, dim, block, scale):
     rows, group, width = q.shape
     total = kv.shape[1]
@@ -278,15 +308,20 @@
             in_specs=[
                 wide, by_row(total, kv.shape[2]), wide, wide, by_row(group, heads), by_row(heads, group),
                 by_row(heads, group), by_row(1, group), full((1, group)), wide, by_row(group, heads),
-                full((group, dim)), full((group, dim)), full((1, dim)),
+                full((group, dim)), full((group, dim)), full((1, dim)), *[pl.BlockSpec(memory_space=pl.ANY)] * 3,
             ],
-            out_specs=[wide, by_row(heads, group), by_row(total, kv.shape[2]), full((1, dim))],
+            out_specs=[
+                wide, by_row(heads, group), by_row(total, kv.shape[2]), full((1, dim)),
+                *[pl.BlockSpec(memory_space=pl.ANY)] * 3,
+            ],
             scratch_shapes=[
                 pltpu.VMEM((repeat * group, dim), bf16),
                 pltpu.VMEM((repeat * group, dim), bf16),
                 pltpu.VMEM((1, repeat * group), f32),
                 pltpu.VMEM((1, repeat * group), f32),
                 pltpu.VMEM((repeat * group, dim), f32),
+                *[pltpu.VMEM(m.shape, m.dtype) for m in moved],
+                pltpu.SemaphoreType.DMA((2, 3)),
             ],
         ),
         out_shape=[
@@ -294,13 +329,14 @@
             jax.ShapeDtypeStruct((rows, heads, group), f32),
             jax.ShapeDtypeStruct(kv.shape, bf16),
             jax.ShapeDtypeStruct((1, dim), f32),
+            *[jax.ShapeDtypeStruct(m.shape, m.dtype) for m in moved],
         ],
         compiler_params=params(),
         cost_estimate=cost(
             5 * rows * heads * group * total * dim, 4 * kv.size + 10 * q.size, rows * heads * group * total // 2
         ),
         name="attend_back",
-    )(bounds, q, kv, dgated, att, logits, logit_rows, lse, start_row, pos_row, nq, rq, cosine, sine, gain[None])
+    )(bounds, q, kv, dgated, att, logits, logit_rows, lse, start_row, pos_row, nq, rq, cosine, sine, gain[None], *moved)
 
 
 def key_back_kernel(kv_heads, dim, dkv_ref, nk_ref, rk_ref, cos_ref, sin_ref, gain_ref, dk_ref, dgain_ref):
@@ -478,23 +514,23 @@
                     def _():
                         self.spread_copy(way, k, s, owner).wait_send()
 
-    def run(self, beside=()):
+    def run(self, beside=(), quiet=(0, 0)):
         beside, done = list(beside), 0
-        slots = self.pieces * len(self.stages)
-        for step in range(self.pieces + len(self.stages) - 1):
-            for s in range(self.pieces):
-                if 0 <= step - s < len(self.stages):
-                    self.stages[step - s](s)
-                    slots -= 1
-                    until = len(beside) if slots == 0 else done + -(-(len(beside) - done) // (slots + 1))
-                    for item in beside[done:until]:
-                        item()
-                    done = until
+        steps = self.pieces + len(self.stages) - 1
+        turns = [(step, s) for step in range(steps) for s in range(self.pieces) if 0 <= step - s < len(self.stages)]
+        slots = [i for i, (step, _) in enumerate(turns) if quiet[0] <= step < steps - quiet[1]]
+        for i, (step, s) in enumerate(turns):
+            self.stages[step - s](s)
+            if i in slots:
+                until = len(beside) * (slots.index(i) + 1) // len(slots)
+                for item in beside[done:until]:
+                    item()
+                done = until
         self.drain_reduce()
         self.drain_spread()
 
 
-def line_all_sum(n, seqs, rows, piece, finish, part_ref, out_ref, land_ref, sems, beside=()):
+def line_all_sum(n, seqs, rows, piece, finish, part_ref, out_ref, land_ref, sems, beside=(), quiet=(0, 0)):
     cuts = [(q, c) for q in range(seqs) for c in range(rows // piece)]
 
     def at(ref):
@@ -502,7 +538,7 @@
             cuts[s][0], pl.ds(pl.multiple_of(owner * rows + cuts[s][1] * piece, piece), piece)]
 
     LineSum(n, len(cuts), at(part_ref), lambda s, total: finish(*cuts[s], total), land_ref, sems, at(out_ref)).run(
-        beside)
+        beside, quiet)
 
 
 def line_scratch(n, seqs, rows, piece, width):
@@ -894,36 +930,38 @@
             else:
                 out[:, to] = total
 
-        buf = plane_scratch[i % 2]
-        land, send, recv = plane_scratch[2 + 3 * i:5 + 3 * i]
+        buf = plane_scratch[i % 3]
+        land, send, recv = plane_scratch[3 + 3 * i:6 + 3 * i]
         sums.append(PlaneSum(bits, n_uly, None, store, buf, land, send, recv))
     last = bits - 2
 
     order = list(range(1, 1 << bits, 2)) + list(range(0, 1 << bits, 2))
+    quiet = back_quiet
     beside = []
+
+    def product(i, turn):
+        def take(value):
+            sums[i].buf[order[turn]] = value.astype(bf16)
+            if order[turn] % 2:
+                sums[i].first_copy(order[turn]).start()
+
+        streamed.product(i, turn, [sums[i].me ^ e for e in order], take)
+
     for i in range(len(jobs) + last + 1):
-        for level in range(last, -1, -1):
+        if i < len(jobs):
+            beside += [functools.partial(product, i, turn) for turn in range(len(order))]
+        for level in range(last):
             j = i - 1 - level
             if 0 <= j < len(jobs):
-                beside.append(functools.partial(sums[j].pull, level))
-                beside.append(functools.partial(sums[j].push, level + 1) if level < last else sums[j].finish)
+                beside += [functools.partial(sums[j].pull, level), functools.partial(sums[j].push, level + 1)]
         if i < len(jobs):
-            job = sums[i]
-
-            def product(turn, i=i, job=job):
-                def take(value):
-                    job.buf[order[turn]] = value.astype(bf16)
-                    if order[turn] % 2:
-                        job.first_copy(order[turn]).start()
-
-                streamed.product(i, turn, [job.me ^ e for e in order], take)
-
-            beside += [functools.partial(product, turn) for turn in range(len(order))]
-            beside += [job.pair, functools.partial(job.push, 0)]
+            beside += [sums[i].pair, functools.partial(sums[i].push, 0)]
+        if 0 <= i - 1 - last < len(jobs):
+            beside += [functools.partial(sums[i - 1 - last].pull, last), sums[i - 1 - last].finish]
 
     line_and_plane_barrier(n, lax.axis_index("tp"), bits, n_uly)
     line_all_sum(n, seqs, rows, piece, finish, part_ref, out_ref, land_ref, (rs_send, rs_recv, ag_send, ag_recv),
-                 beside)
+                 beside, quiet)
 
 
 def norm_back(part, cotangent, middle, gain, a2, cot_all, d_gate, d_up, hidden, n, sizes, collective_id):
@@ -939,7 +977,7 @@
             (jax.ShapeDtypeStruct((1, width), f32),), collective_id, "norm_back")
         grads = outer_sums((a2, cot_all), (0, 0, 1), (d_gate, d_up, hidden), sizes, 0)
         return (out, d_mid, dgain, *grads[:2], grads[2].T)
-    piece = min(64, rows)
+    piece = min(back_piece, rows)
     half = units // 2
     vm, anywhere = pl.BlockSpec(memory_space=pltpu.VMEM), pl.BlockSpec(memory_space=pl.ANY)
     shapes = [
@@ -957,7 +995,7 @@
             *line_scratch(n, seqs, rows, piece, width),
             pltpu.VMEM((2, tokens, each), bf16), pltpu.VMEM((2, tokens, half), bf16),
             pltpu.SemaphoreType.DMA((2,)), pltpu.SemaphoreType.DMA((2,)),
-            plane_scratch[0][0], plane_scratch[0][0],
+            plane_scratch[0][0], plane_scratch[0][0], plane_scratch[0][0],
             *[item for scratch in plane_scratch for item in scratch[1:]],
         ],
         compiler_params=pltpu.CompilerParams(
@@ -1065,7 +1103,7 @@
         partial = mm(cut_ref[:, :q_cols], wq_ref[...], NT)
         partial += mm(cut_ref[:, q_cols:q_cols + kv_cols], wk_ref[...], NT)
         partial += mm(cut_ref[:, q_cols + kv_cols:n_main], wv_ref[...], NT)
-        partial += mm(cut_ref[:, n_main:n_main + heads], wg_ref[...], NT)
+        partial += mm(cut_ref[:, n_main:n_main + heads], wg_ref[...])
         partial = partial.astype(bf16)
         for t in range(n):
             at = slice(t * piece, (t + 1) * piece)
@@ -1073,13 +1111,16 @@
             part_ref[to] = partial[at]
             all_ref[to] = cut_ref[at]
 
-    def part_at(owner, s):
-        q, c = cuts[s]
-        return part_ref.at[pl.ds(pl.multiple_of(row_at(q, owner, c), piece), piece)]
-
-    def own(s, total):
-        q, c = cuts[s]
-        at = slice(c * piece, (c + 1) * piece)
+    split = line_land.shape[2] // len(cuts)
+    short = piece // split
+
+    def part_at(owner, p):
+        q, c = cuts[p // split]
+        return part_ref.at[pl.ds(pl.multiple_of(row_at(q, owner, c) + p % split * short, short), short)]
+
+    def own(p, total):
+        q, c = cuts[p // split]
+        at = slice(c * piece + p % split * short, c * piece + (p % split + 1) * short)
         x = x_ref[q, at].astype(f32)
         inverse = rms_inverse(x)
         unit = x * inverse
@@ -1087,7 +1128,7 @@
         mean = jnp.mean(inner * unit, axis=-1, keepdims=True)
         gin_ref[q, at] = dmid_ref[q, at] + inverse * (inner - unit * mean)
 
-    line = LineSum(n, len(cuts), part_at, own, line_land, (rs_send, rs_recv))
+    line = LineSum(n, len(cuts) * split, part_at, own, line_land, (rs_send, rs_recv))
 
     order = list(range(1, 1 << bits, 2)) + list(range(0, 1 << bits, 2))
     turns = [(dbranch_ref, e) for e in order] + [(first_ref, e) for e in order]
@@ -1101,8 +1142,10 @@
         gout_ref[at] = total.T
 
     def store_first(at, total):
+        if at.start + at.size > n_main:
+            gh_ref[...] = total[:, n_main - at.start:].T[:heads]
         first = 0
-        for out in (gq_ref, gk_ref, gv_ref, gh_ref):
+        for out in (gq_ref, gk_ref, gv_ref):
             lo, hi = max(first, at.start), min(first + out.shape[1], at.start + at.size)
             if lo < hi:
                 out[:, lo - first:hi - first] = total[:, lo - at.start:hi - at.start]
@@ -1130,8 +1173,8 @@
                     lanes += value[:, first + k:first + k + 128] * w_ref[at, k:k + 128].astype(f32)
                 first += w_ref.shape[1]
             total = jnp.sum(lanes.T, axis=0, keepdims=True)
-            last = value[:, n_main:n_main + heads] * wg_ref[at].astype(f32)
-            total += jnp.sum(last.T, axis=0, keepdims=True)
+            last = value[:, n_main:].T[:heads] * wg_ref[:, at].astype(f32)
+            total += jnp.sum(last, axis=0, keepdims=True)
             vec_ref[0, :, at] = total / gain_ref[:, at]
 
     line_bits = n.bit_length() - 1
@@ -1151,20 +1194,23 @@
             vec_copy(k).start()
 
     def levels(job):
-        items = [job.pair, functools.partial(job.push, 0)]
+        items = []
         for level in range(bits - 1):
             items.append(functools.partial(job.pull, level))
             if level + 1 < bits - 1:
                 items.append(functools.partial(job.push, level + 1))
         return items
 
-    early = [functools.partial(product, i) for i in range(len(order))] + levels(out_sum)
+    early = [functools.partial(product, i) for i in range(len(order))]
+    early += [out_sum.pair, functools.partial(out_sum.push, 0)]
     late = [functools.partial(product, i) for i in range(len(order), len(turns))]
+    late.append(functools.partial(vec_step, 0))
+    late += levels(out_sum)[:2]
     late += [first_sum.pair, functools.partial(first_sum.push, 0)]
-    rest = levels(first_sum)[2:]
-    for k in range(steps + 1):
+    rest = levels(out_sum)[2:] + levels(first_sum)
+    for k in range(1, steps + 1):
         late.append(functools.partial(vec_step, k))
-        if rest and k % 2:
+        if k % 2 == 0 and rest:
             late.append(rest.pop(0))
     late += rest
 
@@ -1173,7 +1219,8 @@
         job.compute()
     left_copy(0).start()
     ready = 0
-    for step in range(len(cuts) + bits - 1 + n - 1):
+    line_steps = split * (len(cuts) + bits - 1) + n - 1
+    for step in range(-(-line_steps // split)):
         if step < len(cuts):
             sums[step].pair()
             sums[step].push(0)
@@ -1186,14 +1233,15 @@
                 else:
                     turn(j)
                     ready += 1
-        for s in range(len(cuts)):
-            stage = step - s - (bits - 1)
-            if 0 <= stage < n:
-                line.stages[stage](s)
-                queue = early or (late if ready == len(cuts) else [])
-                for item in queue[:3]:
-                    item()
-                del queue[:3]
+        for turn_of in range(split * step, split * (step + 1)):
+            for p in range(line.pieces):
+                stage = turn_of - p - split * (bits - 1)
+                if 0 <= stage < n:
+                    line.stages[stage](p)
+                    queue = early or (late if ready == len(cuts) else [])
+                    for item in queue[:tail_items]:
+                        item()
+                    del queue[:tail_items]
     for item in early + late:
         item()
     line.drain_reduce()
@@ -1234,10 +1282,10 @@
     plane_scratch += PlaneSum.scratch(bits, each, heads * dim) + PlaneSum.scratch(bits, each, wide)
     shapes = [
         jax.ShapeDtypeStruct(shape, f32) for shape in (
-            x.shape, (each, heads * dim), (each, kv_heads * dim), (each, kv_heads * dim), (each, heads),
+            x.shape, (each, heads * dim), (each, kv_heads * dim), (each, kv_heads * dim), (heads, each),
             (heads * dim, each), (1, width), (1, width), (1, dim), (1, dim))
     ]
-    line = line_scratch(n, seqs, rows, piece, width)
+    line = line_scratch(n, seqs, rows, min(tail_piece, piece), width)
     return pl.pallas_call(
         functools.partial(layer_back_kernel, n, bits, n_uly, heads, kv_heads, dim),
         in_specs=[anywhere] * 3 + [vm] * 17,
@@ -1365,7 +1413,7 @@
             q_ref[q, :, c, :, at] = tiles((rope(unit, qg_ref[...]) * (scale * log2e)).astype(bf16))
             nq_ref[q, :, c, :, at] = tiles(unit.astype(bf16))
             rq_ref[q, :, c, :, h:h + 1] = tiles(inverse)
-        logit_ref[q, :, c] = tiles(mm(a1, wg_ref[...]).astype(bf16).astype(f32))
+        logit_ref[q, :, c] = tiles(mm(a1, wg_ref[...], NT).astype(bf16).astype(f32))
 
     line_and_plane_barrier(n, lax.axis_index("tp"), bits, n_uly)
     for step in range(len(cuts) + n - 1 + bits):
@@ -1416,11 +1464,38 @@
         compiler_params=params(collective_id=collective_id, has_side_effects=True),
         cost_estimate=cost(2 * seqs * n * rows * width * 1024, 200_000_000),
         name="layer_front",
-    )(x, attn_norm[None], w_query, w_key, w_value, w_headgate,
+    )(x, attn_norm[None], w_query, w_key, w_value, w_headgate.T,
       *[t.reshape(n, cut_count, piece, dim) for t in tables], query_norm[None], key_norm[None])
     return [m.reshape(seqs, -1, m.shape[-1]) for m in made]
 
 
+def finish_kernel(count, *refs):
+    sources, mid_ref, adds, targets, out_ref = refs[:count], refs[count], refs[count + 1:-count - 1], refs[-count - 1:-1], refs[-1]
+    for source, target in zip(sources, targets):
+        target[...] = source[...]
+    first = 0
+    for add_ref in adds:
+        last = first + add_ref.shape[0]
+        out_ref[first:last] = (mid_ref[first:last] + add_ref[...].astype(f32)).astype(bf16)
+        first = last
+
+
+def finish(sources, middle, adds):
+    vm = pl.BlockSpec(memory_space=pltpu.VMEM)
+    count = len(sources)
+    made = pl.pallas_call(
+        functools.partial(finish_kernel, count),
+        in_specs=[vm] * (count + 1 + len(adds)),
+        out_specs=[vm] * (count + 1),
+        out_shape=[jax.ShapeDtypeStruct(s.shape, s.dtype) for s in sources]
+        + [jax.ShapeDtypeStruct(middle.shape, bf16)],
+        compiler_params=params(),
+        cost_estimate=cost(middle.size, 20 * middle.size),
+        name="finish",
+    )(*sources, middle, *adds)
+    return made[:-1], made[-1]
+
+
 def flatten(values):
     return values.reshape(-1, values.shape[-1])
 
@@ -1430,7 +1505,7 @@
 
 
 def collect(values):
-    return lax.psum_scatter(values.astype(bf16), "tp", scatter_dimension=1, tiled=True).astype(f32)
+    return lax.psum_scatter(values.astype(bf16), "tp", scatter_dimension=1, tiled=True)
 
 
 def per_device(sizes, inputs, doc_ids, attn_norm, w_query, w_key, w_value, w_headgate, query_norm, key_norm, w_output,
@@ -1513,23 +1588,25 @@
     if near < seqs:
         late_made, d_branch = lax.optimization_barrier((made[near:], d_branch))
         outs.append(collect(late_made))
-    outputs = (middle + jnp.concatenate(outs, axis=0)).astype(bf16)
     d_gated = wide(mm(flatten(d_branch), w_output, NT).astype(bf16))
-    d_q, d_logit, d_kv, d_qgain = attend_back(
+    d_q, d_logit, d_kv, d_qgain, grad_gate, grad_up, grad_down = attend_back(
         q, kv, d_gated, att, logits, logits.transpose(0, 2, 1), lse, bounds, start[:, None, :], positions[None, :], nq,
-        rq, tables, query_norm, heads, kv_heads, dim, block, scale)
+        rq, tables, query_norm, (grad_gate, grad_up, grad_down), heads, kv_heads, dim, block, scale)
     d_logit = jnp.pad(d_logit.astype(bf16).transpose(0, 2, 1), ((0, 0), (0, 0), (0, pad)))
     if fits_plane(sizes, width):
         grad_inputs, *grads = layer_back(
             d_kv, flatten(first), flatten(d_branch), d_q, d_logit, nk, rk, tables, key_norm,
-            (w_query, w_key, w_value, w_headgate), flatten(gated), inputs, attn_norm, d_mid, d_qgain, grad_mlp_norm, n_tensor, sizes, heads, kv_heads, 3)
-        grad_query, grad_key, grad_value, grad_headgate, grad_output = grads[:5]
+            (w_query, w_key, w_value, w_headgate.T), flatten(gated), inputs, attn_norm, d_mid, d_qgain, grad_mlp_norm, n_tensor, sizes, heads, kv_heads, 3)
+        (grad_inputs, grad_query, grad_key, grad_value, grad_headgate, grad_output), outputs = finish(
+            (grad_inputs, *grads[:5]), middle, outs)
+        grad_headgate = grad_headgate.T
         grad_attn_norm, grad_mlp_norm, grad_query_norm, grad_key_norm = (g[0] for g in grads[5:])
     else:
+        outputs = (middle + jnp.concatenate(outs, axis=0).astype(f32)).astype(bf16)
         d_kv = blocks_sum(d_kv, sizes, 3)
         d_kv, d_kgain = key_back(d_kv, nk, rk, tables, key_norm, kv_heads, dim)
         d_all = flatten(jnp.concatenate([d_q, d_kv, d_logit], axis=-1))
-        d_first = collect(wide(mm(d_all, w_first, NT)))
+        d_first = collect(wide(mm(d_all, w_first, NT))).astype(f32)
 
         grad_first, grad_output = outer_sums(
             (flatten(first), flatten(d_branch)), (0, 1), (d_all, flatten(gated)), sizes, 4)

time: 697 us -> 675 us (0.968)
  local copies, waits for them, and re-layouts: 25.9 us -> 14.7 us
  Pallas kernels: 525 us -> 515 us
    pallas_call x1, Pallas kernels: 135 us -> 122 us  [norm_back(): pl.pallas_call(functools.partial(norm_back_kernel, n, seqs, rows, piece,...]
    unnamed x65 -> x37, local copies, waits for them, and re-layouts: 15.4 us -> 4.16 us
where the time goes in v3:
time: 675 us; the launch traced here: 668 us
  Pallas kernels  515 us (76%)
  matrix products  79.8 us (12%)
  waiting for transfers between devices  34.1 us (5%)
  local copies, waits for them, and re-layouts  14.7 us (2%)
  between operations  14.5 us (2%)
  other arithmetic  8.55 us (1%)
    pallas_call x1, Pallas kernels, layer_back(): pl.pallas_call(functools.partial(layer_back_kernel, n, bits, n_uly, heads...  144 us
    pallas_call x1, Pallas kernels, norm_back(): pl.pallas_call(functools.partial(norm_back_kernel, n, seqs, rows, piece,...  122 us
    pallas_call x1, Pallas kernels, line_call(): pl.pallas_call(functools.partial(kernel, n, seqs, rows, piece), in_specs=...  112 us
    pallas_call x1, Pallas kernels, layer_front(): pl.pallas_call(functools.partial(layer_front_kernel, n, bits, n_uly, head...  101 us
    dot_general x8, matrix products, mm(): return lax.dot_general(left, right, dims, preferred_element_type=f32)  79.8 us
    all_gather x2, waiting for transfers between devices, spread(): return lax.all_gather(values.astype(bf16), 'tp', axis=1, tiled=True)  34 us
    pallas_call x1, Pallas kernels, attend_back(): pl.pallas_call(functools.partial(attend_back_kernel, heads, kv_heads, dim...  19.6 us
  transfers between devices with their start and end apart: 4, of which 2 were waited for; matrix products, arithmetic and copies ran while one was open for 13% of the time, Pallas kernels for 45%

profile of v3, /device:TPU:0, one launch (start us, length us, event | category | flops | bytes accessed | tf_op | source)
XLA Modules:
  0.0 667.8 jit_solution(11400121080353512210)
XLA Ops:
  7.3 1.0 fusion.1
  8.3 0.8 pad_maximum_fusion.1.cos_ref
  10.0 2.3 fusion.9
  12.2 100.6 %layer_front.1 = (bf16[2,4,2,64,2048]{4,3,2,1,0:T(8,128)(2,1)}, bf16[2,4,2,64,512]{4,3,2,1,0:T(8,128)(2,1)}, bf16[2,32,2,64,512]{4,3,2,1,0:T(8,128)(2,1)}, bf16[...) custom-call(bf16[2,128,2048]{2,1,0:T(8,128)(2,1)} %x_ref.5, ...), custom_call_target="tpu_custom_call" | custom-call | flops 4294967296 | bytes 200000000 | tf_op jit(solution)/shard_map/layer_front/pallas_call | solution.py:1458
  113.7 1.0 copy.38.start_ref
  116.1 12.1 %attend.1 = (bf16[2,512,512]{2,1,0:T(8,128)(2,1)}, bf16[2,512,512]{2,1,0:T(8,128)(2,1)}, f32[2,4,512]{2,1,0:T(4,128)}) custom-call(s32[2,4]{1,0:T(2,128)} %pad_add_fusion.bounds_ref, bf16[2,512,512]{2,1,0:T(8,128)(2,1)} %bitcast.94, bf16[2,4096,512]{2,1,0:T(8,128)(2,1)} %bitcast.87, s32[2,512,1]{2,1,0:T(8,128)} %copy.38.start_ref, ...), custom_call_target="tpu_custom_call" | custom-call | flops 4294967296 | bytes 11534336 | tf_op jit(solution)/shard_map/attend/pallas_call | solution.py:171
  128.2 5.6 convolution_convert_fusion.1
  133.8 23.3 %all-gather.3.cloned.1.call-done = bf16[1,512,2048]{2,1,0:T(8,128)(2,1)} async-done(((bf16[1,128,2048]{2,1,0:T(8,128)(2,1)}), bf16[1,512,2048]{2,1,0:T(8,128)(2,1)}) %all-gather.3.cloned.1.call-update) | async-done | bytes 2097168 | tf_op jit(solution)/shard_map/all_gather | solution.py:1504
  157.1 111.9 %norm_forward.1 = (bf16[2,512,2048]{2,1,0:T(8,128)(2,1)}, f32[2,128,2048]{2,1,0:T(8,128)}) custom-call(bf16[2,512,2048]{2,1,0:T(8,128)(2,1)} %bitcast.52, bf16[2,128,2048]{2,1,0:T(8,128)(2,1)} %x_ref.5, f32[1,2048]{1,0:T(1,128)} %bitcast.66), custom_call_target="tpu_custom_call" | custom-call | flops 41943040 | bytes 100000000 | tf_op jit(solution)/shard_map/norm_forward/pallas_call | solution.py:569
  269.3 10.6 %fusion.10 = f32[1024,1536]{1,0:T(8,128)S(1)} fusion(bf16[1024,2048]{1,0:T(8,128)(2,1)} %bitcast.75, bf16[2048,1536]{1,0:T(8,128)(2,1)} %param.26), kind=kOutput, calls=%fused_computation.49 | convolution fusion | flops 6442450944 | bytes 16777216 | tf_op jit(solution)/shard_map/dot_general | solution.py:29
  279.9 13.3 %multiply_convert_fusion.2 = (bf16[1024,1536]{1,0:T(8,128)(2,1)S(1)}, f32[1024,1536]{1,0:T(8,128)}) fusion(f32[1024,1536]{1,0:T(8,128)S(1)} %fusion.10, bf16[1024,2048]{1,0:T(8,128)(2,1)S(1)} %bitcast.77, bf16[2048,1536]{1,0:T(8,128)(2,1)} %param.27), kind=kOutput, calls=%fused_computation.3 | convolution fusion | flops 6451888128 | bytes 26214400 | tf_op jit(solution)/shard_map/dot_general | solution.py:29
  293.2 1.6 copy-done.9
  294.9 8.2 %convolution_convert_fusion = bf16[1024,2048]{1,0:T(8,128)(2,1)} fusion(bf16[1024,1536]{1,0:T(8,128)(2,1)S(1)} %get-tuple-element.145.hidden_ref, bf16[1536,2048]{1,0:T(8,128)(2,1)S(1)} %bitcast.72), kind=kOutput, calls=%fused_computation.7 | convolution fusion | flops 6444548096 | bytes 13631488 | tf_op jit(solution)/shard_map/dot_general | solution.py:29
  303.1 10.7 %all-gather.5.cloned.1.call-done = bf16[1,512,2048]{2,1,0:T(8,128)(2,1)} async-done(((bf16[1,128,2048]{2,1,0:T(8,128)(2,1)}), bf16[1,512,2048]{2,1,0:T(8,128)(2,1)}) %all-gather.5.cloned.1.call-update) | async-done | bytes 2097168 | tf_op jit(solution)/shard_map/all_gather | solution.py:1504
  313.8 4.9 fusion.8
  319.2 2.8 pad_maximum_fusion
  322.0 16.7 %multiply_convert_fusion = (bf16[1024,1536]{1,0:T(8,128)(2,1)}, bf16[1024,1536]{1,0:T(8,128)(2,1)}) fusion(f32[1024,1536]{1,0:T(8,128)} %copy-done.10, f32[1024,1536]{1,0:T(8,128)} %get-tuple-element.146, bf16[1024,2048]{1,0:T(8,128)(2,1)S(1)} %bitcast.53, bf16[1536,2048]{1,0:T(8,128)(2,1)} %param.28), kind=kOutput, calls=%fused_computation.1 | convolution fusion | flops 6462898176 | bytes 29360128 | tf_op jit(solution)/shard_map/dot_general | solution.py:29
  338.7 8.7 %fusion.11 = f32[1024,2048]{1,0:T(8,128)S(1)} fusion(bf16[1024,1536]{1,0:T(8,128)(2,1)} %get-tuple-element.137.dgate_ref, bf16[2048,1536]{1,0:T(8,128)(2,1)S(1)} %bitcast.74), kind=kOutput, calls=%fused_computation.50 | convolution fusion | flops 6442450944 | bytes 17825792 | tf_op jit(solution)/shard_map/dot_general | solution.py:29
  347.4 11.2 %add_convert_fusion = bf16[1024,2048]{1,0:T(8,128)(2,1)} fusion(f32[1024,2048]{1,0:T(8,128)S(1)} %fusion.11, bf16[1024,1536]{1,0:T(8,128)(2,1)S(1)} %copy-done.11, bf16[2048,1536]{1,0:T(8,128)(2,1)} %param.27), kind=kOutput, calls=%fused_computation | convolution fusion | flops 6446645248 | bytes 22020096 | tf_op jit(solution)/shard_map/dot_general | solution.py:29
  358.6 121.8 %norm_back.1 = (bf16[2,512,2048]{2,1,0:T(8,128)(2,1)}, f32[2,128,2048]{2,1,0:T(8,128)}, f32[1,2048]{1,0:T(1,128)}, f32[256,1536]{1,0:T(8,128)}, f32[256,1536]{1,0:T(8,128)}, /*index=5*/f32[1536,256]{1,0:T(8,128)}) custom-call(bf16[2,512,2048]{2,1,0:T(8,128)(2,1)} %bitcast.93, bf16[2,128,2048]{2,1,0:T(8,128)(2,1)} %cot_ref.1, ...), custom_call_target="tpu_custom_call" | custom-call | flops 19327352832 | bytes 250000000 | tf_op jit(solution)/shard_map/norm_back/pallas_call | solution.py:989
  482.4 5.5 convolution_convert_fusion.2
  487.9 19.6 %attend_back.1 = (bf16[2,512,512]{2,1,0:T(8,128)(2,1)}, f32[2,4,512]{2,1,0:T(4,128)}, bf16[2,4096,512]{2,1,0:T(8,128)(2,1)}, f32[1,128]{1,0:T(1,128)}, f32[256,1...) custom-call(s32[2,4]{1,0:T(2,128)} %pad_add_fusion.bounds_ref, bf16[2,512,512]{2,1,0:T(8,128)(2,1)} %bitcast.95, ...), custom_call_target="tpu_custom_call" | custom-call | flops 10737418240 | bytes 22020096 | tf_op jit(solution)/shard_map/attend_back/pallas_call | solution.py:303
  509.2 144.1 %layer_back.1 = (f32[2,128,2048]{2,1,0:T(8,128)}, f32[256,512]{1,0:T(8,128)}, f32[256,256]{1,0:T(8,128)}, f32[256,256]{1,0:T(8,128)}, f32[4,256]{1,0:T(4,128)}, ...) custom-call(bf16[2,32,2,64,512]{4,3,2,1,0:T(8,128)(2,1)} %bitcast.89, ...), custom_call_target="tpu_custom_call" | custom-call | flops 9663676416 | bytes 250000000 | tf_op jit(solution)/shard_map/layer_back/pallas_call | solution.py:1289
  653.4 5.1 finish.1
  (65 shorter events, 9.9 us)
Async XLA Ops:
  7.2 121.1 %copy-start = (bf16[512,2048]{1,0:T(8,128)(2,1)S(1)}, bf16[512,2048]{1,0:T(8,128)(2,1)}, u32[]{:S(2)}) copy-start(bf16[512,2048]{1,0:T(8,128)(2,1)} %param.24) | copy-start | bytes 6291460
  7.2 149.9 %all-gather.3.cloned.1.call-start = ((), (), s32[]{:S(2)}) async-start(), calls=%async_computation.2 | async-start | bytes 2621440 | tf_op jit(solution)/shard_map/all_gather | solution.py:1504
  12.2 100.8 %copy-start.3 = (s32[2,4096]{1,0:T(2,128)S(1)}, s32[2,4096]{1,0:T(2,128)}, u32[]{:S(2)}) copy-start(s32[2,4096]{1,0:T(2,128)} %param.16) | copy-start | bytes 98308
  112.8 201.0 %all-gather.5.cloned.1.call-start = ((), (), s32[]{:S(2)}) async-start(), calls=%async_computation.3 | async-start | bytes 2621440 | tf_op jit(solution)/shard_map/all_gather | solution.py:1504
  269.0 384.4 %reduce-scatter.3.cloned.1.call-start = ((), (), s32[]{:S(2)}) async-start(), calls=%async_computation.4 | async-start | bytes 2621440 | tf_op jit(solution)/shard_map/reduce_scatter | solution.py:1508
  269.3 10.6 %copy-start.6 = (bf16[2,512,2048]{2,1,0:T(8,128)(2,1)S(1)}, bf16[2,512,2048]{2,1,0:T(8,128)(2,1)}, u32[]{:S(2)}) copy-start(bf16[2,512,2048]{2,1,0:T(8,128)(2,1)} %get-tuple-element.80) | copy-start | bytes 12582916
  269.3 25.6 %slice-start = ((s8[6291456]{0:T(1024)(128)(4,1)}), s8[4194304]{0:T(1024)(128)(4,1)S(1)}, s32[]{:S(2)}) async-start(s8[6291456]{0:T(1024)(128)(4,1)} %bitcast.71), calls=%async_computation.6 | async-start | bytes 8388608
  279.9 13.3 %copy-start.10 = (f32[1024,1536]{1,0:T(8,128)}, f32[1024,1536]{1,0:T(8,128)S(1)}, u32[]{:S(2)}) copy-start(f32[1024,1536]{1,0:T(8,128)S(1)} %fusion.10) | copy-start | bytes 18874372
  279.9 15.0 %slice-start.1 = ((s8[6291456]{0:T(1024)(128)(4,1)}), s8[2097152]{0:T(1024)(128)(4,1)S(1)}, s32[]{:S(2)}) async-start(s8[6291456]{0:T(1024)(128)(4,1)} %bitcast.71), calls=%async_computation.7 | async-start | bytes 4194304
  293.2 1.6 copy-start.9
  318.7 334.7 %reduce-scatter.5.cloned.1.call-start = ((), (), s32[]{:S(2)}) async-start(), calls=%async_computation.5 | async-start | bytes 2621440 | tf_op jit(solution)/shard_map/reduce_scatter | solution.py:1508
  319.2 19.5 %slice-start.2 = ((s8[6291456]{0:T(1024)(128)(4,1)}), s8[4194304]{0:T(1024)(128)(4,1)S(1)}, s32[]{:S(2)}) async-start(s8[6291456]{0:T(1024)(128)(4,1)} %bitcast.73), calls=%async_computation.8 | async-start | bytes 8388608
  322.0 16.7 %copy-start.1 = (bf16[2,512,2048]{2,1,0:T(8,128)(2,1)}, bf16[2,512,2048]{2,1,0:T(8,128)(2,1)S(1)}, u32[]{:S(2)}) copy-start(bf16[2,512,2048]{2,1,0:T(8,128)(2,1)S(1)} %pad_maximum_fusion) | copy-start | bytes 12582916
  322.0 16.7 %slice-start.3 = ((s8[6291456]{0:T(1024)(128)(4,1)}), s8[2097152]{0:T(1024)(128)(4,1)S(1)}, s32[]{:S(2)}) async-start(s8[6291456]{0:T(1024)(128)(4,1)} %bitcast.73), calls=%async_computation.9 | async-start | bytes 4194304
  338.7 8.8 %copy-start.11 = (bf16[1024,1536]{1,0:T(8,128)(2,1)S(1)}, bf16[1024,1536]{1,0:T(8,128)(2,1)}, u32[]{:S(2)}) copy-start(bf16[1024,1536]{1,0:T(8,128)(2,1)} %get-tuple-element.136.dup_ref) | copy-start | bytes 9437188
  358.6 122.4 %copy-start.2 = (f32[2,4,2,64,4]{4,3,2,1,0:T(8,128)S(1)}, f32[2,4,2,64,4]{4,3,2,1,0:T(8,128)}, u32[]{:S(2)}) copy-start(f32[2,4,2,64,4]{4,3,2,1,0:T(8,128)} %get-tuple-element.75) | copy-start | bytes 49156
  653.3 5.2 copy-start.5
  653.3 5.8 copy-start.8
  653.3 6.3 copy-start.7
  653.3 6.8 %copy-start.4 = (f32[1,2048]{1,0:T(1,128)S(1)}, f32[1,2048]{1,0:T(1,128)}, u32[]{:S(2)}) copy-start(f32[1,2048]{1,0:T(1,128)} %get-tuple-element.122) | copy-start | bytes 24580
Sparse Core Ops, SparseCore 0:
  113.0 44.0 all-gather.2
  269.1 44.6 all-gather.4
  318.8 42.5 reduce-scatter.2
  480.5 42.6 reduce-scatter.4

commit v4 on v3

--- a/solution.py
+++ b/solution.py
@@ -377,6 +377,56 @@
     )(dkv, nk, rk, *tables, gain[None])
 
 
+def hidden_back_kernel(parts, *refs):
+    cots, (w_ref, gate_ref, up_ref, dgate_ref, dup_ref) = refs[:parts], refs[parts:]
+    first = 0
+    for cot_ref in cots:
+        at = slice(first, first + cot_ref.shape[0])
+        grad = mm(cot_ref[...], w_ref[...], NT)
+        gate, up = gate_ref[at], up_ref[at]
+        sigma = jax.nn.sigmoid(gate)
+        dgate_ref[at] = (grad * up * sigma * (1.0 + gate * (1.0 - sigma))).astype(bf16)
+        dup_ref[at] = (grad * gate * sigma).astype(bf16)
+        first = at.stop
+
+
+def hidden_back(cots, w_down, gate, up, block=256):
+    units, width = w_down.shape
+    tokens = gate.shape[0]
+    column = pl.BlockSpec((tokens, block), lambda j: (0, j))
+    return pl.pallas_call(
+        functools.partial(hidden_back_kernel, len(cots)),
+        grid=(units // block,),
+        in_specs=[*[full(c.shape) for c in cots], pl.BlockSpec((block, width), lambda j: (j, 0)), column, column],
+        out_specs=[column, column],
+        out_shape=[jax.ShapeDtypeStruct((tokens, units), bf16)] * 2,
+        compiler_params=params(),
+        cost_estimate=cost(2 * tokens * units * width, 40_000_000),
+        name="hidden_back",
+    )(*cots, w_down, gate, up)
+
+
+def second_back_kernel(dgate_ref, dup_ref, wgate_ref, wup_ref, out_ref):
+    total = mm(dgate_ref[...], wgate_ref[...], NT) + mm(dup_ref[...], wup_ref[...], NT)
+    out_ref[...] = total.astype(bf16)
+
+
+def second_back(d_gate, d_up, w_gate, w_up, block=256):
+    width, units = w_gate.shape
+    tokens = d_gate.shape[0]
+    rows = pl.BlockSpec((block, units), lambda j: (j, 0))
+    return pl.pallas_call(
+        second_back_kernel,
+        grid=(width // block,),
+        in_specs=[full(d_gate.shape), full(d_up.shape), rows, rows],
+        out_specs=pl.BlockSpec((tokens, block), lambda j: (0, j)),
+        out_shape=jax.ShapeDtypeStruct((tokens, width), bf16),
+        compiler_params=params(),
+        cost_estimate=cost(4 * tokens * units * width, 30_000_000),
+        name="second_back",
+    )(d_gate, d_up, w_gate, w_up)
+
+
 def line_barrier(n, me):
     barrier = pltpu.get_barrier_semaphore()
     for way in (1, -1):
@@ -884,29 +934,44 @@
         return pltpu.make_async_copy(
             right.at[:, pl.ds(half * wide, wide)], self.right.at[i % 2], self.right_sems.at[i % 2])
 
-    def left_copy(self, i, turn, place):
+    def left_copies(self, i, turn, place):
         at = pl.ds(pl.multiple_of(place * self.each, self.each), self.each)
-        return pltpu.make_async_copy(self.jobs[i][0].at[:, at], self.left.at[turn % 2], self.left_sems.at[turn % 2])
+        copies, first = [], 0
+        for k, source in enumerate(self.jobs[i][0]):
+            rows = pl.ds(first, source.shape[0])
+            copies.append(pltpu.make_async_copy(
+                source.at[:, at], self.left.at[turn % 2, rows], self.left_sems.at[turn % 2, k]))
+            first += source.shape[0]
+        return copies
 
     def product(self, i, turn, places, take):
         if turn == 0:
             if i == 0:
                 self.right_copy(0).start()
-                self.left_copy(0, 0, places[0]).start()
+                for copy in self.left_copies(0, 0, places[0]):
+                    copy.start()
             self.right_copy(i).wait()
             if i + 1 < len(self.jobs):
                 self.right_copy(i + 1).start()
         if turn + 1 < len(places):
-            self.left_copy(i, turn + 1, places[turn + 1]).start()
-        self.left_copy(i, turn, places[turn]).wait()
+            for copy in self.left_copies(i, turn + 1, places[turn + 1]):
+                copy.start()
+        for copy in self.left_copies(i, turn, places[turn]):
+            copy.wait()
         value = mm(self.left[turn % 2], self.right[i % 2], TN)
         if turn + 1 == len(places) and i + 1 < len(self.jobs):
-            self.left_copy(i + 1, 0, places[0]).start()
+            for copy in self.left_copies(i + 1, 0, places[0]):
+                copy.start()
         take(value)
 
 
-def norm_back_kernel(n, seqs, rows, piece, bits, n_uly, part_ref, cot_ref, mid_ref, gain_ref, a2_ref, cot_all_ref,
-                     dgate_ref, dup_ref, hidden_ref, out_ref, dmid_ref, dgain_ref, ggate_ref, gup_ref, gdown_ref,
+def norm_back_kernel(n, seqs, rows, piece, bits, n_uly, parts, part_ref, cot_ref, mid_ref, gain_ref, a2_ref, *refs):
+    cot_refs, refs = refs[:parts], refs[parts:]
+    norm_back_body(n, seqs, rows, piece, bits, n_uly, part_ref, cot_ref, mid_ref, gain_ref, a2_ref, cot_refs, *refs)
+
+
+def norm_back_body(n, seqs, rows, piece, bits, n_uly, part_ref, cot_ref, mid_ref, gain_ref, a2_ref, cot_refs,
+                   dgate_ref, dup_ref, hidden_ref, out_ref, dmid_ref, dgain_ref, ggate_ref, gup_ref, gdown_ref,
                      land_ref, rs_send, rs_recv, ag_send, ag_recv, left_slots, right_slots, left_sems, right_sems,
                      *plane_scratch):
     dgain_ref[...] = jnp.zeros_like(dgain_ref)
@@ -917,7 +982,7 @@
     jobs = [
         (left, right, half, out)
         for left, right, out in (
-            (a2_ref, dgate_ref, ggate_ref), (a2_ref, dup_ref, gup_ref), (cot_all_ref, hidden_ref, gdown_ref))
+            ((a2_ref,), dgate_ref, ggate_ref), ((a2_ref,), dup_ref, gup_ref), (cot_refs, hidden_ref, gdown_ref))
         for half in range(halves)
     ]
     streamed = StreamedOuter(jobs, ggate_ref.shape[0], left_slots, right_slots, left_sems, right_sems)
@@ -964,7 +1029,7 @@
                  beside, quiet)
 
 
-def norm_back(part, cotangent, middle, gain, a2, cot_all, d_gate, d_up, hidden, n, sizes, collective_id):
+def norm_back(part, cotangent, middle, gain, a2, cots, d_gate, d_up, hidden, n, sizes, collective_id):
     n_ctx, n_uly = sizes
     places = n_ctx * n_uly
     bits = places.bit_length() - 1
@@ -975,7 +1040,7 @@
         out, d_mid, dgain = line_call(
             plain_back_kernel, n, cotangent.shape, part, (cotangent, middle, gain[None]),
             (jax.ShapeDtypeStruct((1, width), f32),), collective_id, "norm_back")
-        grads = outer_sums((a2, cot_all), (0, 0, 1), (d_gate, d_up, hidden), sizes, 0)
+        grads = outer_sums((a2, jnp.concatenate(cots)), (0, 0, 1), (d_gate, d_up, hidden), sizes, 0)
         return (out, d_mid, dgain, *grads[:2], grads[2].T)
     piece = min(back_piece, rows)
     half = units // 2
@@ -987,14 +1052,14 @@
     ]
     plane_scratch = [PlaneSum.scratch(bits, each, half) for _ in range(6)]
     return pl.pallas_call(
-        functools.partial(norm_back_kernel, n, seqs, rows, piece, bits, n_uly),
-        in_specs=[vm] * 4 + [anywhere] * 5,
+        functools.partial(norm_back_kernel, n, seqs, rows, piece, bits, n_uly, len(cots)),
+        in_specs=[vm] * 4 + [anywhere] * (4 + len(cots)),
         out_specs=[vm] * len(shapes),
         out_shape=shapes,
         scratch_shapes=[
             *line_scratch(n, seqs, rows, piece, width),
             pltpu.VMEM((2, tokens, each), bf16), pltpu.VMEM((2, tokens, half), bf16),
-            pltpu.SemaphoreType.DMA((2,)), pltpu.SemaphoreType.DMA((2,)),
+            pltpu.SemaphoreType.DMA((2, len(cots))), pltpu.SemaphoreType.DMA((2,)),
             plane_scratch[0][0], plane_scratch[0][0], plane_scratch[0][0],
             *[item for scratch in plane_scratch for item in scratch[1:]],
         ],
@@ -1002,7 +1067,7 @@
             collective_id=collective_id, has_side_effects=True, vmem_limit_bytes=vmem_bytes),
         cost_estimate=cost(6 * tokens * units * width, 250_000_000),
         name="norm_back",
-    )(part, cotangent, middle, gain[None], a2, cot_all, d_gate, d_up, hidden)
+    )(part, cotangent, middle, gain[None], a2, *cots, d_gate, d_up, hidden)
 
 
 class StoredSum(PlaneSum):
@@ -1440,7 +1505,7 @@
     seqs, rows, width = x.shape
     dim = query_norm.shape[0]
     heads, kv_heads = w_query.shape[1] // dim, w_key.shape[1] // dim
-    piece = min(64, rows)
+    piece = min(32, rows)
     cut_count = rows // piece
     pieces = seqs * cut_count
     vm = pl.BlockSpec(memory_space=pltpu.VMEM)
@@ -1576,18 +1641,14 @@
     silu = gate * sig
     hidden = (silu * up).astype(bf16)
     made, cots = lax.optimization_barrier((wide(mm(hidden, w_down).astype(bf16)), cots))
-    outs = [collect(made[:near])]
-    cot = flatten(jnp.concatenate(cots, axis=0))
-    d_hidden = mm(cot, w_down, NT)
-    d_gate = (d_hidden * up * sig * (1.0 + gate * (1.0 - sig))).astype(bf16)
-    d_up = (d_hidden * silu).astype(bf16)
-    d_second = (mm(d_gate, w_gate, NT) + mm(d_up, w_up, NT)).astype(bf16)
+    cots = [flatten(c) for c in cots]
+    d_gate, d_up = hidden_back(cots, w_down, gate, up)
+    d_second = second_back(d_gate, d_up, w_gate, w_up)
     d_branch, d_mid, grad_mlp_norm, grad_gate, grad_up, grad_down = norm_back(
-        wide(d_second), cotangent, middle, mlp_norm, a2, cot, d_gate, d_up, hidden, n_tensor, sizes, 2)
-
-    if near < seqs:
-        late_made, d_branch = lax.optimization_barrier((made[near:], d_branch))
-        outs.append(collect(late_made))
+        wide(d_second), cotangent, middle, mlp_norm, a2, cots, d_gate, d_up, hidden, n_tensor, sizes, 2)
+
+    made, d_branch = lax.optimization_barrier((made, d_branch))
+    outs = [collect(made)]
     d_gated = wide(mm(flatten(d_branch), w_output, NT).astype(bf16))
     d_q, d_logit, d_kv, d_qgain, grad_gate, grad_up, grad_down = attend_back(
         q, kv, d_gated, att, logits, logits.transpose(0, 2, 1), lse, bounds, start[:, None, :], positions[None, :], nq,

time: 675 us -> 664 us (0.984)
  matrix products: 79.8 us -> 44.1 us
  Pallas kernels: 515 us -> 546 us
    dot_general x8 -> x5, matrix products: 79.8 us -> 44.1 us  [mm(): return lax.dot_general(left, right, dims, preferred_element_type=f32)]
    pallas_call x0 -> x2, Pallas kernels: none -> 34.5 us  [the longest x1 19 us: second_back(): pl.pallas_call(second_back_kernel, grid=(width // block,), in_specs=[full...]
  transfers between devices with their start and end apart: 4 -> 3, of which waited for: 2 -> 2; matrix products, arithmetic and copies ran while one was open for 13% -> 8% of each run, Pallas kernels for 45% -> 27%
where the time goes in v4:
time: 664 us; the launch traced here: 655 us
  Pallas kernels  546 us (82%)
  matrix products  44.1 us (7%)
  waiting for transfers between devices  33.4 us (5%)
  between operations  14.2 us (2%)
  local copies, waits for them, and re-layouts  10.9 us (2%)
    pallas_call x1, Pallas kernels, layer_back(): pl.pallas_call(functools.partial(layer_back_kernel, n, bits, n_uly, heads...  143 us
    pallas_call x1, Pallas kernels, norm_back(): pl.pallas_call(functools.partial(norm_back_kernel, n, seqs, rows, piece,...  122 us
    pallas_call x1, Pallas kernels, line_call(): pl.pallas_call(functools.partial(kernel, n, seqs, rows, piece), in_specs=...  112 us
    pallas_call x1, Pallas kernels, layer_front(): pl.pallas_call(functools.partial(layer_front_kernel, n, bits, n_uly, head...  96.8 us
    dot_general x5, matrix products, mm(): return lax.dot_general(left, right, dims, preferred_element_type=f32)  44.1 us
    all_gather x2, waiting for transfers between devices, spread(): return lax.all_gather(values.astype(bf16), 'tp', axis=1, tiled=True)  33.3 us
    pallas_call x1, Pallas kernels, attend_back(): pl.pallas_call(functools.partial(attend_back_kernel, heads, kv_heads, dim...  19.9 us
    pallas_call x1, Pallas kernels, second_back(): pl.pallas_call(second_back_kernel, grid=(width // block,), in_specs=[full...  19 us
  transfers between devices with their start and end apart: 3, of which 2 were waited for; matrix products, arithmetic and copies ran while one was open for 8% of the time, Pallas kernels for 27%

profile of v4, /device:TPU:0, one launch (start us, length us, event | category | flops | bytes accessed | tf_op | source)
XLA Modules:
  0.0 654.7 jit_solution(6447690872265376187)
XLA Ops:
  7.3 1.0 fusion
  8.3 0.8 pad_maximum_fusion.cos_ref
  9.1 0.8 pad_maximum_fusion.1.sin_ref
  10.0 2.3 fusion.7
  12.2 96.8 %layer_front.1 = (bf16[2,4,4,32,2048]{4,3,2,1,0:T(8,128)(2,1)}, bf16[2,4,4,32,512]{4,3,2,1,0:T(8,128)(2,1)}, bf16[2,32,4,32,512]{4,3,2,1,0:T(8,128)(2,1)}, bf16[...) custom-call(bf16[2,128,2048]{2,1,0:T(8,128)(2,1)} %x_ref.5, ...), custom_call_target="tpu_custom_call" | custom-call | flops 4294967296 | bytes 200000000 | tf_op jit(solution)/shard_map/layer_front/pallas_call | solution.py:1523
  110.2 1.0 copy.38.start_ref
  112.6 12.1 %attend.1 = (bf16[2,512,512]{2,1,0:T(8,128)(2,1)}, bf16[2,512,512]{2,1,0:T(8,128)(2,1)}, f32[2,4,512]{2,1,0:T(4,128)}) custom-call(s32[2,4]{1,0:T(2,128)} %pad_add_fusion.bounds_ref, bf16[2,512,512]{2,1,0:T(8,128)(2,1)} %bitcast.93, bf16[2,4096,512]{2,1,0:T(8,128)(2,1)} %bitcast.86, s32[2,512,1]{2,1,0:T(8,128)} %copy.38.start_ref, ...), custom_call_target="tpu_custom_call" | custom-call | flops 4294967296 | bytes 11534336 | tf_op jit(solution)/shard_map/attend/pallas_call | solution.py:171
  124.7 5.6 convolution_convert_fusion.1
  130.3 23.0 %all-gather.3.cloned.1.call-done = bf16[1,512,2048]{2,1,0:T(8,128)(2,1)} async-done(((bf16[1,128,2048]{2,1,0:T(8,128)(2,1)}), bf16[1,512,2048]{2,1,0:T(8,128)(2,1)}) %all-gather.3.cloned.1.call-update) | async-done | bytes 2097168 | tf_op jit(solution)/shard_map/all_gather | solution.py:1569
  153.3 111.9 %norm_forward.1 = (bf16[2,512,2048]{2,1,0:T(8,128)(2,1)}, f32[2,128,2048]{2,1,0:T(8,128)}) custom-call(bf16[2,512,2048]{2,1,0:T(8,128)(2,1)} %bitcast.51, bf16[2,128,2048]{2,1,0:T(8,128)(2,1)} %x_ref.5, f32[1,2048]{1,0:T(1,128)} %bitcast.63), custom_call_target="tpu_custom_call" | custom-call | flops 41943040 | bytes 100000000 | tf_op jit(solution)/shard_map/norm_forward/pallas_call | solution.py:619
  265.4 10.8 %fusion.8.refs_3_ = f32[1024,1536]{1,0:T(8,128)S(1)} fusion(bf16[1024,2048]{1,0:T(8,128)(2,1)} %bitcast.70, bf16[2048,1536]{1,0:T(8,128)(2,1)} %wgate_ref.1), kind=kOutput, calls=%fused_computation.42 | convolution fusion | flops 6442450944 | bytes 16777216 | tf_op jit(solution)/shard_map/dot_general | solution.py:29
  276.3 13.3 %multiply_convert_fusion = (bf16[1024,1536]{1,0:T(8,128)(2,1)S(1)}, f32[1024,1536]{1,0:T(8,128)}) fusion(f32[1024,1536]{1,0:T(8,128)S(1)} %fusion.8.refs_3_, bf16[1024,2048]{1,0:T(8,128)(2,1)S(1)} %bitcast.72, bf16[2048,1536]{1,0:T(8,128)(2,1)} %wup_ref.1), kind=kOutput, calls=%fused_computation | convolution fusion | flops 6451888128 | bytes 26214400 | tf_op jit(solution)/shard_map/dot_general | solution.py:29
  289.6 1.8 copy-done.9
  291.4 8.2 %convolution_convert_fusion = bf16[1024,2048]{1,0:T(8,128)(2,1)} fusion(bf16[1024,1536]{1,0:T(8,128)(2,1)S(1)} %get-tuple-element.145.refs_4_, bf16[1536,2048]{1,0:T(8,128)(2,1)S(1)} %bitcast.69), kind=kOutput, calls=%fused_computation.1 | convolution fusion | flops 6444548096 | bytes 13631488 | tf_op jit(solution)/shard_map/dot_general | solution.py:29
  299.6 10.4 %all-gather.5.cloned.1.call-done = bf16[1,512,2048]{2,1,0:T(8,128)(2,1)} async-done(((bf16[1,128,2048]{2,1,0:T(8,128)(2,1)}), bf16[1,512,2048]{2,1,0:T(8,128)(2,1)}) %all-gather.5.cloned.1.call-update) | async-done | bytes 2097168 | tf_op jit(solution)/shard_map/all_gather | solution.py:1569
  310.0 15.5 %hidden_back.1 = (bf16[1024,1536]{1,0:T(8,128)(2,1)}, bf16[1024,1536]{1,0:T(8,128)(2,1)}) custom-call(bf16[512,2048]{1,0:T(8,128)(2,1)} %bitcast.73, bf16[512,2048]{1,0:T(8,128)(2,1)} %bitcast.75, bf16[1536,2048]{1,0:T(8,128)(2,1)} %refs_2_.1, f32[1024,1536]{1,0:T(8,128)} %copy-done.8, f32[1024,1536]{1,0:T(8,128)} %get-tuple-element.146.refs_4_), custom_call_target="tpu_custom_call" | custom-call | flops 6442450944 | bytes 40000000 | tf_op jit(solution)/shard_map/hidden_back/pallas_call | solution.py:397
  325.5 19.0 %second_back.1 = bf16[1024,2048]{1,0:T(8,128)(2,1)} custom-call(bf16[1024,1536]{1,0:T(8,128)(2,1)} %get-tuple-element.88.dgate_ref.refs_2_, bf16[1024,1536]{1,0:T(8,128)(2,1)} %get-tuple-element.89.dup_ref.refs_3_, bf16[2048,1536]{1,0:T(8,128)(2,1)} %wgate_ref.1, bf16[2048,1536]{1,0:T(8,128)(2,1)} %wup_ref.1), custom_call_target="tpu_custom_call" | custom-call | flops 12884901888 | bytes 30000000 | tf_op jit(solution)/shard_map/second_back/pallas_call | solution.py:418
  344.5 121.5 %norm_back.1 = (bf16[2,512,2048]{2,1,0:T(8,128)(2,1)}, f32[2,128,2048]{2,1,0:T(8,128)}, f32[1,2048]{1,0:T(1,128)}, f32[256,1536]{1,0:T(8,128)}, f32[256,1536]{1,0:T(8,128)}, /*index=5*/f32[1536,256]{1,0:T(8,128)}) custom-call(bf16[2,512,2048]{2,1,0:T(8,128)(2,1)} %bitcast.92, bf16[2,128,2048]{2,1,0:T(8,128)(2,1)} %cot_ref.1, ...), custom_call_target="tpu_custom_call" | custom-call | flops 19327352832 | bytes 250000000 | tf_op jit(solution)/shard_map/norm_back/pallas_call | solution.py:1054
  466.1 1.0 copy-done.1
  467.1 0.8 copy.42
  469.1 6.1 convolution_convert_fusion.2
  475.2 19.9 %attend_back.1 = (bf16[2,512,512]{2,1,0:T(8,128)(2,1)}, f32[2,4,512]{2,1,0:T(4,128)}, bf16[2,4096,512]{2,1,0:T(8,128)(2,1)}, f32[1,128]{1,0:T(1,128)}, f32[256,1...) custom-call(s32[2,4]{1,0:T(2,128)} %pad_add_fusion.bounds_ref, bf16[2,512,512]{2,1,0:T(8,128)(2,1)} %bitcast.94, ...), custom_call_target="tpu_custom_call" | custom-call | flops 10737418240 | bytes 22020096 | tf_op jit(solution)/shard_map/attend_back/pallas_call | solution.py:303
  496.9 143.5 %layer_back.1 = (f32[2,128,2048]{2,1,0:T(8,128)}, f32[256,512]{1,0:T(8,128)}, f32[256,256]{1,0:T(8,128)}, f32[256,256]{1,0:T(8,128)}, f32[4,256]{1,0:T(4,128)}, ...) custom-call(bf16[2,32,2,64,512]{4,3,2,1,0:T(8,128)(2,1)} %bitcast.88, ...), custom_call_target="tpu_custom_call" | custom-call | flops 9663676416 | bytes 250000000 | tf_op jit(solution)/shard_map/layer_back/pallas_call | solution.py:1354
  640.4 5.4 finish.1
  (50 shorter events, 8.0 us)
Async XLA Ops:
  7.2 117.5 %copy-start = (bf16[512,2048]{1,0:T(8,128)(2,1)S(1)}, bf16[512,2048]{1,0:T(8,128)(2,1)}, u32[]{:S(2)}) copy-start(bf16[512,2048]{1,0:T(8,128)(2,1)} %param.24) | copy-start | bytes 6291460
  7.2 146.1 %all-gather.3.cloned.1.call-start = ((), (), s32[]{:S(2)}) async-start(), calls=%async_computation.1 | async-start | bytes 2621440 | tf_op jit(solution)/shard_map/all_gather | solution.py:1569
  12.2 97.3 %copy-start.2 = (s32[2,4096]{1,0:T(2,128)S(1)}, s32[2,4096]{1,0:T(2,128)}, u32[]{:S(2)}) copy-start(s32[2,4096]{1,0:T(2,128)} %param.16) | copy-start | bytes 98308
  109.0 201.0 %all-gather.5.cloned.1.call-start = ((), (), s32[]{:S(2)}) async-start(), calls=%async_computation.2 | async-start | bytes 2621440 | tf_op jit(solution)/shard_map/all_gather | solution.py:1569
  265.2 375.2 %reduce-scatter.2.cloned.1.call-start = ((), (), s32[]{:S(2)}) async-start(), calls=%async_computation.3 | async-start | bytes 5242880 | tf_op jit(solution)/shard_map/reduce_scatter | solution.py:1573
  265.4 10.8 %copy-start.5 = (bf16[2,512,2048]{2,1,0:T(8,128)(2,1)S(1)}, bf16[2,512,2048]{2,1,0:T(8,128)(2,1)}, u32[]{:S(2)}) copy-start(bf16[2,512,2048]{2,1,0:T(8,128)(2,1)} %get-tuple-element.82) | copy-start | bytes 12582916
  265.4 26.0 %slice-start = ((s8[6291456]{0:T(1024)(128)(4,1)}), s8[4194304]{0:T(1024)(128)(4,1)S(1)}, s32[]{:S(2)}) async-start(s8[6291456]{0:T(1024)(128)(4,1)} %bitcast.68), calls=%async_computation.4 | async-start | bytes 8388608
  276.2 13.4 %copy-start.8 = (f32[1024,1536]{1,0:T(8,128)}, f32[1024,1536]{1,0:T(8,128)S(1)}, u32[]{:S(2)}) copy-start(f32[1024,1536]{1,0:T(8,128)S(1)} %fusion.8.refs_3_) | copy-start | bytes 18874372
  276.3 15.2 %slice-start.1 = ((s8[6291456]{0:T(1024)(128)(4,1)}), s8[2097152]{0:T(1024)(128)(4,1)S(1)}, s32[]{:S(2)}) async-start(s8[6291456]{0:T(1024)(128)(4,1)} %bitcast.68), calls=%async_computation.5 | async-start | bytes 4194304
  289.6 1.8 copy-start.9
  466.1 1.0 copy-start.1
  640.3 5.4 copy-start.4
  640.4 6.0 copy-start.7
  640.4 6.5 copy-start.6
  640.4 7.0 %copy-start.3 = (f32[1,2048]{1,0:T(1,128)S(1)}, f32[1,2048]{1,0:T(1,128)}, u32[]{:S(2)}) copy-start(f32[1,2048]{1,0:T(1,128)} %get-tuple-element.126) | copy-start | bytes 24580
Sparse Core Ops, SparseCore 0:
  109.1 44.0 all-gather.2
  265.3 44.6 all-gather.4
  466.2 75.2 reduce-scatter.1

commit v5 on v4

--- a/solution.py
+++ b/solution.py
@@ -564,13 +564,15 @@
                     def _():
                         self.spread_copy(way, k, s, owner).wait_send()
 
-    def run(self, beside=(), quiet=(0, 0)):
+    def run(self, beside=(), quiet=(0, 0), after=None):
         beside, done = list(beside), 0
         steps = self.pieces + len(self.stages) - 1
         turns = [(step, s) for step in range(steps) for s in range(self.pieces) if 0 <= step - s < len(self.stages)]
         slots = [i for i, (step, _) in enumerate(turns) if quiet[0] <= step < steps - quiet[1]]
         for i, (step, s) in enumerate(turns):
             self.stages[step - s](s)
+            if after and step - s == len(self.stages) - 1:
+                after(s)
             if i in slots:
                 until = len(beside) * (slots.index(i) + 1) // len(slots)
                 for item in beside[done:until]:
@@ -580,7 +582,8 @@
         self.drain_spread()
 
 
-def line_all_sum(n, seqs, rows, piece, finish, part_ref, out_ref, land_ref, sems, beside=(), quiet=(0, 0)):
+def line_all_sum(n, seqs, rows, piece, finish, part_ref, out_ref, land_ref, sems, beside=(), quiet=(0, 0),
+                 after=None):
     cuts = [(q, c) for q in range(seqs) for c in range(rows // piece)]
 
     def at(ref):
@@ -588,7 +591,7 @@
             cuts[s][0], pl.ds(pl.multiple_of(owner * rows + cuts[s][1] * piece, piece), piece)]
 
     LineSum(n, len(cuts), at(part_ref), lambda s, total: finish(*cuts[s], total), land_ref, sems, at(out_ref)).run(
-        beside, quiet)
+        beside, quiet, after and (lambda s: after(*cuts[s])))
 
 
 def line_scratch(n, seqs, rows, piece, width):
@@ -965,13 +968,14 @@
         take(value)
 
 
-def norm_back_kernel(n, seqs, rows, piece, bits, n_uly, parts, part_ref, cot_ref, mid_ref, gain_ref, a2_ref, *refs):
+def norm_back_kernel(n, seqs, rows, piece, bits, n_uly, parts, part_ref, cot_ref, mid_ref, gain_ref, wo_ref, a2_ref, *refs):
     cot_refs, refs = refs[:parts], refs[parts:]
-    norm_back_body(n, seqs, rows, piece, bits, n_uly, part_ref, cot_ref, mid_ref, gain_ref, a2_ref, cot_refs, *refs)
-
-
-def norm_back_body(n, seqs, rows, piece, bits, n_uly, part_ref, cot_ref, mid_ref, gain_ref, a2_ref, cot_refs,
-                   dgate_ref, dup_ref, hidden_ref, out_ref, dmid_ref, dgain_ref, ggate_ref, gup_ref, gdown_ref,
+    norm_back_body(n, seqs, rows, piece, bits, n_uly, part_ref, cot_ref, mid_ref, gain_ref, wo_ref, a2_ref, cot_refs,
+                   *refs)
+
+
+def norm_back_body(n, seqs, rows, piece, bits, n_uly, part_ref, cot_ref, mid_ref, gain_ref, wo_ref, a2_ref, cot_refs,
+                   dgate_ref, dup_ref, hidden_ref, out_ref, dmid_ref, dgain_ref, ggate_ref, gup_ref, gdown_ref, dgated_ref,
                      land_ref, rs_send, rs_recv, ag_send, ag_recv, left_slots, right_slots, left_sems, right_sems,
                      *plane_scratch):
     dgain_ref[...] = jnp.zeros_like(dgain_ref)
@@ -1002,6 +1006,13 @@
 
     order = list(range(1, 1 << bits, 2)) + list(range(0, 1 << bits, 2))
     quiet = back_quiet
+
+    def branch(q, c):
+        spots = [slice(t * rows + c * piece, t * rows + (c + 1) * piece) for t in range(n)]
+        value = mm(jnp.concatenate([out_ref[q, at] for at in spots], axis=0), wo_ref[...], NT).astype(bf16)
+        for t, at in enumerate(spots):
+            dgated_ref[q, at] = value[t * piece:(t + 1) * piece]
+
     beside = []
 
     def product(i, turn):
@@ -1026,10 +1037,10 @@
 
     line_and_plane_barrier(n, lax.axis_index("tp"), bits, n_uly)
     line_all_sum(n, seqs, rows, piece, finish, part_ref, out_ref, land_ref, (rs_send, rs_recv, ag_send, ag_recv),
-                 beside, quiet)
-
-
-def norm_back(part, cotangent, middle, gain, a2, cots, d_gate, d_up, hidden, n, sizes, collective_id):
+                 beside, quiet, branch)
+
+
+def norm_back(part, cotangent, middle, gain, w_output, a2, cots, d_gate, d_up, hidden, n, sizes, collective_id):
     n_ctx, n_uly = sizes
     places = n_ctx * n_uly
     bits = places.bit_length() - 1
@@ -1041,19 +1052,20 @@
             plain_back_kernel, n, cotangent.shape, part, (cotangent, middle, gain[None]),
             (jax.ShapeDtypeStruct((1, width), f32),), collective_id, "norm_back")
         grads = outer_sums((a2, jnp.concatenate(cots)), (0, 0, 1), (d_gate, d_up, hidden), sizes, 0)
-        return (out, d_mid, dgain, *grads[:2], grads[2].T)
+        d_gated = mm(flatten(out), w_output, NT).astype(bf16).reshape(*part.shape[:2], -1)
+        return (out, d_mid, dgain, *grads[:2], grads[2].T, d_gated)
     piece = min(back_piece, rows)
     half = units // 2
     vm, anywhere = pl.BlockSpec(memory_space=pltpu.VMEM), pl.BlockSpec(memory_space=pl.ANY)
     shapes = [
         jax.ShapeDtypeStruct(part.shape, bf16), jax.ShapeDtypeStruct(cotangent.shape, f32),
         jax.ShapeDtypeStruct((1, width), f32), *[jax.ShapeDtypeStruct((each, units), f32)] * 2,
-        jax.ShapeDtypeStruct((units, each), f32),
+        jax.ShapeDtypeStruct((units, each), f32), jax.ShapeDtypeStruct((*part.shape[:2], w_output.shape[0]), bf16),
     ]
     plane_scratch = [PlaneSum.scratch(bits, each, half) for _ in range(6)]
     return pl.pallas_call(
         functools.partial(norm_back_kernel, n, seqs, rows, piece, bits, n_uly, len(cots)),
-        in_specs=[vm] * 4 + [anywhere] * (4 + len(cots)),
+        in_specs=[vm] * 5 + [anywhere] * (4 + len(cots)),
         out_specs=[vm] * len(shapes),
         out_shape=shapes,
         scratch_shapes=[
@@ -1067,7 +1079,7 @@
             collective_id=collective_id, has_side_effects=True, vmem_limit_bytes=vmem_bytes),
         cost_estimate=cost(6 * tokens * units * width, 250_000_000),
         name="norm_back",
-    )(part, cotangent, middle, gain[None], a2, *cots, d_gate, d_up, hidden)
+    )(part, cotangent, middle, gain[None], w_output, a2, *cots, d_gate, d_up, hidden)
 
 
 class StoredSum(PlaneSum):
@@ -1644,12 +1656,11 @@
     cots = [flatten(c) for c in cots]
     d_gate, d_up = hidden_back(cots, w_down, gate, up)
     d_second = second_back(d_gate, d_up, w_gate, w_up)
-    d_branch, d_mid, grad_mlp_norm, grad_gate, grad_up, grad_down = norm_back(
-        wide(d_second), cotangent, middle, mlp_norm, a2, cots, d_gate, d_up, hidden, n_tensor, sizes, 2)
+    d_branch, d_mid, grad_mlp_norm, grad_gate, grad_up, grad_down, d_gated = norm_back(
+        wide(d_second), cotangent, middle, mlp_norm, w_output, a2, cots, d_gate, d_up, hidden, n_tensor, sizes, 2)
 
     made, d_branch = lax.optimization_barrier((made, d_branch))
     outs = [collect(made)]
-    d_gated = wide(mm(flatten(d_branch), w_output, NT).astype(bf16))
     d_q, d_logit, d_kv, d_qgain, grad_gate, grad_up, grad_down = attend_back(
         q, kv, d_gated, att, logits, logits.transpose(0, 2, 1), lse, bounds, start[:, None, :], positions[None, :], nq,
         rq, tables, query_norm, (grad_gate, grad_up, grad_down), heads, kv_heads, dim, block, scale)
@@ -1658,10 +1669,10 @@
         grad_inputs, *grads = layer_back(
             d_kv, flatten(first), flatten(d_branch), d_q, d_logit, nk, rk, tables, key_norm,
             (w_query, w_key, w_value, w_headgate.T), flatten(gated), inputs, attn_norm, d_mid, d_qgain, grad_mlp_norm, n_tensor, sizes, heads, kv_heads, 3)
-        (grad_inputs, grad_query, grad_key, grad_value, grad_headgate, grad_output), outputs = finish(
-            (grad_inputs, *grads[:5]), middle, outs)
+        (grad_inputs, grad_query, grad_key, grad_value, grad_headgate, grad_output, *gains), outputs = finish(
+            (grad_inputs, *grads), middle, outs)
         grad_headgate = grad_headgate.T
-        grad_attn_norm, grad_mlp_norm, grad_query_norm, grad_key_norm = (g[0] for g in grads[5:])
+        grad_attn_norm, grad_mlp_norm, grad_query_norm, grad_key_norm = (g[0] for g in gains)
     else:
         outputs = (middle + jnp.concatenate(outs, axis=0).astype(f32)).astype(bf16)
         d_kv = blocks_sum(d_kv, sizes, 3)

time: 664 us -> 659 us (level)
    dot_general x5 -> x4, matrix products: 44.1 us -> 38 us  [mm(): return lax.dot_general(left, right, dims, preferred_element_type=f32)]
  transfers between devices with their start and end apart: 3 -> 3, of which waited for: 2 -> 2; matrix products, arithmetic and copies ran while one was open for 8% -> 7% of each run, Pallas kernels for 27% -> 27%
where the time goes in v5:
time: 659 us; the launch traced here: 650 us
  Pallas kernels  549 us (83%)
  matrix products  38 us (6%)
  waiting for transfers between devices  33.4 us (5%)
  between operations  14.1 us (2%)
  local copies, waits for them, and re-layouts  8.58 us (1%)
    pallas_call x1, Pallas kernels, layer_back(): pl.pallas_call(functools.partial(layer_back_kernel, n, bits, n_uly, heads...  143 us
    pallas_call x1, Pallas kernels, norm_back(): pl.pallas_call(functools.partial(norm_back_kernel, n, seqs, rows, piece,...  125 us
    pallas_call x1, Pallas kernels, line_call(): pl.pallas_call(functools.partial(kernel, n, seqs, rows, piece), in_specs=...  112 us
    pallas_call x1, Pallas kernels, layer_front(): pl.pallas_call(functools.partial(layer_front_kernel, n, bits, n_uly, head...  96.7 us
    dot_general x4, matrix products, mm(): return lax.dot_general(left, right, dims, preferred_element_type=f32)  38 us
    all_gather x2, waiting for transfers between devices, spread(): return lax.all_gather(values.astype(bf16), 'tp', axis=1, tiled=True)  33.3 us
    pallas_call x1, Pallas kernels, attend_back(): pl.pallas_call(functools.partial(attend_back_kernel, heads, kv_heads, dim...  20.3 us
    pallas_call x1, Pallas kernels, second_back(): pl.pallas_call(second_back_kernel, grid=(width // block,), in_specs=[full...  19 us
  transfers between devices with their start and end apart: 3, of which 2 were waited for; matrix products, arithmetic and copies ran while one was open for 7% of the time, Pallas kernels for 27%

profile of v5, /device:TPU:0, one launch (start us, length us, event | category | flops | bytes accessed | tf_op | source)
XLA Modules:
  0.0 649.6 jit_solution(1395428752621068526)
XLA Ops:
  7.3 1.0 fusion
  8.3 0.8 pad_maximum_fusion.cos_ref
  9.1 0.8 pad_maximum_fusion.1.sin_ref
  9.9 2.3 fusion.7
  12.2 96.7 %layer_front.1 = (bf16[2,4,4,32,2048]{4,3,2,1,0:T(8,128)(2,1)}, bf16[2,4,4,32,512]{4,3,2,1,0:T(8,128)(2,1)}, bf16[2,32,4,32,512]{4,3,2,1,0:T(8,128)(2,1)}, bf16[...) custom-call(bf16[2,128,2048]{2,1,0:T(8,128)(2,1)} %x_ref.5, ...), custom_call_target="tpu_custom_call" | custom-call | flops 4294967296 | bytes 200000000 | tf_op jit(solution)/shard_map/layer_front/pallas_call | solution.py:1535
  110.1 1.0 copy.38.start_ref
  112.6 12.2 %attend.1 = (bf16[2,512,512]{2,1,0:T(8,128)(2,1)}, bf16[2,512,512]{2,1,0:T(8,128)(2,1)}, f32[2,4,512]{2,1,0:T(4,128)}) custom-call(s32[2,4]{1,0:T(2,128)} %pad_add_fusion.bounds_ref, bf16[2,512,512]{2,1,0:T(8,128)(2,1)} %bitcast.91, bf16[2,4096,512]{2,1,0:T(8,128)(2,1)} %bitcast.85, s32[2,512,1]{2,1,0:T(8,128)} %copy.38.start_ref, ...), custom_call_target="tpu_custom_call" | custom-call | flops 4294967296 | bytes 11534336 | tf_op jit(solution)/shard_map/attend/pallas_call | solution.py:171
  124.8 5.6 convolution_convert_fusion.1
  130.4 22.8 %all-gather.3.cloned.1.call-done = bf16[1,512,2048]{2,1,0:T(8,128)(2,1)} async-done(((bf16[1,128,2048]{2,1,0:T(8,128)(2,1)}), bf16[1,512,2048]{2,1,0:T(8,128)(2,1)}) %all-gather.3.cloned.1.call-update) | async-done | bytes 2097168 | tf_op jit(solution)/shard_map/all_gather | solution.py:1581
  153.2 111.9 %norm_forward.1 = (bf16[2,512,2048]{2,1,0:T(8,128)(2,1)}, f32[2,128,2048]{2,1,0:T(8,128)}) custom-call(bf16[2,512,2048]{2,1,0:T(8,128)(2,1)} %bitcast.48, bf16[2,128,2048]{2,1,0:T(8,128)(2,1)} %x_ref.5, f32[1,2048]{1,0:T(1,128)} %bitcast.60), custom_call_target="tpu_custom_call" | custom-call | flops 41943040 | bytes 100000000 | tf_op jit(solution)/shard_map/norm_forward/pallas_call | solution.py:622
  265.4 10.8 %fusion.8.refs_3_ = f32[1024,1536]{1,0:T(8,128)S(1)} fusion(bf16[1024,2048]{1,0:T(8,128)(2,1)} %bitcast.65, bf16[2048,1536]{1,0:T(8,128)(2,1)} %wgate_ref.1), kind=kOutput, calls=%fused_computation.41 | convolution fusion | flops 6442450944 | bytes 16777216 | tf_op jit(solution)/shard_map/dot_general | solution.py:29
  276.2 13.3 %multiply_convert_fusion = (bf16[1024,1536]{1,0:T(8,128)(2,1)S(1)}, f32[1024,1536]{1,0:T(8,128)}) fusion(f32[1024,1536]{1,0:T(8,128)S(1)} %fusion.8.refs_3_, bf16[1024,2048]{1,0:T(8,128)(2,1)S(1)} %bitcast.67, bf16[2048,1536]{1,0:T(8,128)(2,1)} %wup_ref.1), kind=kOutput, calls=%fused_computation | convolution fusion | flops 6451888128 | bytes 26214400 | tf_op jit(solution)/shard_map/dot_general | solution.py:29
  289.5 1.7 copy-done.5
  291.2 8.2 %convolution_convert_fusion = bf16[1024,2048]{1,0:T(8,128)(2,1)} fusion(bf16[1024,1536]{1,0:T(8,128)(2,1)S(1)} %get-tuple-element.155.refs_4_, bf16[1536,2048]{1,0:T(8,128)(2,1)S(1)} %bitcast.64), kind=kOutput, calls=%fused_computation.1 | convolution fusion | flops 6444548096 | bytes 13631488 | tf_op jit(solution)/shard_map/dot_general | solution.py:29
  299.4 10.5 %all-gather.5.cloned.1.call-done = bf16[1,512,2048]{2,1,0:T(8,128)(2,1)} async-done(((bf16[1,128,2048]{2,1,0:T(8,128)(2,1)}), bf16[1,512,2048]{2,1,0:T(8,128)(2,1)}) %all-gather.5.cloned.1.call-update) | async-done | bytes 2097168 | tf_op jit(solution)/shard_map/all_gather | solution.py:1581
  309.9 15.5 %hidden_back.1 = (bf16[1024,1536]{1,0:T(8,128)(2,1)}, bf16[1024,1536]{1,0:T(8,128)(2,1)}) custom-call(bf16[512,2048]{1,0:T(8,128)(2,1)} %bitcast.68, bf16[512,2048]{1,0:T(8,128)(2,1)} %bitcast.70, bf16[1536,2048]{1,0:T(8,128)(2,1)} %refs_2_.1, f32[1024,1536]{1,0:T(8,128)} %copy-done.4, f32[1024,1536]{1,0:T(8,128)} %get-tuple-element.156.refs_4_), custom_call_target="tpu_custom_call" | custom-call | flops 6442450944 | bytes 40000000 | tf_op jit(solution)/shard_map/hidden_back/pallas_call | solution.py:397
  325.4 19.0 %second_back.1 = bf16[1024,2048]{1,0:T(8,128)(2,1)} custom-call(bf16[1024,1536]{1,0:T(8,128)(2,1)} %get-tuple-element.92.dgate_ref.refs_2_, bf16[1024,1536]{1,0:T(8,128)(2,1)} %get-tuple-element.93.dup_ref.refs_3_, bf16[2048,1536]{1,0:T(8,128)(2,1)} %wgate_ref.1, bf16[2048,1536]{1,0:T(8,128)(2,1)} %wup_ref.1), custom_call_target="tpu_custom_call" | custom-call | flops 12884901888 | bytes 30000000 | tf_op jit(solution)/shard_map/second_back/pallas_call | solution.py:418
  344.4 125.0 %norm_back.1 = (bf16[2,512,2048]{2,1,0:T(8,128)(2,1)}, f32[2,128,2048]{2,1,0:T(8,128)}, f32[1,2048]{1,0:T(1,128)}, f32[256,1536]{1,0:T(8,128)}, f32[256,1536]{1,...) custom-call(bf16[2,512,2048]{2,1,0:T(8,128)(2,1)} %bitcast.90, bf16[2,128,2048]{2,1,0:T(8,128)(2,1)} %cot_ref.1, ...), custom_call_target="tpu_custom_call" | custom-call | flops 19327352832 | bytes 250000000 | tf_op jit(solution)/shard_map/norm_back/pallas_call | solution.py:1066
  469.5 1.0 copy-done
  470.5 0.8 copy.42
  472.4 20.3 %attend_back.1 = (bf16[2,512,512]{2,1,0:T(8,128)(2,1)}, f32[2,4,512]{2,1,0:T(4,128)}, bf16[2,4096,512]{2,1,0:T(8,128)(2,1)}, f32[1,128]{1,0:T(1,128)}, f32[256,1...) custom-call(s32[2,4]{1,0:T(2,128)} %pad_add_fusion.bounds_ref, bf16[2,512,512]{2,1,0:T(8,128)(2,1)} %bitcast.92, ...), custom_call_target="tpu_custom_call" | custom-call | flops 10737418240 | bytes 22020096 | tf_op jit(solution)/shard_map/attend_back/pallas_call | solution.py:303
  493.6 0.8 pad.4.clone
  494.4 143.1 %layer_back.1 = (f32[2,128,2048]{2,1,0:T(8,128)}, f32[256,512]{1,0:T(8,128)}, f32[256,256]{1,0:T(8,128)}, f32[256,256]{1,0:T(8,128)}, f32[4,256]{1,0:T(4,128)}, ...) custom-call(bf16[2,32,2,64,512]{4,3,2,1,0:T(8,128)(2,1)} %bitcast.87, ...), custom_call_target="tpu_custom_call" | custom-call | flops 9663676416 | bytes 250000000 | tf_op jit(solution)/shard_map/layer_back/pallas_call | solution.py:1366
  637.5 5.4 finish.1
  (37 shorter events, 5.0 us)
Async XLA Ops:
  7.2 146.1 %all-gather.3.cloned.1.call-start = ((), (), s32[]{:S(2)}) async-start(), calls=%async_computation.1 | async-start | bytes 2621440 | tf_op jit(solution)/shard_map/all_gather | solution.py:1581
  12.2 97.3 %copy-start.1 = (s32[2,4096]{1,0:T(2,128)S(1)}, s32[2,4096]{1,0:T(2,128)}, u32[]{:S(2)}) copy-start(s32[2,4096]{1,0:T(2,128)} %param.16) | copy-start | bytes 98308
  109.0 200.9 %all-gather.5.cloned.1.call-start = ((), (), s32[]{:S(2)}) async-start(), calls=%async_computation.2 | async-start | bytes 2621440 | tf_op jit(solution)/shard_map/all_gather | solution.py:1581
  112.6 12.2 %copy-start.3 = (bf16[512,2048]{1,0:T(8,128)(2,1)S(1)}, bf16[512,2048]{1,0:T(8,128)(2,1)}, u32[]{:S(2)}) copy-start(bf16[512,2048]{1,0:T(8,128)(2,1)} %wo_ref.1) | copy-start | bytes 6291460
  265.1 372.4 %reduce-scatter.2.cloned.1.call-start = ((), (), s32[]{:S(2)}) async-start(), calls=%async_computation.3 | async-start | bytes 5242880 | tf_op jit(solution)/shard_map/reduce_scatter | solution.py:1585
  265.4 10.8 %copy-start.2 = (bf16[2,512,2048]{2,1,0:T(8,128)(2,1)S(1)}, bf16[2,512,2048]{2,1,0:T(8,128)(2,1)}, u32[]{:S(2)}) copy-start(bf16[2,512,2048]{2,1,0:T(8,128)(2,1)} %get-tuple-element.87) | copy-start | bytes 12582916
  265.4 25.9 %slice-start = ((s8[6291456]{0:T(1024)(128)(4,1)}), s8[4194304]{0:T(1024)(128)(4,1)S(1)}, s32[]{:S(2)}) async-start(s8[6291456]{0:T(1024)(128)(4,1)} %bitcast.63), calls=%async_computation.4 | async-start | bytes 8388608
  276.2 13.3 %copy-start.4 = (f32[1024,1536]{1,0:T(8,128)}, f32[1024,1536]{1,0:T(8,128)S(1)}, u32[]{:S(2)}) copy-start(f32[1024,1536]{1,0:T(8,128)S(1)} %fusion.8.refs_3_) | copy-start | bytes 18874372
  276.2 15.0 %slice-start.1 = ((s8[6291456]{0:T(1024)(128)(4,1)}), s8[2097152]{0:T(1024)(128)(4,1)S(1)}, s32[]{:S(2)}) async-start(s8[6291456]{0:T(1024)(128)(4,1)} %bitcast.63), calls=%async_computation.5 | async-start | bytes 4194304
  289.5 1.7 copy-start.5
  469.4 1.0 copy-start
Sparse Core Ops, SparseCore 0:
  109.1 44.0 all-gather.2
  265.3 44.5 all-gather.4
  469.6 74.7 reduce-scatter.1
